TPU v7x, 32 devices: a whole 2x2x4 slice. The times are simulated.
32 devices in a mesh: frame: 4 (over y, core), expert: 8 (over z, x).
Axes of the slice: x: 2, y: 2, z: 4, core: 2. Of those that a mesh axis runs over, the one named last changes fastest.
Arguments:
- frames: bfloat16 [8, 4096, 1408], P('expert', 'frame'), may hold values from -16 to 16
- frame_counts: int32 [8], P('expert'), may hold values from 1 to 16, as said below
- latents: bfloat16 [32, 1408], replicated, may hold values from -36 to 36
- w_kv: bfloat16 [1408, 2816], P('expert'), may hold values from -0.15625 to 0.15625
- w_proj: bfloat16 [1408, 6144], P('expert', 'frame'), may hold values from -0.15625 to 0.15625
- norm_gain: bfloat16 [6144], replicated, may hold values from 0.099609375 to 1.8984375
- router: bfloat16 [6144, 8], replicated, may hold values from -0.078125 to 0.078125
- expert_ids: int32 [256, 2], P('expert'), may hold values from 0 to 7, all different within a row; in each aligned block of 32 rows (0 to 31, 32 to 63, ...) at most 16 rows name the same one
- w_gate: bfloat16 [8, 6144, 8192], P('expert', None, 'frame'), may hold values from -0.078125 to 0.078125
- w_up: bfloat16 [8, 6144, 8192], P('expert', None, 'frame'), may hold values from -0.078125 to 0.078125
- w_down: bfloat16 [8, 8192, 6144], P('expert', 'frame'), may hold values from -0.25 to 0.25
Outputs:
- layer_out: bfloat16 [256, 6144], P('expert', 'frame')
Inputs may be any that keep to these rules, and one draw needn't show every extreme that they name: `frame_counts`: some clip has all 16 frames valid and some other clip exactly one. `expert_ids`: each row names two different experts. Within the 32 rows of one index of expert no expert is named by more than 16 rows, and in some of these blocks one expert is named by exactly 16.
All inputs are finite; a program needn't handle non-finite values.
Results may differ from a plain program's by a relative error of at most 0.022.
Values may be sent and summed in bfloat16 or wider, within the bound.
No kernel may reach another device: no remote copies, remote signals or barrier semaphores. Data moves between devices by JAX's collectives and lax.ppermute only.
A program may use at most 192 MiB of HBM per device.

v0:
```python
import math

import jax
import jax.numpy as jnp
from jax import lax
from jax.sharding import PartitionSpec as P

HEADS = 16
PATCH = 256


NEG_BIG = -1e30
EPSILON = 1e-05


def joined(value, axis, join):
    pieces = jax.tree.map(lambda part: lax.all_gather(part, axis), value)
    head = jax.tree.map(lambda part: part[0], pieces)
    tail = jax.tree.map(lambda part: part[1:], pieces)
    subtotal, _ = lax.scan(lambda subtotal, piece: (join(subtotal, piece), None), head, tail)
    return subtotal


def rescale(weighted, factor):
    return (weighted.reshape(factor.shape + (-1,)) * factor[..., None]).reshape(weighted.shape)


def combine_parts(earlier, later):
    peak_left, totals_left, weighted_left = earlier
    peak_right, totals_right, weighted_right = later
    peak_both = jnp.maximum(peak_left, peak_right)
    factor_left = jnp.exp(peak_left - peak_both)
    factor_right = jnp.exp(peak_right - peak_both)
    totals_both = totals_left * factor_left + totals_right * factor_right
    weighted_both = rescale(weighted_left, factor_left) + rescale(weighted_right, factor_right)
    return (peak_both, totals_both, weighted_both)


def local(
    frames, frame_counts, latents, w_kv, w_proj, norm_gain, router, expert_ids, w_gate, w_up, w_down
):
    clip_count, frame_tokens, width = frames.shape
    head_count = HEADS
    head_size = width // head_count
    latent_count = latents.shape[0]
    tokens_here = clip_count * latent_count
    flat_frames = frames.reshape(clip_count * frame_tokens, width)
    columns = flat_frames
    kv_sum = jnp.dot(
        columns,
        lax.all_gather(w_kv, "expert", axis=0, tiled=True),
        preferred_element_type=jnp.float32,
    )
    key_value = kv_sum.astype(jnp.bfloat16).reshape(clip_count, frame_tokens, 2 * width)
    key_rows = key_value[:, :, :width].reshape(clip_count, frame_tokens, head_count, head_size)
    value_rows = key_value[:, :, width:].reshape(clip_count, frame_tokens, head_count, head_size)
    queries = latents.reshape(latent_count, head_count, head_size)
    scores = jnp.einsum(
        "lhd,cphd->clhp", queries, key_rows, preferred_element_type=jnp.float32
    ) / math.sqrt(head_size)
    frames_here = frame_tokens // PATCH
    frame_of = (
        lax.axis_index("frame") * frames_here + jnp.arange(frame_tokens, dtype=jnp.int32) // PATCH
    )
    valid = (frame_of[None, :] < frame_counts[:, None])[:, None, None, :]
    masked = jnp.where(valid, scores, NEG_BIG)
    peak = jnp.max(masked, axis=-1)
    expos = jnp.where(valid, jnp.exp(masked - peak[..., None]), 0.0)
    totals = jnp.sum(expos, axis=-1)
    weighted = jnp.einsum("clhp,cphd->clhd", expos, value_rows, preferred_element_type=jnp.float32)
    weighted = weighted.reshape(clip_count, latent_count, width)
    peak_all, totals_all, weighted_all = joined((peak, totals, weighted), "frame", combine_parts)
    pooled = (
        rescale(weighted_all, 1.0 / totals_all).reshape(tokens_here, width).astype(jnp.bfloat16)
    )
    columns = pooled
    x_part = jnp.dot(
        columns,
        lax.all_gather(w_proj, "expert", axis=0, tiled=True),
        preferred_element_type=jnp.float32,
    ).astype(jnp.bfloat16)
    part_width = w_proj.shape[1]
    model_width = router.shape[0]
    gain_all = norm_gain.astype(jnp.float32)
    router_all = router.astype(jnp.float32)
    x_float = x_part.astype(jnp.float32)
    x_whole = lax.all_gather(x_part, "frame", axis=1, tiled=True).astype(jnp.float32)
    squares = jnp.sum(x_whole * x_whole, axis=-1)
    raw_logits = jnp.dot(x_whole * gain_all, router_all, precision=lax.Precision.HIGHEST)
    scale = lax.rsqrt(squares / model_width + EPSILON)
    normed = (x_whole * scale[:, None] * gain_all).astype(jnp.bfloat16)
    logits = raw_logits * scale[:, None]
    chosen = jnp.take_along_axis(logits, expert_ids, axis=1)
    gates = jax.nn.softmax(chosen, axis=-1)
    expert_total = router.shape[1]
    capacity = tokens_here // 2
    pair_ids = expert_ids.reshape(-1)
    onehot = (pair_ids[:, None] == jnp.arange(expert_total, dtype=jnp.int32)[None, :]).astype(
        jnp.int32
    )
    earlier_hits = jnp.cumsum(onehot, axis=0) - onehot
    position = jnp.sum(earlier_hits * onehot, axis=-1)
    slot_of = pair_ids * capacity + position
    pair_hit = (
        slot_of[None, :] == jnp.arange(expert_total * capacity, dtype=jnp.int32)[:, None]
    ).astype(jnp.float32)
    select = pair_hit.reshape(-1, tokens_here, 2).sum(-1).astype(jnp.bfloat16)
    mixing = (pair_hit * gates.reshape(-1)[None, :]).reshape(-1, tokens_here, 2).sum(-1)
    packed = jnp.dot(select, normed, preferred_element_type=jnp.float32).astype(jnp.bfloat16)
    shard_count = lax.axis_size("expert") // expert_total
    row_width = packed.shape[1]
    send_rows = jnp.broadcast_to(
        packed.reshape(expert_total, 1, capacity, row_width),
        (expert_total, shard_count, capacity, row_width),
    )
    send_rows = send_rows.reshape(expert_total * shard_count, capacity, row_width)
    gate_local = w_gate[0]
    up_local = w_up[0]
    down_local = w_down[0]
    arrived = lax.all_to_all(send_rows, "expert", split_axis=0, concat_axis=0, tiled=True)
    flat_rows = arrived.reshape(-1, arrived.shape[-1])
    gate_val = jnp.dot(flat_rows, gate_local, preferred_element_type=jnp.float32)
    up_val = jnp.dot(flat_rows, up_local, preferred_element_type=jnp.float32)
    hidden_rows = (jax.nn.silu(gate_val) * up_val).astype(jnp.bfloat16)
    hidden = hidden_rows.reshape(arrived.shape[0], arrived.shape[1], -1)
    slot_rows = hidden.reshape(-1, hidden.shape[-1])
    columns = down_local
    summed = lax.psum_scatter(
        lax.dot_general(
            columns, slot_rows, (((0,), (1,)), ((), ())), preferred_element_type=jnp.float32
        ).astype(jnp.bfloat16),
        "frame",
        scatter_dimension=0,
        tiled=True,
    )
    outgoing = summed.reshape(part_width, -1, capacity)
    returned = lax.all_to_all(outgoing, "expert", split_axis=1, concat_axis=1, tiled=True)
    per_expert = (
        returned.astype(jnp.float32).reshape(part_width, expert_total, shard_count, capacity).sum(2)
    )
    per_expert = per_expert.reshape(part_width, expert_total * capacity)
    moe_part = jnp.dot(per_expert, mixing, precision=lax.Precision.HIGHEST)
    return (x_float + jnp.transpose(moe_part)).astype(jnp.bfloat16)


def solution(mesh):
    in_specs = (
        P("expert", "frame", None),
        P("expert"),
        P(),
        P("expert", None),
        P("expert", "frame"),
        P(),
        P(),
        P("expert", None),
        P("expert", None, "frame"),
        P("expert", None, "frame"),
        P("expert", "frame", None),
    )
    out_specs = P("expert", "frame")
    return jax.shard_map(local, mesh=mesh, in_specs=in_specs, out_specs=out_specs, check_vma=False)
```

profile of v0, /device:TPU:0, one launch (start us, length us, event | category | flops | bytes accessed | tf_op | source)
XLA Modules:
  0.0 341.8 jit_solution(9732100011328238051)
XLA Ops:
  6.5 0.7 all-gather.7.cloned.1.call-update
  7.3 0.7 all-gather.9.cloned.1.call-update
  8.1 0.7 bitcast_or_fusion
  8.7 0.8 copy.94
  10.2 1.2 reshape.198
  11.3 0.7 convert_element_type.54
  12.0 0.1 copy.96
  12.1 0.1 reshape.206
  12.2 0.1 eq.30
  12.4 0.1 reduce_window_sum.11
  12.5 0.2 select_reduce_fusion.1
  12.7 0.1 reduce_sum.62
  12.8 0.1 copy.95
  12.9 0.7 multiply_add_fusion
  13.6 117.4 %all-gather.7.cloned.1.call-done = bf16[1408,2816]{1,0:T(8,128)(2,1)} async-done(((bf16[176,2816]{1,0:T(8,128)(2,1)}), bf16[1408,2816]{1,0:T(8,128)(2,1)}) %all-gather.7.cloned.1.call-update) | async-done | bytes 7929872 | tf_op jit(solution)/shard_map/all_gather | solution.py:51
  131.0 12.1 %convert_bitcast_fusion = bf16[1,1024,2816]{2,1,0:T(8,128)(2,1)S(1)} fusion(bf16[1408,2816]{1,0:T(8,128)(2,1)} %all-gather.7.cloned.1.call-done, bf16[1,1024,1408]{2,1,0:T(8,128)(2,1)S(1)} %copy-done), kind=kOutput, calls=%fused_computation.20 | convolution fusion | flops 8123056128 | bytes 16580608 | tf_op jit(solution)/shard_map/dot_general | solution.py:49
  143.1 2.9 fusion.73
  146.0 3.1 copy.87
  149.1 4.6 %copy.89 = bf16[1,1024,1408]{1,2,0:T(8,128)(2,1)} copy(bf16[1,1024,1408]{2,1,0:T(8,128)(2,1)} %get-tuple-element.88) | data formatting | bytes 5767168 | tf_op jit(solution)/shard_map/slice | solution.py:56
  153.8 0.7 bitcast_reduce_fusion
  154.4 1.6 copy-done.5
  156.0 1.2 fusion.33
  157.3 0.2 copy.90
  157.4 0.1 all_gather_reshape.3
  157.6 8.4 %all_gather.29 = f32[4,1,32,1408]{3,2,1,0:T(8,128)S(1)} all-gather(f32[1,1,32,1408]{3,2,1,0:T(8,128)S(1)} %all_gather_reshape.3), channel_id=1, replica_groups=mesh['frame'=4,'expert'=8] {'frame'}, dimensions={0}, use_global_device_ids=true | all-gather | bytes 901120 | tf_op jit(solution)/shard_map/all_gather | solution.py:17
  166.0 0.6 fusion.32
  166.6 5.2 %all-gather.3 = f32[4,32,16]{1,2,0:T(8,128)S(1)} all-gather(f32[1,32,16]{1,2,0:T(8,128)S(1)} %bitcast.143), channel_id=3, replica_groups=mesh['frame'=4,'expert'=8] {'frame'}, dimensions={0}, use_global_device_ids=true | all-gather | bytes 10240 | tf_op jit(solution)/shard_map/all_gather | solution.py:17
  171.8 5.2 %all-gather.2 = f32[4,32,16]{1,2,0:T(8,128)S(1)} all-gather(f32[1,32,16]{1,2,0:T(8,128)S(1)} %bitcast.142), channel_id=2, replica_groups=mesh['frame'=4,'expert'=8] {'frame'}, dimensions={0}, use_global_device_ids=true | all-gather | bytes 10240 | tf_op jit(solution)/shard_map/all_gather | solution.py:17
  177.0 2.6 while.14
  177.1 0.1 copy.104
  177.1 0.1 mul.206
  177.3 0.2 mul.207
  177.4 0.1 copy.105
  177.5 0.1 mul.208
  177.6 0.2 mul.209
  177.9 0.1 copy.104
  178.0 0.1 mul.206
  178.1 0.2 mul.207
  178.3 0.1 copy.105
  178.4 0.1 mul.208
  178.5 0.2 mul.209
  178.9 0.1 mul.206
  179.0 0.2 mul.207
  179.2 0.1 mul.208
  179.4 0.2 mul.209
  179.7 0.1 mul.125
  179.8 0.2 mul.126
  180.0 25.8 %all-gather.9.cloned.1.call-done = bf16[1408,1536]{1,0:T(8,128)(2,1)} async-done(((bf16[176,1536]{1,0:T(8,128)(2,1)}), bf16[1408,1536]{1,0:T(8,128)(2,1)}) %all-gather.9.cloned.1.call-update) | async-done | bytes 4325392 | tf_op jit(solution)/shard_map/all_gather | solution.py:79
  205.8 3.0 convolution_convert_fusion.1
  208.8 6.4 %all_gather.31 = bf16[32,6144]{1,0:T(8,128)(2,1)S(1)} all-gather(bf16[32,1536]{1,0:T(8,128)(2,1)S(1)} %convolution_convert_fusion.1), channel_id=1, replica_groups=mesh['frame'=4,'expert'=8] {'frame'}, dimensions={1}, use_global_device_ids=true | all-gather | bytes 491520 | tf_op jit(solution)/shard_map/all_gather | solution.py:87
  215.3 0.2 fusion.47
  215.5 0.5 convolution_multiply_fusion
  216.0 0.7 gather_fusion
  216.8 0.1 reshape.209
  216.9 0.1 copy.97
  217.0 0.1 convert_reduce_fusion
  217.1 0.6 convolution_convert_fusion
  217.7 40.4 %all_to_all.10 = bf16[8,16,6144]{2,1,0:T(8,128)(2,1)S(1)} all-to-all(bf16[8,16,6144]{2,1,0:T(8,128)(2,1)S(1)} %bitcast.138), channel_id=1, replica_groups=mesh['frame'=4,'expert'=8] {'expert'}, dimensions={0} | all-to-all | bytes 3145728 | tf_op jit(solution)/shard_map/all_to_all | solution.py:120
  258.1 1.1 copy-done.2
  259.3 10.9 %fusion.9 = f32[128,2048]{1,0:T(8,128)} fusion(bf16[128,6144]{1,0:T(8,128)(2,1)S(1)} %bitcast.135, bf16[1,6144,2048]{2,1,0:T(8,128)(2,1)} %param.21), kind=kOutput, calls=%fused_computation.15 | convolution fusion | flops 3221225472 | bytes 27787264 | tf_op jit(solution)/shard_map/dot_general | solution.py:122
  270.2 19.8 %fusion.14 = bf16[6144,128]{0,1:T(8,128)(2,1)} fusion(bf16[1,2048,6144]{2,1,0:T(8,128)(2,1)} %param.23, bf16[128,6144]{1,0:T(8,128)(2,1)} %bitcast.136, bf16[1,6144,2048]{2,1,0:T(8,128)(2,1)} %param.22, f32[128,2048]{1,0:T(8,128)} %fusion.9), kind=kOutput, calls=%fused_computation.19 | convolution fusion | flops 6444810240 | bytes 54525952 | tf_op jit(solution)/shard_map/dot_general | solution.py:129
  290.1 26.9 %reduce-scatter.2.cloned.1.call-done = bf16[1536,128]{0,1:T(8,128)(2,1)} async-done(((bf16[6144,128]{0,1:T(8,128)(2,1)}), bf16[1536,128]{0,1:T(8,128)(2,1)}) %reduce-scatter.2.cloned.1.call-update) | async-done | bytes 393232 | tf_op jit(solution)/shard_map/reduce_scatter | solution.py:128
  317.0 17.4 %all_to_all.11 = bf16[1536,8,16]{0,2,1:T(8,128)(2,1)S(1)} all-to-all(bf16[1536,8,16]{0,2,1:T(8,128)(2,1)} %bitcast.141), channel_id=1, replica_groups=mesh['frame'=4,'expert'=8] {'expert'}, dimensions={1} | all-to-all | bytes 786432 | tf_op jit(solution)/shard_map/all_to_all | solution.py:137
  334.4 0.9 fusion.26
  (46 shorter events, 0.9 us)
Async XLA Ops:
  6.5 124.5 %copy-start = (bf16[1,1024,1408]{2,1,0:T(8,128)(2,1)S(1)}, bf16[1,1024,1408]{2,1,0:T(8,128)(2,1)}, u32[]{:S(2)}) copy-start(bf16[1,1024,1408]{2,1,0:T(8,128)(2,1)} %param.13) | copy-start | bytes 8650756
  6.5 124.5 %all-gather.7.cloned.1.call-start = ((), (), s32[]{:S(2)}) async-start(), calls=%async_computation.3 | async-start | bytes 8921088 | tf_op jit(solution)/shard_map/all_gather | solution.py:51
  7.3 198.5 %all-gather.9.cloned.1.call-start = ((), (), s32[]{:S(2)}) async-start(), calls=%async_computation.4 | async-start | bytes 4866048 | tf_op jit(solution)/shard_map/all_gather | solution.py:79
  8.0 308.9 %reduce-scatter.2.cloned.1.call-start = ((), (), s32[]{:S(2)}) async-start(), calls=%async_computation.5 | async-start | bytes 1966080 | tf_op jit(solution)/shard_map/reduce_scatter | solution.py:128
  153.8 2.3 copy-start.5
  154.4 2.8 copy-start.3
  157.4 8.6 %copy-start.4 = (f32[16,1024,32]{1,2,0:T(8,128)S(1)}, f32[16,1024,32]{1,2,0:T(8,128)}, u32[]{:S(2)}) copy-start(f32[16,1024,32]{1,2,0:T(8,128)} %copy-done.3) | copy-start | bytes 6291460
  180.0 35.5 %copy-start.6 = (bf16[6144,8]{0,1:T(8,128)(2,1)S(1)}, bf16[6144,8]{0,1:T(8,128)(2,1)}, u32[]{:S(2)}) copy-start(bf16[6144,8]{0,1:T(8,128)(2,1)} %param.19) | copy-start | bytes 294916
  216.0 0.9 copy-start.7
  258.1 1.1 copy-start.2
  270.2 65.1 %copy-start.1 = (bf16[1,1024,1408]{2,1,0:T(8,128)(2,1)S(1)}, bf16[1,1024,1408]{2,1,0:T(8,128)(2,1)}, u32[]{:S(2)}) copy-start(bf16[1,1024,1408]{2,1,0:T(8,128)(2,1)} %param.13) | copy-start | bytes 8650756
Sparse Core Ops, SparseCore 0:
  9.5 121.4 all-gather.6
  133.2 72.5 all-gather.8
  290.2 26.7 reduce-scatter.1
where the time goes:
time: 342 us
  waiting for transfers between devices  172 us (50%)
  blocking collectives  82.9 us (24%)
  matrix products  49.8 us (15%)
  local copies, waits for them, and re-layouts  19.6 us (6%)
  between operations  13.9 us (4%)
  other arithmetic  3.75 us (1%)
    all_gather x1, waiting for transfers between devices, local(): lax.all_gather(w_kv, 'expert', axis=0, tiled=True)  117 us
    all_to_all x1, blocking collectives, local(): lax.all_to_all(send_rows, 'expert', split_axis=0, concat_axis=0, tiled=True)  40.4 us
    reduce_scatter x1, waiting for transfers between devices, local(): lax.psum_scatter(lax.dot_general(columns, slot_rows, (((0,), (1,)), ((),...  26.9 us
    all_gather x1, waiting for transfers between devices, local(): lax.all_gather(w_proj, 'expert', axis=0, tiled=True)  25.8 us
    dot_general x1, matrix products, local(): lax.dot_general(columns, slot_rows, (((0,), (1,)), ((), ())), preferred_e...  19.8 us
    all_gather x3, blocking collectives, joined(): pieces = jax.tree.map(lambda part: lax.all_gather(part, axis), value)  18.7 us
    all_to_all x1, blocking collectives, local(): lax.all_to_all(outgoing, 'expert', split_axis=1, concat_axis=1, tiled=True)  17.4 us
    dot_general x1, matrix products, local(): jnp.dot(columns, lax.all_gather(w_kv, 'expert', axis=0, tiled=True), pref...  12.1 us
  transfers between devices with their start and end apart: 3, of which 3 were waited for; matrix products, arithmetic and copies ran while one was open for 10% of the time, Pallas kernels for 0%

commit v1 on v0

--- a/solution.py
+++ b/solution.py
@@ -3,6 +3,8 @@
 import jax
 import jax.numpy as jnp
 from jax import lax
+from jax.experimental import pallas as pl
+from jax.experimental.pallas import tpu as pltpu
 from jax.sharding import PartitionSpec as P
 
 HEADS = 16
@@ -143,6 +145,351 @@
     return (x_float + jnp.transpose(moe_part)).astype(jnp.bfloat16)
 
 
+def swap(value, axis, bits, size):
+    return lax.ppermute(value, axis, [(i, i ^ bits) for i in range(size)])
+
+
+def after(value, *earlier):
+    return lax.optimization_barrier((value, *earlier))[0]
+
+
+PIECES = (
+    tuple((2 * d, 0) for d in range(4)),
+    tuple((2 * d + 1, 0) for d in range(4)),
+    tuple((2 * d, 2) for d in range(4)),
+    tuple((2 * d + 1, 2) for d in (0, 1)),
+    tuple((2 * d + 1, 2) for d in (2, 3)),
+)
+PLACES = tuple(places for group in PIECES for places in (group, tuple((e, f + 1) for e, f in group)))
+
+
+def along_z(piece):
+    return jnp.stack([piece] + [swap(piece, "expert", 2 * d, 8) for d in (1, 2, 3)])
+
+
+def spread(column, *earlier):
+    core = lambda value: swap(value, "frame", 1, 4)
+    by_x = swap(column, "expert", 1, 8)
+    by_y = swap(column, "frame", 2, 4)
+    low = swap(by_y[:2], "expert", 1, 8)
+    high = swap(by_x[2:], "frame", 2, 4)
+    groups = []
+    for value in (column, by_x, by_y, low, high):
+        groups += [value, core(value)]
+    return groups, (low, high, by_x)
+
+
+def place_pieces(where, pieces, whole):
+    rows = pieces[0].shape[1]
+    for places, piece in zip(PLACES, pieces):
+        for at, (e_bits, f_bits) in enumerate(places):
+            row = pl.multiple_of((where[0] ^ e_bits) * rows, 16)
+            whole[where[1] ^ f_bits, pl.ds(row, rows), :] = piece[at]
+
+
+def attend_body(where, frames, *refs):
+    pieces, (pooled_frames, states, whole) = refs[: len(PLACES)], refs[len(PLACES) :]
+    place_pieces(where, pieces, whole)
+    tokens = frames.shape[0]
+    row = lax.broadcasted_iota(jnp.int32, (tokens, whole.shape[2]), 0)
+    valid = row < where[2]
+    for group in range(whole.shape[0]):
+        scores = jnp.dot(frames[...], whole[group], preferred_element_type=jnp.float32)
+        masked = jnp.where(valid, scores, NEG_BIG)
+        peak = jnp.max(masked, axis=0, keepdims=True)
+        expos = jnp.where(valid, jnp.exp(masked - peak), 0.0)
+        total = jnp.sum(expos, axis=0, keepdims=True)
+        some = total > 0.0
+        safe = jnp.where(some, total, 1.0)
+        weights = (expos * (1.0 / safe)).astype(jnp.bfloat16)
+        states[pl.ds(group, 1), :] = jnp.where(some, peak + jnp.log(safe), NEG_BIG)
+        pooled_frames[group] = lax.dot_general(
+            weights, frames[...], (((0,), (0,)), ((), ())), preferred_element_type=jnp.float32
+        ).astype(jnp.bfloat16)
+
+
+def values_body(where, pooled_frames, states, *refs):
+    pieces, (packed, whole) = refs[: len(PLACES)], refs[len(PLACES) :]
+    place_pieces(where, pieces, whole)
+    groups, pairs, _ = pooled_frames.shape
+    width = whole.shape[2]
+    head_size = width // 4
+    latents = pairs // 4
+    head_of = lax.broadcasted_iota(jnp.int32, (latents, width), 1) // head_size
+    for group in range(groups):
+        every = jnp.dot(pooled_frames[group], whole[group], preferred_element_type=jnp.float32)
+        own = jnp.zeros((latents, width), jnp.float32)
+        for head in range(4):
+            own = jnp.where(head_of == head, every[head * latents : (head + 1) * latents, :], own)
+        start = group * 384
+        packed[:, start : start + width] = own.astype(jnp.bfloat16)
+        packed[:, start + width : start + 384] = states[group]
+
+
+def combine_body(where, parts, pooled):
+    latents = parts.shape[1]
+    width = 352
+    head_size = width // 4
+    head_of = lax.broadcasted_iota(jnp.int32, (latents, width), 1) // head_size
+    for turn in range(4):
+        start = pl.multiple_of((where[0] ^ turn) * 384, 128)
+        logs, values = [], []
+        for part in range(4):
+            block = parts[part, :, pl.ds(start, 384)].astype(jnp.float32)
+            state = block[:, width : width + 4] + block[:, width + 4 : width + 8]
+            state = state + block[:, width + 8 : width + 12]
+            logs.append(state)
+            values.append(block[:, :width])
+        peak = jnp.maximum(jnp.maximum(logs[0], logs[1]), jnp.maximum(logs[2], logs[3]))
+        shares = [jnp.exp(state - peak) for state in logs]
+        inverse = 1.0 / (shares[0] + shares[1] + shares[2] + shares[3])
+        joined_up = jnp.zeros((latents, width), jnp.float32)
+        for share, value in zip(shares, values):
+            share = share * inverse
+            spread_out = jnp.zeros((latents, width), jnp.float32)
+            for head in range(4):
+                spread_out = jnp.where(head_of == head, share[:, head : head + 1], spread_out)
+            joined_up = joined_up + value * spread_out
+        pooled[turn] = jnp.zeros((latents, 384), jnp.bfloat16)
+        pooled[turn, :, :width] = joined_up.astype(jnp.bfloat16)
+
+
+def enter_body(where, own, other, gain, gate_w, up_w, gate_out, up_out, squares):
+    turn, step = pl.program_id(0), pl.program_id(1)
+    depth = gate_w.shape[1]
+
+    @pl.when((turn == 0) & (step == 0))
+    def _():
+        gate_out[...] = jnp.zeros_like(gate_out)
+        up_out[...] = jnp.zeros_like(up_out)
+        squares[...] = jnp.zeros_like(squares)
+
+    def add(rows):
+        block = rows[:, pl.ds(pl.multiple_of(step * depth, 128), depth)].astype(jnp.float32)
+        total = jnp.sum(block * block, axis=1, keepdims=True)
+        squares[...] += jnp.broadcast_to(total, squares.shape)
+        gained = (block * gain[0].astype(jnp.float32)).astype(jnp.bfloat16)
+        gate_out[...] += jnp.dot(gained, gate_w[0], preferred_element_type=jnp.float32)
+        up_out[...] += jnp.dot(gained, up_w[0], preferred_element_type=jnp.float32)
+
+    pl.when(turn == 0)(lambda: add(own))
+    pl.when(turn == 1)(lambda: add(other))
+
+
+def near_body(where, own, other, gain, gate_w, up_w, gate_out, up_out, squares):
+    enter_body(where, own, other, gain, gate_w, up_w, gate_out, up_out, squares)
+
+
+def far_body(where, own, other, gain, gate_w, up_w, gate_in, up_in, squares_in, hidden, gate_sum, up_sum, squares):
+    enter_body(where, own, other, gain, gate_w, up_w, gate_sum, up_sum, squares)
+
+    @pl.when((pl.program_id(0) == 1) & (pl.program_id(1) == pl.num_programs(1) - 1))
+    def _():
+        width = gain.shape[2] * pl.num_programs(1) * 4
+        mean = (squares[:, :1] + squares_in[:, :1]) / width
+        scale = lax.rsqrt(mean + EPSILON)
+        gate_val = (gate_sum[...] + gate_in[...]) * scale
+        up_val = (up_sum[...] + up_in[...]) * scale
+        hidden[...] = (gate_val / (1.0 + jnp.exp(-gate_val)) * up_val).astype(jnp.bfloat16)
+
+
+def expert_in(where, own, other, gain, gate_w, up_w, bits, earlier=None):
+    rows, columns = own.shape
+    depth = 512
+    steps = columns // depth
+    hidden_width = gate_w.shape[2]
+    whole = lambda shape: pl.BlockSpec(shape, lambda turn, step, where: (0, 0))
+    chunk = lambda turn, step, where: (where[1] ^ (bits + turn)) * steps + step
+    gain_spec = pl.BlockSpec((1, 1, depth), lambda turn, step, where: (chunk(turn, step, where), 0, 0))
+    weight_spec = pl.BlockSpec((1, depth, hidden_width), lambda turn, step, where: (0, chunk(turn, step, where), 0))
+    sums = [
+        jax.ShapeDtypeStruct((rows, hidden_width), jnp.float32),
+        jax.ShapeDtypeStruct((rows, hidden_width), jnp.float32),
+        jax.ShapeDtypeStruct((rows, 128), jnp.float32),
+    ]
+    in_specs = [whole(own.shape), whole(other.shape), gain_spec, weight_spec, weight_spec]
+    operands = [own, other, gain.reshape(-1, 1, depth), gate_w, up_w]
+    if earlier is None:
+        out_shape, out_specs, scratch, body = sums, [whole(s.shape) for s in sums], [], near_body
+    else:
+        out_shape = jax.ShapeDtypeStruct((rows, hidden_width), jnp.bfloat16)
+        out_specs = whole(out_shape.shape)
+        scratch = [pltpu.VMEM(s.shape, s.dtype) for s in sums]
+        in_specs += [whole(s.shape) for s in sums]
+        operands += list(earlier)
+        body = far_body
+    return pl.pallas_call(
+        body,
+        out_shape=out_shape,
+        grid_spec=pltpu.PrefetchScalarGridSpec(
+            num_scalar_prefetch=1, grid=(2, steps), in_specs=in_specs, out_specs=out_specs, scratch_shapes=scratch
+        ),
+        cost_estimate=cost(8 * rows * columns * hidden_width, 8 * columns * hidden_width),
+    )(where, *operands)
+
+
+def cost(flops, moved):
+    return pl.CostEstimate(flops=flops, transcendentals=0, bytes_accessed=moved)
+
+
+def down_body(where, hidden, weight, out):
+    out[0] = jnp.dot(hidden[...], weight[0], preferred_element_type=jnp.float32).astype(jnp.bfloat16)
+
+
+def expert_out(where, hidden, down_w, bits):
+    rows, depth = hidden.shape
+    part = down_w.shape[2] // 4
+    width = 512
+    steps = part // width
+    return pl.pallas_call(
+        down_body,
+        out_shape=jax.ShapeDtypeStruct((2, rows, part), jnp.bfloat16),
+        grid_spec=pltpu.PrefetchScalarGridSpec(
+            num_scalar_prefetch=1,
+            grid=(2, steps),
+            in_specs=[
+                pl.BlockSpec((rows, depth), lambda turn, step, where: (0, 0)),
+                pl.BlockSpec(
+                    (1, depth, width),
+                    lambda turn, step, where: (0, 0, (where[1] ^ (bits + turn)) * steps + step),
+                ),
+            ],
+            out_specs=pl.BlockSpec((1, rows, width), lambda turn, step, where: (turn, 0, step)),
+        ),
+        cost_estimate=cost(4 * rows * depth * part, 4 * depth * part),
+    )(where, hidden, down_w)
+
+
+def in_vmem(body, out_shape, scratch=()):
+    space = lambda _: pl.BlockSpec(memory_space=pltpu.VMEM)
+
+    def call(where, *operands):
+        return pl.pallas_call(
+            body,
+            out_shape=out_shape,
+            in_specs=[pl.BlockSpec(memory_space=pltpu.SMEM)] + [space(o) for o in operands],
+            out_specs=jax.tree.map(space, out_shape),
+            scratch_shapes=list(scratch),
+        )(where, *operands)
+
+    return call
+
+
+def fast_local(
+    frames, frame_counts, latents, w_kv, w_proj, norm_gain, router, expert_ids, w_gate, w_up, w_down
+):
+    _, frame_tokens, width = frames.shape
+    latent_count = latents.shape[0]
+    head_size = width // HEADS
+    e, f = lax.axis_index("expert"), lax.axis_index("frame")
+    rows = w_kv.shape[0]
+    quarter = width // 4
+    frames_here = frame_tokens // PATCH
+    valid_tokens = jnp.clip((frame_counts[0] - f * frames_here) * PATCH, 0, frame_tokens)
+    where = jnp.stack([e, f, valid_tokens]).astype(jnp.int32)
+
+    head_here = f * 4 + jnp.arange(4, dtype=jnp.int32)
+    head_of = jnp.arange(width, dtype=jnp.int32) // head_size
+    spaced = jnp.where(
+        head_here[:, None, None] == head_of[None, None, :], latents[None], jnp.zeros((), jnp.bfloat16)
+    ).reshape(4 * latent_count, width)
+    asked = lax.dot_general(
+        w_kv[:, :width], spaced, (((1,), (1,)), ((), ())), preferred_element_type=jnp.float32
+    )
+    asked = (asked / math.sqrt(head_size)).astype(jnp.bfloat16)
+    asked_column = along_z(asked)
+    asked_pieces, asked_x = spread(asked_column)
+    value_piece = lax.dynamic_slice(w_kv, (0, width + f * quarter), (rows, quarter))
+    value_column = along_z(after(value_piece, asked_column))
+    value_pieces, value_x = spread(after(value_column, *asked_x))
+    proj_other = swap(after(w_proj, *value_x), "expert", 1, 8)
+
+    pooled_frames, states = in_vmem(
+        attend_body,
+        (
+            jax.ShapeDtypeStruct((4, 4 * latent_count, width), jnp.bfloat16),
+            jax.ShapeDtypeStruct((4, 4 * latent_count), jnp.float32),
+        ),
+        [pltpu.VMEM((4, width, 4 * latent_count), jnp.bfloat16)],
+    )(where, frames[0], *asked_pieces)
+    by_latent = jnp.transpose(states.reshape(4, 4, latent_count), (0, 2, 1))
+    high = lax.reduce_precision(by_latent, 8, 7)
+    middle = lax.reduce_precision(by_latent - high, 8, 7)
+    low = (by_latent - high) - middle
+    blank = jnp.zeros((4, latent_count, 20), jnp.float32)
+    state_columns = jnp.concatenate([high, middle, low, blank], axis=-1).astype(jnp.bfloat16)
+    packed = in_vmem(
+        values_body,
+        jax.ShapeDtypeStruct((latent_count, 4 * 384), jnp.bfloat16),
+        [pltpu.VMEM((4, width, quarter), jnp.bfloat16)],
+    )(where, pooled_frames, state_columns, *value_pieces)
+    parts = lax.all_gather(packed, "frame")
+    z_index = jnp.stack([e // 2]).astype(jnp.int32)
+    pooled = in_vmem(combine_body, jax.ShapeDtypeStruct((4, latent_count, 384), jnp.bfloat16))(z_index, parts)
+
+    own_first = e % 2 == 0
+    proj_rows = jnp.where(
+        own_first, jnp.concatenate([w_proj, proj_other]), jnp.concatenate([proj_other, w_proj])
+    )
+    proj_rows = jnp.pad(proj_rows, ((0, 384 - 2 * rows), (0, 0)))
+    gathered = jnp.concatenate([pooled[0]] + [swap(pooled[d], "expert", 2 * d, 8) for d in (1, 2, 3)])
+    partial = jnp.dot(gathered, proj_rows, preferred_element_type=jnp.float32).astype(jnp.bfloat16)
+    partial = partial.reshape(4, latent_count, -1)
+    x_sum = partial[0].astype(jnp.float32)
+    for d in (1, 2, 3):
+        x_sum = x_sum + swap(partial[d], "expert", 2 * d, 8).astype(jnp.float32)
+    x_part = x_sum.astype(jnp.bfloat16)
+    x_float = x_part.astype(jnp.float32)
+    part_width = x_part.shape[1]
+
+    expert_total = router.shape[1]
+    capacity = latent_count // 2
+    pair_ids = expert_ids.reshape(-1)
+    onehot = (pair_ids[:, None] == jnp.arange(expert_total, dtype=jnp.int32)[None, :]).astype(jnp.int32)
+    earlier_hits = jnp.cumsum(onehot, axis=0) - onehot
+    position = jnp.sum(earlier_hits * onehot, axis=-1)
+    slot_of = pair_ids * capacity + position
+    pair_hit = (
+        slot_of[None, :] == jnp.arange(expert_total * capacity, dtype=jnp.int32)[:, None]
+    ).astype(jnp.float32)
+    select = pair_hit.reshape(-1, latent_count, 2).sum(-1).astype(jnp.bfloat16)
+    send_rows = jnp.dot(select, x_part, preferred_element_type=jnp.float32).astype(jnp.bfloat16)
+    arrived = lax.all_to_all(
+        send_rows.reshape(expert_total, capacity, part_width), "expert", split_axis=0, concat_axis=0, tiled=True
+    ).reshape(-1, part_width)
+
+    from_core = swap(arrived, "frame", 1, 4)
+    from_y = swap(arrived, "frame", 2, 4)
+    from_both = swap(from_y, "frame", 1, 4)
+    near = expert_in(where, arrived, from_core, norm_gain, w_gate, w_up, 0)
+    hidden = expert_in(where, from_y, from_both, norm_gain, w_gate, w_up, 2, near)
+    far_parts = expert_out(where, hidden, w_down, 2)
+    chip_far = far_parts[0].astype(jnp.float32) + swap(far_parts[1], "frame", 1, 4).astype(jnp.float32)
+    y_sum = swap(chip_far.astype(jnp.bfloat16), "frame", 2, 4)
+    near_parts = expert_out(after(where, chip_far), hidden, w_down, 0)
+    own_sum = near_parts[0].astype(jnp.float32) + swap(near_parts[1], "frame", 1, 4).astype(jnp.float32)
+    summed = (own_sum + y_sum.astype(jnp.float32)).astype(jnp.bfloat16)
+    returned = lax.all_to_all(
+        summed.reshape(expert_total, capacity, part_width), "expert", split_axis=0, concat_axis=0, tiled=True
+    ).reshape(-1, part_width)
+
+    gain_here = lax.dynamic_slice(norm_gain, (f * part_width,), (part_width,)).astype(jnp.float32)
+    router_here = lax.dynamic_slice(router, (f * part_width, 0), (part_width, expert_total)).astype(jnp.float32)
+    raw = jnp.dot(x_float * gain_here, router_here, precision=lax.Precision.HIGHEST)
+    sums = jnp.concatenate([raw, jnp.sum(x_float * x_float, axis=-1, keepdims=True)], axis=-1)
+    sums = sums + swap(sums, "frame", 1, 4)
+    sums = sums + swap(sums, "frame", 2, 4)
+    scale = lax.rsqrt(sums[:, expert_total] / router.shape[0] + EPSILON)
+    logits = sums[:, :expert_total] * scale[:, None]
+    chosen = jnp.take_along_axis(logits, expert_ids, axis=1)
+    gates = jax.nn.softmax(chosen, axis=-1)
+    mixing = (pair_hit * gates.reshape(-1)[None, :]).reshape(-1, latent_count, 2).sum(-1)
+    moe_part = lax.dot_general(
+        mixing, returned.astype(jnp.float32), (((0,), (0,)), ((), ())), precision=lax.Precision.HIGHEST
+    )
+    return (x_float + moe_part).astype(jnp.bfloat16)
+
+
 def solution(mesh):
     in_specs = (
         P("expert", "frame", None),
@@ -158,4 +505,6 @@
         P("expert", "frame", None),
     )
     out_specs = P("expert", "frame")
-    return jax.shard_map(local, mesh=mesh, in_specs=in_specs, out_specs=out_specs, check_vma=False)
+    small = mesh.shape["frame"] == 4 and mesh.shape["expert"] == 8
+    body = fast_local if small else local
+    return jax.shard_map(body, mesh=mesh, in_specs=in_specs, out_specs=out_specs, check_vma=False)

time: 342 us -> 211 us (0.62)
  waiting for transfers between devices: 172 us -> 49.7 us
  Pallas kernels: 0 us -> 65.1 us
  matrix products: 49.8 us -> 3.06 us
  blocking collectives: 82.9 us -> 39.8 us
  starting transfers between devices: 0.08 us -> 36.2 us
  between operations: 13.9 us -> 1.13 us
  local copies, waits for them, and re-layouts: 19.6 us -> 11.7 us
    all_gather x2 -> x0, waiting for transfers between devices: 143 us -> none  [the longest x1 117 us: local(): lax.all_gather(w_kv, 'expert', axis=0, tiled=True)]
    pallas_call x0 -> x7, Pallas kernels: none -> 65.1 us  [the longest x2 27.8 us: expert_in(): pl.pallas_call(body, out_shape=out_shape, grid_spec=pltpu.PrefetchScalarG...]
    ppermute x0 -> x39, waiting for transfers between devices: none -> 49.7 us  [swap(): return lax.ppermute(value, axis, [(i, i ^ bits) for i in range(size)])]
    dot_general x9 -> x5, matrix products: 49.8 us -> 3.06 us  [the longest x1 1.33 us: fast_local(): lax.dot_general(w_kv[:, :width], spaced, (((1,), (1,)), ((), ())), prefer...]
    ppermute x0 -> x39, starting transfers between devices: none -> 36.2 us  [swap(): return lax.ppermute(value, axis, [(i, i ^ bits) for i in range(size)])]
    reduce_scatter x1 -> x0, waiting for transfers between devices: 26.9 us -> none  [local(): lax.psum_scatter(lax.dot_general(columns, slot_rows, (((0,), (1,)), ((),...]
    all_to_all x2, blocking collectives: 57.8 us -> 31.8 us  [the longest x1 17.4 us: fast_local(): lax.all_to_all(summed.reshape(expert_total, capacity, part_width), 'exper...]
    all_gather x4 -> x1, blocking collectives: 25.2 us -> 7.96 us  [fast_local(): parts = lax.all_gather(packed, 'frame')]
  transfers between devices with their start and end apart: 3 -> 39, of which waited for: 3 -> 13; matrix products, arithmetic and copies ran while one was open for 10% -> 4% of each run, Pallas kernels for 0% -> 20%
where the time goes in v1:
time: 211 us
  Pallas kernels  65.1 us (31%)
  waiting for transfers between devices  49.7 us (24%)
  blocking collectives  39.8 us (19%)
  starting transfers between devices  36.2 us (17%)
  local copies, waits for them, and re-layouts  11.7 us (6%)
  other arithmetic  3.93 us (2%)
  matrix products  3.06 us (1%)
    ppermute x39, waiting for transfers between devices, swap(): return lax.ppermute(value, axis, [(i, i ^ bits) for i in range(size)])  49.7 us
    ppermute x39, starting transfers between devices, swap(): return lax.ppermute(value, axis, [(i, i ^ bits) for i in range(size)])  36.2 us
    pallas_call x2, Pallas kernels, expert_in(): pl.pallas_call(body, out_shape=out_shape, grid_spec=pltpu.PrefetchScalarG...  27.8 us
    pallas_call x3, Pallas kernels, call(): pl.pallas_call(body, out_shape=out_shape, in_specs=[pl.BlockSpec(memory_s...  19.9 us
    pallas_call x2, Pallas kernels, expert_out(): pl.pallas_call(down_body, out_shape=jax.ShapeDtypeStruct((2, rows, part),...  17.5 us
    all_to_all x1, blocking collectives, fast_local(): lax.all_to_all(summed.reshape(expert_total, capacity, part_width), 'exper...  17.4 us
    all_to_all x1, blocking collectives, fast_local(): lax.all_to_all(send_rows.reshape(expert_total, capacity, part_width), 'ex...  14.4 us
    all_gather x1, blocking collectives, fast_local(): parts = lax.all_gather(packed, 'frame')  7.96 us
  transfers between devices with their start and end apart: 39, of which 13 were waited for; matrix products, arithmetic and copies ran while one was open for 4% of the time, Pallas kernels for 20%

profile of v1, /device:TPU:0, one launch (start us, length us, event | category | flops | bytes accessed | tf_op | source)
XLA Modules:
  0.0 210.7 jit_solution(7503900628332092481)
XLA Ops:
  0.1 0.9 broadcast_select_fusion
  1.1 1.3 fusion.2
  2.4 4.1 %collective-permute-start.1 = (bf16[176,128]{1,0:T(8,128)(2,1)S(1)}, bf16[176,128]{1,0:T(8,128)(2,1)S(1)}, u32[]{:S(2)}, u32[]{:S(2)}) collective-permute-start(bf16[176,128]{1,0:T(8,128)(2,1)S(1)} %bitcast.79), channel_id=1, source_target_pairs={{0,4},{1,5},{2,6},{3,7},{4,0},{5,1},{6,2},{7,3},{8,12},{9,13},{10,... | collective-permute-start | bytes 135176 | tf_op jit(solution)/shard_map/ppermute | solution.py:149
  6.5 1.4 collective-permute-start.2
  8.1 0.9 collective-permute-done.1
  9.0 3.4 %collective-permute-done.2 = bf16[176,128]{1,0:T(8,128)(2,1)S(1)} collective-permute-done((bf16[176,128]{1,0:T(8,128)(2,1)S(1)}, bf16[176,128]{1,0:T(8,128)(2,1)S(1)}, u32[]{:S(2)}, u32[]{:S(2)}) %collective-permute-start.2) | collective-permute-done | bytes 45088 | tf_op jit(solution)/shard_map/ppermute | solution.py:149
  12.5 1.6 collective-permute-start.4
  14.0 1.5 collective-permute-start.6
  15.5 1.0 constant_dynamic-slice_fusion
  16.7 2.7 %collective-permute-start.13 = (bf16[176,352]{1,0:T(8,128)(2,1)S(1)}, bf16[176,352]{1,0:T(8,128)(2,1)S(1)}, u32[]{:S(2)}, u32[]{:S(2)}) collective-permute-start(bf16[176,352]{1,0:T(8,128)(2,1)S(1)} %constant_dynamic-slice_fusion), channel_id=1, source_target_pairs={{0,4},{1,5},{2,6},{3,7},{4,0},{5,1},{6,2},{7,3},{8,12},{9,13},{10,... | collective-permute-start | bytes 371720 | tf_op jit(solution)/shard_map/ppermute | solution.py:149
  19.4 1.6 collective-permute-start.14
  21.0 0.6 collective-permute-start.10
  21.6 0.6 collective-permute-start.8
  22.2 6.4 %collective-permute-done.13 = bf16[176,352]{1,0:T(8,128)(2,1)S(1)} collective-permute-done((bf16[176,352]{1,0:T(8,128)(2,1)S(1)}, bf16[176,352]{1,0:T(8,128)(2,1)S(1)}, u32[]{:S(2)}, u32[]{:S(2)}) %collective-permute-start.13) | collective-permute-done | bytes 123936 | tf_op jit(solution)/shard_map/ppermute | solution.py:149
  28.9 0.5 collective-permute-start.18
  29.4 0.5 collective-permute-start.16
  30.0 0.5 collective-permute-start.11
  30.7 8.4 %collective-permute-done.18.refs_4_ = bf16[4,176,352]{2,1,0:T(8,128)(2,1)S(1)} collective-permute-done((bf16[4,176,352]{2,1,0:T(8,128)(2,1)S(1)}, bf16[4,176,352]{2,1,0:T(8,128)(2,1)S(1)}, u32[]{:S(2)}, u32[]{:S(2)}) %collective-permute-start.18) | collective-permute-done | bytes 495648 | tf_op jit(solution)/shard_map/ppermute | solution.py:149
  39.1 0.8 slice.84
  40.3 0.7 slice.85
  41.3 0.5 collective-permute-start.20
  41.8 0.8 collective-permute-start.22
  43.8 0.5 collective-permute-start.19
  44.4 0.6 pad_add_fusion.where
  45.3 12.6 %shard_map.109 = (bf16[4,128,1408]{2,1,0:T(8,128)(2,1)}, f32[4,128]{1,0:T(4,128)}) custom-call(s32[3]{0:T(128)} %pad_add_fusion.where, bf16[1024,1408]{1,0:T(8,128)(2,1)} %bitcast.66, bf16[4,176,128]{2,1,0:T(8,128)(2,1)} %copy-done.8, bf16[4,176,128]{2,1,0:T(8,128)(2,1)} %copy-done.20, bf16[4,176,128]{2,1,0:T(8,128)(2,1)} %copy-done.13, ...), custom_call_target="tpu_custom_call" | custom-call | tf_op jit(solution)/shard_map/pallas_call | solution.py:367
  57.9 0.8 reshape.151
  59.4 1.6 collective-permute-start.27
  61.0 0.7 maximum_maximum_fusion.states
  61.8 0.6 copy-done.18
  62.7 0.6 copy-done.11
  63.3 4.6 %shard_map.110 = bf16[32,1536]{1,0:T(8,128)(2,1)} custom-call(s32[3]{0:T(128)} %pad_add_fusion.where, bf16[4,128,1408]{2,1,0:T(8,128)(2,1)} %get-tuple-element.14.pooled_frames, bf16[4,32,32]{2,1,0:T(8,128)(2,1)} %maximum_maximum_fusion.states, bf16[4,176,352]{2,1,0:T(8,128)(2,1)} %copy-done.4, bf16[4,176,352]{2,1,0:T(8,128)(2,1)} %copy-done.9, ...), custom_call_target="tpu_custom_call" | custom-call | tf_op jit(solution)/shard_map/pallas_call | solution.py:367
  68.0 8.0 %all-gather = bf16[128,1536]{1,0:T(8,128)(2,1)} all-gather(bf16[32,1536]{1,0:T(8,128)(2,1)} %shard_map.110), channel_id=2, replica_groups=mesh['frame'=4,'expert'=8] {'frame'}, dimensions={0}, use_global_device_ids=true | all-gather | bytes 491520 | tf_op jit(solution)/shard_map/all_gather | solution.py:426
  75.9 2.6 %shard_map.111 = bf16[4,32,384]{2,1,0:T(8,128)(2,1)} custom-call(s32[1]{0:T(128)} %bitcast.where, bf16[4,32,1536]{2,1,0:T(8,128)(2,1)} %bitcast.73), custom_call_target="tpu_custom_call" | custom-call | tf_op jit(solution)/shard_map/pallas_call | solution.py:367
  78.5 0.8 slice_bitcast_fusion.7
  79.3 4.4 %collective-permute-start.24 = (bf16[32,384]{1,0:T(8,128)(2,1)S(1)}, bf16[32,384]{1,0:T(8,128)(2,1)S(1)}, u32[]{:S(2)}, u32[]{:S(2)}) collective-permute-start(bf16[32,384]{1,0:T(8,128)(2,1)S(1)} %get-tuple-element.35), channel_id=1, source_target_pairs={{0,2},{1,3},{2,0},{3,1},{4,6},{5,7},{6,4},{7,5},{8,10},{9,11},{10,... | collective-permute-start | bytes 73736 | tf_op jit(solution)/shard_map/ppermute | solution.py:149
  83.7 1.8 collective-permute-start.25
  85.5 1.4 collective-permute-start.26
  87.2 1.4 collective-permute-done.25
  88.6 2.5 %collective-permute-done.26 = bf16[32,384]{1,0:T(8,128)(2,1)S(1)} collective-permute-done((bf16[32,384]{1,0:T(8,128)(2,1)S(1)}, bf16[32,384]{1,0:T(8,128)(2,1)S(1)}, u32[]{:S(2)}, u32[]{:S(2)}) %collective-permute-start.26) | collective-permute-done | bytes 24608 | tf_op jit(solution)/shard_map/ppermute | solution.py:149
  91.7 1.8 collective-permute-start.29
  93.5 2.4 %collective-permute-start.30 = (bf16[32,1536]{1,0:T(8,128)(2,1)S(1)}, bf16[32,1536]{1,0:T(8,128)(2,1)S(1)}, u32[]{:S(2)}, u32[]{:S(2)}) collective-permute-start(bf16[32,1536]{1,0:T(8,128)(2,1)S(1)} %get-tuple-element.30), channel_id=1, source_target_pairs={{0,6},{1,7},{2,4},{3,5},{4,2},{5,3},{6,0},{7,1},{8,14},{9,15},{10,... | collective-permute-start | bytes 294920 | tf_op jit(solution)/shard_map/ppermute | solution.py:149
  96.3 5.2 %collective-permute-done.29 = bf16[32,1536]{1,0:T(8,128)(2,1)S(1)} collective-permute-done((bf16[32,1536]{1,0:T(8,128)(2,1)S(1)}, bf16[32,1536]{1,0:T(8,128)(2,1)S(1)}, u32[]{:S(2)}, u32[]{:S(2)}) %collective-permute-start.29) | collective-permute-done | bytes 98336 | tf_op jit(solution)/shard_map/ppermute | solution.py:149
  102.0 1.1 collective-permute-done.31
  103.1 0.8 collective-permute-start.32
  104.1 2.6 %collective-permute-done.32 = f32[32,9]{0,1:T(8,128)S(1)} collective-permute-done((f32[32,9]{0,1:T(8,128)S(1)}, f32[32,9]{0,1:T(8,128)S(1)}, u32[]{:S(2)}, u32[]{:S(2)}) %collective-permute-start.32) | collective-permute-done | bytes 1184 | tf_op jit(solution)/shard_map/ppermute | solution.py:149
  106.8 0.7 gather_fusion
  108.2 14.4 %all_to_all.10 = bf16[8,16,1536]{2,1,0:T(8,128)(2,1)S(1)} all-to-all(bf16[8,16,1536]{2,1,0:T(8,128)(2,1)S(1)} %bitcast.71), channel_id=1, replica_groups=mesh['frame'=4,'expert'=8] {'expert'}, dimensions={0} | all-to-all | bytes 786432 | tf_op jit(solution)/shard_map/all_to_all | solution.py:457
  122.6 0.8 collective-permute-start.33
  123.4 6.9 %collective-permute-done.33.own = bf16[128,1536]{1,0:T(8,128)(2,1)S(1)} collective-permute-done((bf16[128,1536]{1,0:T(8,128)(2,1)S(1)}, bf16[128,1536]{1,0:T(8,128)(2,1)S(1)}, u32[]{:S(2)}, u32[]{:S(2)}) %collective-permute-start.33) | collective-permute-done | bytes 393248 | tf_op jit(solution)/shard_map/ppermute | solution.py:149
  130.4 0.7 reshape.172.gain
  131.0 0.8 copy-done.16
  131.8 13.5 %shard_map.112 = (f32[128,2048]{1,0:T(8,128)}, f32[128,2048]{1,0:T(8,128)}, f32[128,128]{1,0:T(8,128)}) custom-call(s32[3]{0:T(128)} %pad_add_fusion.where, bf16[128,1536]{1,0:T(8,128)(2,1)} %bitcast.69, bf16[128,1536]{1,0:T(8,128)(2,1)} %copy-done.16, bf16[12,1,512]{2,1,0:T(2,128)(2,1)} %reshape.172.gain, bf16[1,6144,2048]{2,1,0:T(8,128)(2,1)} %gate_w.3, ...), custom_call_target="tpu_custom_call" | custom-call | flops 3221225472 | bytes 25165824 | tf_op jit(solution)/shard_map/pallas_call | solution.py:321
  145.3 0.7 copy-done.17
  146.1 14.3 %shard_map.113.hidden = bf16[128,2048]{1,0:T(8,128)(2,1)} custom-call(s32[3]{0:T(128)} %pad_add_fusion.where, bf16[128,1536]{1,0:T(8,128)(2,1)} %copy-done.15, bf16[128,1536]{1,0:T(8,128)(2,1)} %copy-done.17, bf16[12,1,512]{2,1,0:T(2,128)(2,1)} %reshape.172.gain, bf16[1,6144,2048]{2,1,0:T(8,128)(2,1)} %gate_w.3, bf16[1,6144,2048]{2,1,0:T(8,128)(2,1)} %up_w.3, ...), custom_call_target="tpu_custom_call" | custom-call | flops 3221225472 | bytes 25165824 | tf_op jit(solution)/shard_map/pallas_call | solution.py:321
  160.3 8.7 %shard_map.114 = bf16[2,128,1536]{2,1,0:T(8,128)(2,1)} custom-call(s32[3]{0:T(128)} %pad_add_fusion.where, bf16[128,2048]{1,0:T(8,128)(2,1)} %shard_map.113.hidden, bf16[1,2048,6144]{2,1,0:T(8,128)(2,1)} %weight.3), custom_call_target="tpu_custom_call" | custom-call | flops 1610612736 | bytes 12582912 | tf_op jit(solution)/shard_map/pallas_call | solution.py:344
  169.1 1.0 slice_bitcast_fusion.2
  170.1 0.5 collective-permute-start.36
  170.6 8.7 %shard_map.115 = bf16[2,128,1536]{2,1,0:T(8,128)(2,1)} custom-call(s32[3]{0:T(128)} %pad_add_fusion.where, bf16[128,2048]{1,0:T(8,128)(2,1)} %shard_map.113.hidden, bf16[1,2048,6144]{2,1,0:T(8,128)(2,1)} %weight.3), custom_call_target="tpu_custom_call" | custom-call | flops 1610612736 | bytes 12582912 | tf_op jit(solution)/shard_map/pallas_call | solution.py:344
  179.3 1.1 slice_bitcast_fusion
  180.8 0.9 collective-permute-start.38
  181.7 0.5 collective-permute-done.37
  182.2 10.0 %collective-permute-done.38 = bf16[128,1536]{1,0:T(8,128)(2,1)S(1)} collective-permute-done((bf16[128,1536]{1,0:T(8,128)(2,1)S(1)}, bf16[128,1536]{1,0:T(8,128)(2,1)S(1)}, u32[]{:S(2)}, u32[]{:S(2)}) %collective-permute-start.38) | collective-permute-done | bytes 393248 | tf_op jit(solution)/shard_map/ppermute | solution.py:149
  192.4 17.4 %all_to_all.11 = bf16[8,16,1536]{2,1,0:T(8,128)(2,1)S(1)} all-to-all(bf16[8,16,1536]{2,1,0:T(8,128)(2,1)S(1)} %bitcast.72), channel_id=1, replica_groups=mesh['frame'=4,'expert'=8] {'expert'}, dimensions={0} | all-to-all | bytes 786432 | tf_op jit(solution)/shard_map/all_to_all | solution.py:472
  209.7 0.9 fusion
  (134 shorter events, 6.3 us)
Async XLA Ops:
  0.0 101.6 %copy-start = (bf16[6144,8]{0,1:T(8,128)(2,1)S(1)}, bf16[6144,8]{0,1:T(8,128)(2,1)}, u32[]{:S(2)}) copy-start(bf16[6144,8]{0,1:T(8,128)(2,1)} %param.17) | copy-start | bytes 294916
  2.4 28.1 %copy-start.26 = (s32[32,2]{0,1:T(2,128)S(1)}, s32[32,2]{0,1:T(2,128)}, u32[]{:S(2)}) copy-start(s32[32,2]{0,1:T(2,128)} %param.18) | copy-start | bytes 772
  2.4 6.6 %collective-permute-start.1 = (bf16[176,128]{1,0:T(8,128)(2,1)S(1)}, bf16[176,128]{1,0:T(8,128)(2,1)S(1)}, u32[]{:S(2)}, u32[]{:S(2)}) collective-permute-start(bf16[176,128]{1,0:T(8,128)(2,1)S(1)} %bitcast.79), channel_id=1, source_target_pairs={{0,4},{1,5},{2,6},{3,7},{4,0},{5,1},{6,2},{7,3},{8,12},{9,13},{10,... | collective-permute-start | bytes 135176 | tf_op jit(solution)/shard_map/ppermute | solution.py:149
  6.5 5.9 %collective-permute-start.2 = (bf16[176,128]{1,0:T(8,128)(2,1)S(1)}, bf16[176,128]{1,0:T(8,128)(2,1)S(1)}, u32[]{:S(2)}, u32[]{:S(2)}) collective-permute-start(bf16[176,128]{1,0:T(8,128)(2,1)S(1)} %bitcast.80), channel_id=1, source_target_pairs={{0,6},{1,7},{2,4},{3,5},{4,2},{5,3},{6,0},{7,1},{8,14},{9,15},{10,... | collective-permute-start | bytes 135176 | tf_op jit(solution)/shard_map/ppermute | solution.py:149
  7.9 4.5 %collective-permute-start = (bf16[176,128]{1,0:T(8,128)(2,1)S(1)}, bf16[176,128]{1,0:T(8,128)(2,1)S(1)}, u32[]{:S(2)}, u32[]{:S(2)}) collective-permute-start(bf16[176,128]{1,0:T(8,128)(2,1)S(1)} %bitcast.81), channel_id=1, source_target_pairs={{0,2},{1,3},{2,0},{3,1},{4,6},{5,7},{6,4},{7,5},{8,10},{9,11},{10,... | collective-permute-start | bytes 135176 | tf_op jit(solution)/shard_map/ppermute | solution.py:149
  12.5 28.6 %copy-start.8 = (bf16[4,176,128]{2,1,0:T(8,128)(2,1)}, bf16[4,176,128]{2,1,0:T(8,128)(2,1)S(1)}, u32[]{:S(2)}) copy-start(bf16[4,176,128]{2,1,0:T(8,128)(2,1)S(1)} %pad_maximum_fusion.1.refs_0_) | copy-start | bytes 540676
  12.5 8.6 %collective-permute-start.4 = (bf16[4,176,128]{2,1,0:T(8,128)(2,1)S(1)}, bf16[4,176,128]{2,1,0:T(8,128)(2,1)S(1)}, u32[]{:S(2)}, u32[]{:S(2)}) collective-permute-start(bf16[4,176,128]{2,1,0:T(8,128)(2,1)S(1)} %pad_maximum_fusion.1.refs_0_), channel_id=1, source_target_pairs={{0,1},{1,0},{2,3},{3,2},{4,5},{5,4},{6,7},{7,6},{8,9},{9,8},{10,11... | collective-permute-start | bytes 540680 | tf_op jit(solution)/shard_map/ppermute | solution.py:149
  14.0 7.6 %collective-permute-start.6 = (bf16[4,176,128]{2,1,0:T(8,128)(2,1)S(1)}, bf16[4,176,128]{2,1,0:T(8,128)(2,1)S(1)}, u32[]{:S(2)}, u32[]{:S(2)}) collective-permute-start(bf16[4,176,128]{2,1,0:T(8,128)(2,1)S(1)} %pad_maximum_fusion.1.refs_0_), channel_id=1, source_target_pairs={{0,16},{8,24},{16,0},{24,8},{1,17},{9,25},{17,1},{25,9},{2,18},{10... | collective-permute-start | bytes 540680 | tf_op jit(solution)/shard_map/ppermute | solution.py:149
  16.6 5.7 %collective-permute-start.12 = (bf16[176,352]{1,0:T(8,128)(2,1)S(1)}, bf16[176,352]{1,0:T(8,128)(2,1)S(1)}, u32[]{:S(2)}, u32[]{:S(2)}) collective-permute-start(bf16[176,352]{1,0:T(8,128)(2,1)S(1)} %constant_dynamic-slice_fusion), channel_id=1, source_target_pairs={{0,2},{1,3},{2,0},{3,1},{4,6},{5,7},{6,4},{7,5},{8,10},{9,11},{10,... | collective-permute-start | bytes 371720 | tf_op jit(solution)/shard_map/ppermute | solution.py:149
  16.7 12.0 %collective-permute-start.13 = (bf16[176,352]{1,0:T(8,128)(2,1)S(1)}, bf16[176,352]{1,0:T(8,128)(2,1)S(1)}, u32[]{:S(2)}, u32[]{:S(2)}) collective-permute-start(bf16[176,352]{1,0:T(8,128)(2,1)S(1)} %constant_dynamic-slice_fusion), channel_id=1, source_target_pairs={{0,4},{1,5},{2,6},{3,7},{4,0},{5,1},{6,2},{7,3},{8,12},{9,13},{10,... | collective-permute-start | bytes 371720 | tf_op jit(solution)/shard_map/ppermute | solution.py:149
  19.4 9.3 %collective-permute-start.14 = (bf16[176,352]{1,0:T(8,128)(2,1)S(1)}, bf16[176,352]{1,0:T(8,128)(2,1)S(1)}, u32[]{:S(2)}, u32[]{:S(2)}) collective-permute-start(bf16[176,352]{1,0:T(8,128)(2,1)S(1)} %constant_dynamic-slice_fusion), channel_id=1, source_target_pairs={{0,6},{1,7},{2,4},{3,5},{4,2},{5,3},{6,0},{7,1},{8,14},{9,15},{10,... | collective-permute-start | bytes 371720 | tf_op jit(solution)/shard_map/ppermute | solution.py:149
  21.0 20.0 %copy-start.13 = (bf16[4,176,128]{2,1,0:T(8,128)(2,1)}, bf16[4,176,128]{2,1,0:T(8,128)(2,1)S(1)}, u32[]{:S(2)}) copy-start(bf16[4,176,128]{2,1,0:T(8,128)(2,1)S(1)} %collective-permute-done.4.refs_2_) | copy-start | bytes 540676
  21.0 7.8 %collective-permute-start.10 = (bf16[2,176,128]{2,1,0:T(8,128)(2,1)S(1)}, bf16[2,176,128]{2,1,0:T(8,128)(2,1)S(1)}, u32[]{:S(2)}, u32[]{:S(2)}) collective-permute-start(bf16[2,176,128]{2,1,0:T(8,128)(2,1)S(1)} %slice.83), channel_id=1, source_target_pairs={{0,16},{8,24},{16,0},{24,8},{1,17},{9,25},{17,1},{25,9},{2,18},{10... | collective-permute-start | bytes 270344 | tf_op jit(solution)/shard_map/ppermute | solution.py:149
  21.6 19.4 %copy-start.14 = (bf16[4,176,128]{2,1,0:T(8,128)(2,1)}, bf16[4,176,128]{2,1,0:T(8,128)(2,1)S(1)}, u32[]{:S(2)}) copy-start(bf16[4,176,128]{2,1,0:T(8,128)(2,1)S(1)} %collective-permute-done.6.refs_4_) | copy-start | bytes 540676
  21.6 7.2 %collective-permute-start.8 = (bf16[2,176,128]{2,1,0:T(8,128)(2,1)S(1)}, bf16[2,176,128]{2,1,0:T(8,128)(2,1)S(1)}, u32[]{:S(2)}, u32[]{:S(2)}) collective-permute-start(bf16[2,176,128]{2,1,0:T(8,128)(2,1)S(1)} %slice.82), channel_id=1, source_target_pairs={{0,1},{1,0},{2,3},{3,2},{4,5},{5,4},{6,7},{7,6},{8,9},{9,8},{10,11... | collective-permute-start | bytes 270344 | tf_op jit(solution)/shard_map/ppermute | solution.py:149
  28.8 29.1 %copy-start.4 = (bf16[4,176,352]{2,1,0:T(8,128)(2,1)}, bf16[4,176,352]{2,1,0:T(8,128)(2,1)S(1)}, u32[]{:S(2)}) copy-start(bf16[4,176,352]{2,1,0:T(8,128)(2,1)S(1)} %pad_maximum_fusion.refs_0_) | copy-start | bytes 1486852
  28.8 15.0 %copy-start.21 = (bf16[2,176,128]{2,1,0:T(8,128)(2,1)}, bf16[2,176,128]{2,1,0:T(8,128)(2,1)S(1)}, u32[]{:S(2)}) copy-start(bf16[2,176,128]{2,1,0:T(8,128)(2,1)S(1)} %collective-permute-done.10.refs_8_) | copy-start | bytes 270340
  28.9 14.9 %copy-start.22 = (bf16[2,176,128]{2,1,0:T(8,128)(2,1)}, bf16[2,176,128]{2,1,0:T(8,128)(2,1)S(1)}, u32[]{:S(2)}) copy-start(bf16[2,176,128]{2,1,0:T(8,128)(2,1)S(1)} %collective-permute-done.8.refs_6_) | copy-start | bytes 270340
  28.9 10.2 %collective-permute-start.18 = (bf16[4,176,352]{2,1,0:T(8,128)(2,1)S(1)}, bf16[4,176,352]{2,1,0:T(8,128)(2,1)S(1)}, u32[]{:S(2)}, u32[]{:S(2)}) collective-permute-start(bf16[4,176,352]{2,1,0:T(8,128)(2,1)S(1)} %pad_maximum_fusion.refs_0_), channel_id=1, source_target_pairs={{0,16},{8,24},{16,0},{24,8},{1,17},{9,25},{17,1},{25,9},{2,18},{10... | collective-permute-start | bytes 1486856 | tf_op jit(solution)/shard_map/ppermute | solution.py:149
  29.4 10.5 %collective-permute-start.16 = (bf16[4,176,352]{2,1,0:T(8,128)(2,1)S(1)}, bf16[4,176,352]{2,1,0:T(8,128)(2,1)S(1)}, u32[]{:S(2)}, u32[]{:S(2)}) collective-permute-start(bf16[4,176,352]{2,1,0:T(8,128)(2,1)S(1)} %pad_maximum_fusion.refs_0_), channel_id=1, source_target_pairs={{0,1},{1,0},{2,3},{3,2},{4,5},{5,4},{6,7},{7,6},{8,9},{9,8},{10,11... | collective-permute-start | bytes 1486856 | tf_op jit(solution)/shard_map/ppermute | solution.py:149
  30.0 11.1 %collective-permute-start.3 = (bf16[4,176,128]{2,1,0:T(8,128)(2,1)S(1)}, bf16[4,176,128]{2,1,0:T(8,128)(2,1)S(1)}, u32[]{:S(2)}, u32[]{:S(2)}) collective-permute-start(bf16[4,176,128]{2,1,0:T(8,128)(2,1)S(1)} %pad_maximum_fusion.1.refs_0_), channel_id=1, source_target_pairs={{0,8},{8,0},{16,24},{24,16},{1,9},{9,1},{17,25},{25,17},{2,10},{10... | collective-permute-start | bytes 540680 | tf_op jit(solution)/shard_map/ppermute | solution.py:149
  30.0 11.4 %collective-permute-start.11 = (bf16[2,176,128]{2,1,0:T(8,128)(2,1)S(1)}, bf16[2,176,128]{2,1,0:T(8,128)(2,1)S(1)}, u32[]{:S(2)}, u32[]{:S(2)}) collective-permute-start(bf16[2,176,128]{2,1,0:T(8,128)(2,1)S(1)} %collective-permute-done.10.refs_8_), channel_id=1, source_target_pairs={{0,8},{8,0},{16,24},{24,16},{1,9},{9,1},{17,25},{25,17},{2,10},{10... | collective-permute-start | bytes 270344 | tf_op jit(solution)/shard_map/ppermute | solution.py:149
  30.5 11.4 %collective-permute-start.9 = (bf16[2,176,128]{2,1,0:T(8,128)(2,1)S(1)}, bf16[2,176,128]{2,1,0:T(8,128)(2,1)S(1)}, u32[]{:S(2)}, u32[]{:S(2)}) collective-permute-start(bf16[2,176,128]{2,1,0:T(8,128)(2,1)S(1)} %collective-permute-done.8.refs_6_), channel_id=1, source_target_pairs={{0,8},{8,0},{16,24},{24,16},{1,9},{9,1},{17,25},{25,17},{2,10},{10... | collective-permute-start | bytes 270344 | tf_op jit(solution)/shard_map/ppermute | solution.py:149
  39.1 18.9 %copy-start.6 = (bf16[4,176,352]{2,1,0:T(8,128)(2,1)}, bf16[4,176,352]{2,1,0:T(8,128)(2,1)S(1)}, u32[]{:S(2)}) copy-start(bf16[4,176,352]{2,1,0:T(8,128)(2,1)S(1)} %collective-permute-done.18.refs_4_) | copy-start | bytes 1486852
  39.1 4.6 %collective-permute-start.5 = (bf16[4,176,128]{2,1,0:T(8,128)(2,1)S(1)}, bf16[4,176,128]{2,1,0:T(8,128)(2,1)}, u32[]{:S(2)}, u32[]{:S(2)}) collective-permute-start(bf16[4,176,128]{2,1,0:T(8,128)(2,1)S(1)} %collective-permute-done.4.refs_2_), channel_id=1, source_target_pairs={{0,8},{8,0},{16,24},{24,16},{1,9},{9,1},{17,25},{25,17},{2,10},{10... | collective-permute-start | bytes 540680 | tf_op jit(solution)/shard_map/ppermute | solution.py:149
  39.9 18.1 %copy-start.7 = (bf16[4,176,352]{2,1,0:T(8,128)(2,1)}, bf16[4,176,352]{2,1,0:T(8,128)(2,1)S(1)}, u32[]{:S(2)}) copy-start(bf16[4,176,352]{2,1,0:T(8,128)(2,1)S(1)} %collective-permute-done.16.refs_2_) | copy-start | bytes 1486852
  39.9 3.9 %collective-permute-start.7 = (bf16[4,176,128]{2,1,0:T(8,128)(2,1)S(1)}, bf16[4,176,128]{2,1,0:T(8,128)(2,1)}, u32[]{:S(2)}, u32[]{:S(2)}) collective-permute-start(bf16[4,176,128]{2,1,0:T(8,128)(2,1)S(1)} %collective-permute-done.6.refs_4_), channel_id=1, source_target_pairs={{0,8},{8,0},{16,24},{24,16},{1,9},{9,1},{17,25},{25,17},{2,10},{10... | collective-permute-start | bytes 540680 | tf_op jit(solution)/shard_map/ppermute | solution.py:149
  41.0 4.2 %copy-start.20 = (bf16[4,176,128]{2,1,0:T(8,128)(2,1)}, bf16[4,176,128]{2,1,0:T(8,128)(2,1)S(1)}, u32[]{:S(2)}) copy-start(bf16[4,176,128]{2,1,0:T(8,128)(2,1)S(1)} %collective-permute-done.3.refs_1_) | copy-start | bytes 540676
  41.1 18.4 %collective-permute-start.15 = (bf16[4,176,352]{2,1,0:T(8,128)(2,1)S(1)}, bf16[4,176,352]{2,1,0:T(8,128)(2,1)S(1)}, u32[]{:S(2)}, u32[]{:S(2)}) collective-permute-start(bf16[4,176,352]{2,1,0:T(8,128)(2,1)S(1)} %pad_maximum_fusion.refs_0_), channel_id=1, source_target_pairs={{0,8},{8,0},{16,24},{24,16},{1,9},{9,1},{17,25},{25,17},{2,10},{10... | collective-permute-start | bytes 1486856 | tf_op jit(solution)/shard_map/ppermute | solution.py:149
  41.3 2.4 %copy-start.23 = (bf16[2,176,128]{2,1,0:T(8,128)(2,1)}, bf16[2,176,128]{2,1,0:T(8,128)(2,1)S(1)}, u32[]{:S(2)}) copy-start(bf16[2,176,128]{2,1,0:T(8,128)(2,1)S(1)} %collective-permute-done.11.refs_9_) | copy-start | bytes 270340
  41.3 17.5 %collective-permute-start.20 = (bf16[2,176,352]{2,1,0:T(8,128)(2,1)}, bf16[2,176,352]{2,1,0:T(8,128)(2,1)}, u32[]{:S(2)}, u32[]{:S(2)}) collective-permute-start(bf16[2,176,352]{2,1,0:T(8,128)(2,1)} %slice.84), channel_id=1, source_target_pairs={{0,1},{1,0},{2,3},{3,2},{4,5},{5,4},{6,7},{7,6},{8,9},{9,8},{10,11... | collective-permute-start | bytes 743432 | tf_op jit(solution)/shard_map/ppermute | solution.py:149
  41.8 1.9 copy-start.24
  41.8 17.1 %collective-permute-start.22 = (bf16[2,176,352]{2,1,0:T(8,128)(2,1)}, bf16[2,176,352]{2,1,0:T(8,128)(2,1)}, u32[]{:S(2)}, u32[]{:S(2)}) collective-permute-start(bf16[2,176,352]{2,1,0:T(8,128)(2,1)} %slice.85), channel_id=1, source_target_pairs={{0,16},{8,24},{16,0},{24,8},{1,17},{9,25},{17,1},{25,9},{2,18},{10... | collective-permute-start | bytes 743432 | tf_op jit(solution)/shard_map/ppermute | solution.py:149
  43.7 18.0 %collective-permute-start.17 = (bf16[4,176,352]{2,1,0:T(8,128)(2,1)S(1)}, bf16[4,176,352]{2,1,0:T(8,128)(2,1)S(1)}, u32[]{:S(2)}, u32[]{:S(2)}) collective-permute-start(bf16[4,176,352]{2,1,0:T(8,128)(2,1)S(1)} %collective-permute-done.16.refs_2_), channel_id=1, source_target_pairs={{0,8},{8,0},{16,24},{24,16},{1,9},{9,1},{17,25},{25,17},{2,10},{10... | collective-permute-start | bytes 1486856 | tf_op jit(solution)/shard_map/ppermute | solution.py:149
  43.8 17.9 %collective-permute-start.19 = (bf16[4,176,352]{2,1,0:T(8,128)(2,1)S(1)}, bf16[4,176,352]{2,1,0:T(8,128)(2,1)S(1)}, u32[]{:S(2)}, u32[]{:S(2)}) collective-permute-start(bf16[4,176,352]{2,1,0:T(8,128)(2,1)S(1)} %collective-permute-done.18.refs_4_), channel_id=1, source_target_pairs={{0,8},{8,0},{16,24},{24,16},{1,9},{9,1},{17,25},{25,17},{2,10},{10... | collective-permute-start | bytes 1486856 | tf_op jit(solution)/shard_map/ppermute | solution.py:149
  58.8 2.9 %collective-permute-start.21 = (bf16[2,176,352]{2,1,0:T(8,128)(2,1)}, bf16[2,176,352]{2,1,0:T(8,128)(2,1)S(1)}, u32[]{:S(2)}, u32[]{:S(2)}) collective-permute-start(bf16[2,176,352]{2,1,0:T(8,128)(2,1)} %collective-permute-done.20.refs_6_), channel_id=1, source_target_pairs={{0,8},{8,0},{16,24},{24,16},{1,9},{9,1},{17,25},{25,17},{2,10},{10... | collective-permute-start | bytes 743432 | tf_op jit(solution)/shard_map/ppermute | solution.py:149
  58.9 2.8 %collective-permute-start.23 = (bf16[2,176,352]{2,1,0:T(8,128)(2,1)}, bf16[2,176,352]{2,1,0:T(8,128)(2,1)S(1)}, u32[]{:S(2)}, u32[]{:S(2)}) collective-permute-start(bf16[2,176,352]{2,1,0:T(8,128)(2,1)} %collective-permute-done.22.refs_8_), channel_id=1, source_target_pairs={{0,8},{8,0},{16,24},{24,16},{1,9},{9,1},{17,25},{25,17},{2,10},{10... | collective-permute-start | bytes 743432 | tf_op jit(solution)/shard_map/ppermute | solution.py:149
  59.4 3.1 %copy-start.9 = (bf16[4,176,352]{2,1,0:T(8,128)(2,1)}, bf16[4,176,352]{2,1,0:T(8,128)(2,1)S(1)}, u32[]{:S(2)}) copy-start(bf16[4,176,352]{2,1,0:T(8,128)(2,1)S(1)} %collective-permute-done.15.refs_1_) | copy-start | bytes 1486852
  59.4 27.4 %collective-permute-start.27 = (bf16[176,1536]{1,0:T(8,128)(2,1)}, bf16[176,1536]{1,0:T(8,128)(2,1)S(1)}, u32[]{:S(2)}, u32[]{:S(2)}) collective-permute-start(bf16[176,1536]{1,0:T(8,128)(2,1)} %param.15), channel_id=1, source_target_pairs={{0,1},{1,0},{2,3},{3,2},{4,5},{5,4},{6,7},{7,6},{8,9},{9,8},{10,11... | collective-permute-start | bytes 1622024 | tf_op jit(solution)/shard_map/ppermute | solution.py:149
  61.7 0.8 copy-start.19
  61.7 1.0 copy-start.10
  62.5 0.8 copy-start.11
  68.0 18.9 %copy-start.12 = (bf16[176,1536]{1,0:T(8,128)(2,1)S(1)}, bf16[176,1536]{1,0:T(8,128)(2,1)}, u32[]{:S(2)}) copy-start(bf16[176,1536]{1,0:T(8,128)(2,1)} %param.15) | copy-start | bytes 1622020
  79.3 7.9 %collective-permute-start.24 = (bf16[32,384]{1,0:T(8,128)(2,1)S(1)}, bf16[32,384]{1,0:T(8,128)(2,1)S(1)}, u32[]{:S(2)}, u32[]{:S(2)}) collective-permute-start(bf16[32,384]{1,0:T(8,128)(2,1)S(1)} %get-tuple-element.35), channel_id=1, source_target_pairs={{0,2},{1,3},{2,0},{3,1},{4,6},{5,7},{6,4},{7,5},{8,10},{9,11},{10,... | collective-permute-start | bytes 73736 | tf_op jit(solution)/shard_map/ppermute | solution.py:149
  83.7 4.9 %collective-permute-start.25 = (bf16[32,384]{1,0:T(8,128)(2,1)S(1)}, bf16[32,384]{1,0:T(8,128)(2,1)S(1)}, u32[]{:S(2)}, u32[]{:S(2)}) collective-permute-start(bf16[32,384]{1,0:T(8,128)(2,1)S(1)} %get-tuple-element.34), channel_id=1, source_target_pairs={{0,4},{1,5},{2,6},{3,7},{4,0},{5,1},{6,2},{7,3},{8,12},{9,13},{10,... | collective-permute-start | bytes 73736 | tf_op jit(solution)/shard_map/ppermute | solution.py:149
  85.5 5.6 %collective-permute-start.26 = (bf16[32,384]{1,0:T(8,128)(2,1)S(1)}, bf16[32,384]{1,0:T(8,128)(2,1)S(1)}, u32[]{:S(2)}, u32[]{:S(2)}) collective-permute-start(bf16[32,384]{1,0:T(8,128)(2,1)S(1)} %get-tuple-element.33), channel_id=1, source_target_pairs={{0,6},{1,7},{2,4},{3,5},{4,2},{5,3},{6,0},{7,1},{8,14},{9,15},{10,... | collective-permute-start | bytes 73736 | tf_op jit(solution)/shard_map/ppermute | solution.py:149
  87.2 8.8 %copy-start.25 = (bf16[6144]{0:T(1024)(128)(2,1)S(1)}, bf16[6144]{0:T(1024)(128)(2,1)}, u32[]{:S(2)}) copy-start(bf16[6144]{0:T(1024)(128)(2,1)} %param.16) | copy-start | bytes 36868
  91.5 4.8 %collective-permute-start.28 = (bf16[32,1536]{1,0:T(8,128)(2,1)S(1)}, bf16[32,1536]{1,0:T(8,128)(2,1)S(1)}, u32[]{:S(2)}, u32[]{:S(2)}) collective-permute-start(bf16[32,1536]{1,0:T(8,128)(2,1)S(1)} %get-tuple-element.29), channel_id=1, source_target_pairs={{0,2},{1,3},{2,0},{3,1},{4,6},{5,7},{6,4},{7,5},{8,10},{9,11},{10,... | collective-permute-start | bytes 294920 | tf_op jit(solution)/shard_map/ppermute | solution.py:149
  91.7 9.7 %collective-permute-start.29 = (bf16[32,1536]{1,0:T(8,128)(2,1)S(1)}, bf16[32,1536]{1,0:T(8,128)(2,1)S(1)}, u32[]{:S(2)}, u32[]{:S(2)}) collective-permute-start(bf16[32,1536]{1,0:T(8,128)(2,1)S(1)} %get-tuple-element.31), channel_id=1, source_target_pairs={{0,4},{1,5},{2,6},{3,7},{4,0},{5,1},{6,2},{7,3},{8,12},{9,13},{10,... | collective-permute-start | bytes 294920 | tf_op jit(solution)/shard_map/ppermute | solution.py:149
  93.5 7.9 %collective-permute-start.30 = (bf16[32,1536]{1,0:T(8,128)(2,1)S(1)}, bf16[32,1536]{1,0:T(8,128)(2,1)S(1)}, u32[]{:S(2)}, u32[]{:S(2)}) collective-permute-start(bf16[32,1536]{1,0:T(8,128)(2,1)S(1)} %get-tuple-element.30), channel_id=1, source_target_pairs={{0,6},{1,7},{2,4},{3,5},{4,2},{5,3},{6,0},{7,1},{8,14},{9,15},{10,... | collective-permute-start | bytes 294920 | tf_op jit(solution)/shard_map/ppermute | solution.py:149
  101.9 1.2 collective-permute-start.31
  103.1 3.7 %collective-permute-start.32 = (f32[32,9]{0,1:T(8,128)S(1)}, f32[32,9]{0,1:T(8,128)S(1)}, u32[]{:S(2)}, u32[]{:S(2)}) collective-permute-start(f32[32,9]{0,1:T(8,128)S(1)} %fusion.29), channel_id=1, source_target_pairs={{0,16},{8,24},{16,0},{24,8},{1,17},{9,25},{17,1},{25,9},{2,18},{10... | collective-permute-start | bytes 3464 | tf_op jit(solution)/shard_map/ppermute | solution.py:149
  122.6 8.5 %copy-start.5 = (bf16[8,16,1536]{2,1,0:T(8,128)(2,1)}, bf16[8,16,1536]{2,1,0:T(8,128)(2,1)S(1)}, u32[]{:S(2)}) copy-start(bf16[8,16,1536]{2,1,0:T(8,128)(2,1)S(1)} %all_to_all.10) | copy-start | bytes 1179652
  122.6 7.8 %collective-permute-start.33 = (bf16[128,1536]{1,0:T(8,128)(2,1)S(1)}, bf16[128,1536]{1,0:T(8,128)(2,1)S(1)}, u32[]{:S(2)}, u32[]{:S(2)}) collective-permute-start(bf16[128,1536]{1,0:T(8,128)(2,1)S(1)} %bitcast.67), channel_id=1, source_target_pairs={{0,16},{8,24},{16,0},{24,8},{1,17},{9,25},{17,1},{25,9},{2,18},{10... | collective-permute-start | bytes 1179656 | tf_op jit(solution)/shard_map/ppermute | solution.py:149
  123.4 7.6 %collective-permute-start.35 = (bf16[128,1536]{1,0:T(8,128)(2,1)S(1)}, bf16[128,1536]{1,0:T(8,128)(2,1)S(1)}, u32[]{:S(2)}, u32[]{:S(2)}) collective-permute-start(bf16[128,1536]{1,0:T(8,128)(2,1)S(1)} %bitcast.68), channel_id=1, source_target_pairs={{0,8},{8,0},{16,24},{24,16},{1,9},{9,1},{17,25},{25,17},{2,10},{10... | collective-permute-start | bytes 1179656 | tf_op jit(solution)/shard_map/ppermute | solution.py:149
  130.4 14.9 %copy-start.15 = (bf16[128,1536]{1,0:T(8,128)(2,1)}, bf16[128,1536]{1,0:T(8,128)(2,1)S(1)}, u32[]{:S(2)}) copy-start(bf16[128,1536]{1,0:T(8,128)(2,1)S(1)} %collective-permute-done.33.own) | copy-start | bytes 1179652
  130.4 14.9 %collective-permute-start.34 = (bf16[128,1536]{1,0:T(8,128)(2,1)S(1)}, bf16[128,1536]{1,0:T(8,128)(2,1)S(1)}, u32[]{:S(2)}, u32[]{:S(2)}) collective-permute-start(bf16[128,1536]{1,0:T(8,128)(2,1)S(1)} %collective-permute-done.33.own), channel_id=1, source_target_pairs={{0,8},{8,0},{16,24},{24,16},{1,9},{9,1},{17,25},{25,17},{2,10},{10... | collective-permute-start | bytes 1179656 | tf_op jit(solution)/shard_map/ppermute | solution.py:149
  131.0 0.8 copy-start.16
  170.1 10.6 %copy-start.3 = (bf16[2,128,1536]{2,1,0:T(8,128)(2,1)S(1)}, bf16[2,128,1536]{2,1,0:T(8,128)(2,1)}, u32[]{:S(2)}) copy-start(bf16[2,128,1536]{2,1,0:T(8,128)(2,1)} %shard_map.114) | copy-start | bytes 2359300
  170.1 10.6 %collective-permute-start.36 = (bf16[128,1536]{1,0:T(8,128)(2,1)S(1)}, bf16[128,1536]{1,0:T(8,128)(2,1)S(1)}, u32[]{:S(2)}, u32[]{:S(2)}) collective-permute-start(bf16[128,1536]{1,0:T(8,128)(2,1)S(1)} %slice_bitcast_fusion.2), channel_id=1, source_target_pairs={{0,8},{8,0},{16,24},{24,16},{1,9},{9,1},{17,25},{25,17},{2,10},{10... | collective-permute-start | bytes 1179656 | tf_op jit(solution)/shard_map/ppermute | solution.py:149
  179.3 12.9 %copy-start.2 = (bf16[2,128,1536]{2,1,0:T(8,128)(2,1)S(1)}, bf16[2,128,1536]{2,1,0:T(8,128)(2,1)}, u32[]{:S(2)}) copy-start(bf16[2,128,1536]{2,1,0:T(8,128)(2,1)} %shard_map.115) | copy-start | bytes 2359300
  180.4 1.8 collective-permute-start.37
  180.7 30.0 %copy-start.1 = (bf16[6144,8]{0,1:T(8,128)(2,1)S(1)}, bf16[6144,8]{0,1:T(8,128)(2,1)}, u32[]{:S(2)}) copy-start(bf16[6144,8]{0,1:T(8,128)(2,1)} %param.17) | copy-start | bytes 294916
  180.8 11.4 %collective-permute-start.38 = (bf16[128,1536]{1,0:T(8,128)(2,1)S(1)}, bf16[128,1536]{1,0:T(8,128)(2,1)S(1)}, u32[]{:S(2)}, u32[]{:S(2)}) collective-permute-start(bf16[128,1536]{1,0:T(8,128)(2,1)S(1)} %fusion.32), channel_id=1, source_target_pairs={{0,16},{8,24},{16,0},{24,8},{1,17},{9,25},{17,1},{25,9},{2,18},{10... | collective-permute-start | bytes 1179656 | tf_op jit(solution)/shard_map/ppermute | solution.py:149
  (2 other events, 1.4 us)

commit v2 on v0

--- a/solution.py
+++ b/solution.py
@@ -1,8 +1,11 @@
+import functools
 import math
 
 import jax
 import jax.numpy as jnp
 from jax import lax
+from jax.experimental import pallas as pl
+from jax.experimental.pallas import tpu as pltpu
 from jax.sharding import PartitionSpec as P
 
 HEADS = 16
@@ -143,6 +146,411 @@
     return (x_float + jnp.transpose(moe_part)).astype(jnp.bfloat16)
 
 
+def swap(value, axis, bits, size):
+    return lax.ppermute(value, axis, [(i, i ^ bits) for i in range(size)])
+
+
+def hold(value, *earlier):
+    if not earlier:
+        return value
+    there = functools.reduce(jnp.logical_and, [array[(0,) * array.ndim] < jnp.inf for array in earlier])
+    return jnp.where(there, value, jnp.zeros((), value.dtype))
+
+
+PIECES = tuple(tuple((2 * d + e_bit, f_bits) for d in range(4)) for e_bit, f_bits in ((0, 0), (1, 0), (0, 2), (1, 2)))
+PLACES = tuple(places for group in PIECES for places in (group, tuple((e, f + 1) for e, f in group)))
+
+
+def along_z(piece):
+    return jnp.stack([piece] + [swap(piece, "expert", 2 * d, 8) for d in (1, 2, 3)])
+
+
+def spread(column):
+    diagonal = [(8 * f + e, 8 * (f ^ 2) + (e ^ 1)) for f in range(4) for e in range(8)]
+    by_x = swap(column, "expert", 1, 8)
+    by_y = swap(column, "frame", 2, 4)
+    by_both = lax.ppermute(column, ("frame", "expert"), diagonal)
+    groups = []
+    for value in (column, by_x, by_y, by_both):
+        groups += [value, swap(value, "frame", 1, 4)]
+    return groups, by_both
+
+
+def each_piece(where, pieces):
+    rows = pieces[0].shape[1]
+    for places, piece in zip(PLACES, pieces):
+        for at, (e_bits, f_bits) in enumerate(places):
+            row = pl.multiple_of((where[0] ^ e_bits) * rows, 16)
+            yield pl.ds(row, rows), where[1] ^ f_bits, piece[at]
+
+
+def attend_body(where, frames, *refs):
+    pieces, (pooled_frames, states, whole) = refs[: len(PLACES)], refs[-3:]
+    for row_range, column, piece in each_piece(where, pieces):
+        columns = piece.shape[1]
+        whole[row_range, pl.ds(pl.multiple_of(column * columns, 128), columns)] = piece
+    tokens = frames.shape[0]
+    half = whole.shape[1] // 2
+    valid = lax.broadcasted_iota(jnp.int32, (tokens, half), 0) < where[2]
+    for part in range(2):
+        columns = pl.ds(part * half, half)
+        scores = jnp.dot(frames[...], whole[:, columns], preferred_element_type=jnp.float32)
+        masked = jnp.where(valid, scores, NEG_BIG)
+        peak = jnp.max(masked, axis=0, keepdims=True)
+        expos = jnp.where(valid, jnp.exp(masked - peak), 0.0)
+        total = jnp.sum(expos, axis=0, keepdims=True)
+        some = total > 0.0
+        safe = jnp.where(some, total, 1.0)
+        weights = (expos * (1.0 / safe)).astype(jnp.bfloat16)
+        states[:, columns] = jnp.where(some, peak + jnp.log(safe), NEG_BIG)
+        pooled_frames[columns, :] = lax.dot_general(
+            weights, frames[...], (((0,), (0,)), ((), ())), preferred_element_type=jnp.float32
+        ).astype(jnp.bfloat16)
+
+
+def values_body(where, pooled_frames, states, *refs):
+    pieces, (packed, whole) = refs[: len(PLACES)], refs[len(PLACES) :]
+    for row_range, column, piece in each_piece(where, pieces):
+        whole[column, row_range, :] = piece
+    groups, _, width = whole.shape
+    head_size = width // 4
+    pairs = pooled_frames.shape[0] // groups
+    latents = pairs // 4
+    head_of = lax.broadcasted_iota(jnp.int32, (latents, width), 1) // head_size
+    for group in range(groups):
+        rows = pooled_frames[group * pairs : (group + 1) * pairs, :]
+        every = jnp.dot(rows, whole[group], preferred_element_type=jnp.float32)
+        own = jnp.zeros((latents, width), jnp.float32)
+        for head in range(4):
+            own = jnp.where(head_of == head, every[head * latents : (head + 1) * latents, :], own)
+        for copy in range(packed.shape[1]):
+            packed[group, copy, :, :width] = own.astype(jnp.bfloat16)
+            packed[group, copy, :, width:] = states[group]
+
+
+def combine_body(where, parts, pooled):
+    latents = parts.shape[2]
+    width = 352
+    head_size = width // 4
+    head_of = lax.broadcasted_iota(jnp.int32, (latents, width), 1) // head_size
+    for turn in range(4):
+        logs, values = [], []
+        for part in range(4):
+            block = parts[where[0] ^ turn, part].astype(jnp.float32)
+            state = block[:, width : width + 4] + block[:, width + 4 : width + 8]
+            state = state + block[:, width + 8 : width + 12]
+            logs.append(state)
+            values.append(block[:, :width])
+        peak = jnp.maximum(jnp.maximum(logs[0], logs[1]), jnp.maximum(logs[2], logs[3]))
+        shares = [jnp.exp(state - peak) for state in logs]
+        inverse = 1.0 / (shares[0] + shares[1] + shares[2] + shares[3])
+        joined_up = jnp.zeros((latents, width), jnp.float32)
+        for share, value in zip(shares, values):
+            share = share * inverse
+            spread_out = jnp.zeros((latents, width), jnp.float32)
+            for head in range(4):
+                spread_out = jnp.where(head_of == head, share[:, head : head + 1], spread_out)
+            joined_up = joined_up + value * spread_out
+        pooled[turn] = jnp.zeros((latents, 384), jnp.bfloat16)
+        pooled[turn, :, :width] = joined_up.astype(jnp.bfloat16)
+
+
+DEPTH = 256
+DOWN_WIDTH = 256
+SLOTS = 5
+
+
+def streamed(blocks):
+    depth = SLOTS
+    copies = [
+        [
+            pltpu.make_async_copy(source, buffer.at[at % depth], semaphores.at[which, at % depth])
+            for which, (source, buffer) in enumerate(zip(sources, buffers))
+        ]
+        for at, (sources, buffers, semaphores, _) in enumerate(blocks)
+    ]
+    for group in copies[: depth - 1]:
+        for copy in group:
+            copy.start()
+    for at, (_, buffers, _, work) in enumerate(blocks):
+        if at + depth - 1 < len(blocks):
+            for copy in copies[at + depth - 1]:
+                copy.start()
+        for copy in copies[at]:
+            copy.wait()
+        work(*[buffer.at[at % depth] for buffer in buffers])
+
+
+def entering(where, bits, rows, gain, gate_w, up_w, gate_sum, up_sum, squares, gate_buffer, up_buffer, semaphores):
+    steps = rows[0].shape[1] // DEPTH
+    for turn, source in enumerate(rows):
+        chunk = where[1] ^ (bits + turn)
+        for at in range(steps):
+            block_index = chunk * steps + at
+            depth_rows = pl.ds(pl.multiple_of(block_index * DEPTH, DEPTH), DEPTH)
+
+            def work(gate_block, up_block, source=source, at=at, block_index=block_index, first=turn + at == 0):
+                block = source[:, at * DEPTH : (at + 1) * DEPTH].astype(jnp.float32)
+                total = jnp.sum(block * block, axis=1, keepdims=True)
+                gained = (block * gain[block_index].astype(jnp.float32)).astype(jnp.bfloat16)
+                gate_part = jnp.dot(gained, gate_block[...], preferred_element_type=jnp.float32)
+                up_part = jnp.dot(gained, up_block[...], preferred_element_type=jnp.float32)
+                if first:
+                    squares[...] = jnp.broadcast_to(total, squares.shape)
+                    gate_sum[...] = gate_part
+                    up_sum[...] = up_part
+                else:
+                    squares[...] += jnp.broadcast_to(total, squares.shape)
+                    gate_sum[...] += gate_part
+                    up_sum[...] += up_part
+
+            sources = (gate_w.at[0, depth_rows, :], up_w.at[0, depth_rows, :])
+            yield sources, (gate_buffer, up_buffer), semaphores, work
+
+
+def leaving(where, bits, hidden, down_w, parts, buffer, semaphores):
+    steps = parts.shape[2] // DOWN_WIDTH
+    for turn, bit in enumerate(bits):
+        for at in range(steps):
+            start = pl.multiple_of(((where[1] ^ bit) * steps + at) * DOWN_WIDTH, DOWN_WIDTH)
+
+            def work(down_block, turn=turn, at=at):
+                parts[turn, :, at * DOWN_WIDTH : (at + 1) * DOWN_WIDTH] = jnp.dot(
+                    hidden[...], down_block[...], preferred_element_type=jnp.float32
+                ).astype(jnp.bfloat16)
+
+            yield (down_w.at[0, :, pl.ds(start, DOWN_WIDTH)],), (buffer,), semaphores, work
+
+
+def near_body(where, own, other, gain, gate_w, up_w, gate_sum, up_sum, squares, *scratch):
+    streamed(list(entering(where, 0, (own, other), gain, gate_w, up_w, gate_sum, up_sum, squares, *scratch)))
+
+
+def far_body(where, own, other, gain, gate_w, up_w, gate_in, up_in, squares_in, down_w, hidden, parts, *scratch):
+    (gate_sum, up_sum, squares), buffers, (down_buffer, down_semaphores) = scratch[:3], scratch[3:6], scratch[6:]
+    blocks = list(entering(where, 2, (own, other), gain, gate_w, up_w, gate_sum, up_sum, squares, *buffers))
+    last_work = blocks[-1][3]
+
+    def finish(gate_block, up_block):
+        last_work(gate_block, up_block)
+        mean = (squares[:, :1] + squares_in[:, :1]) / up_w.shape[1]
+        scale = lax.rsqrt(mean + EPSILON)
+        gate_val = (gate_sum[...] + gate_in[...]) * scale
+        up_val = (up_sum[...] + up_in[...]) * scale
+        hidden[...] = (gate_val / (1.0 + jnp.exp(-gate_val)) * up_val).astype(jnp.bfloat16)
+
+    blocks[-1] = (*blocks[-1][:3], finish)
+    streamed(blocks + list(leaving(where, (2, 3), hidden, down_w, parts, down_buffer, down_semaphores)))
+
+
+def last_body(bit, where, hidden, down_w, before, parts, buffer, semaphores):
+    streamed(list(leaving(where, (bit,), hidden, down_w, parts, buffer, semaphores)))
+
+
+def cost(flops, moved):
+    return pl.CostEstimate(flops=flops, transcendentals=0, bytes_accessed=moved)
+
+
+SMEM_SPEC = pl.BlockSpec(memory_space=pltpu.SMEM)
+VMEM_SPEC = pl.BlockSpec(memory_space=pltpu.VMEM)
+HBM_SPEC = pl.BlockSpec(memory_space=pltpu.HBM)
+
+
+def weight_buffers(hidden_width):
+    block = pltpu.VMEM((SLOTS, DEPTH, hidden_width), jnp.bfloat16)
+    return [block, block, pltpu.SemaphoreType.DMA((2, SLOTS))]
+
+
+def down_buffers(hidden_width):
+    return [pltpu.VMEM((SLOTS, hidden_width, DOWN_WIDTH), jnp.bfloat16), pltpu.SemaphoreType.DMA((1, SLOTS))]
+
+
+def expert_near(where, own, other, gain, gate_w, up_w):
+    rows, columns = own.shape
+    hidden_width = up_w.shape[2]
+    sums = [jax.ShapeDtypeStruct((rows, wide), jnp.float32) for wide in (hidden_width, hidden_width, 128)]
+    return pl.pallas_call(
+        near_body,
+        out_shape=sums,
+        in_specs=[SMEM_SPEC] + [VMEM_SPEC] * 3 + [HBM_SPEC] * 2,
+        out_specs=[VMEM_SPEC] * 3,
+        scratch_shapes=weight_buffers(hidden_width),
+        compiler_params=pltpu.CompilerParams(vmem_limit_bytes=20 * 2**20),
+        cost_estimate=cost(8 * rows * columns * hidden_width, 8 * columns * hidden_width),
+    )(where, own, other, gain, gate_w, up_w)
+
+
+def expert_far(where, own, other, gain, gate_w, up_w, near, down_w):
+    rows, columns = own.shape
+    hidden_width = up_w.shape[2]
+    return pl.pallas_call(
+        far_body,
+        out_shape=(
+            jax.ShapeDtypeStruct((rows, hidden_width), jnp.bfloat16),
+            jax.ShapeDtypeStruct((2, rows, columns), jnp.bfloat16),
+        ),
+        in_specs=[SMEM_SPEC] + [VMEM_SPEC] * 3 + [HBM_SPEC] * 2 + [VMEM_SPEC] * 3 + [HBM_SPEC],
+        out_specs=(VMEM_SPEC, VMEM_SPEC),
+        scratch_shapes=[pltpu.VMEM(s.shape, s.dtype) for s in near]
+        + weight_buffers(hidden_width)
+        + down_buffers(hidden_width),
+        compiler_params=pltpu.CompilerParams(vmem_limit_bytes=32 * 2**20),
+        cost_estimate=cost(12 * rows * columns * hidden_width, 12 * columns * hidden_width),
+    )(where, own, other, gain, gate_w, up_w, *near, down_w)
+
+
+def expert_last(where, bit, hidden, down_w, before, columns):
+    rows, depth = hidden.shape
+    return pl.pallas_call(
+        functools.partial(last_body, bit),
+        out_shape=jax.ShapeDtypeStruct((1, rows, columns), jnp.bfloat16),
+        in_specs=[SMEM_SPEC, VMEM_SPEC, HBM_SPEC, pl.BlockSpec(memory_space=pl.ANY)],
+        out_specs=VMEM_SPEC,
+        scratch_shapes=down_buffers(depth),
+        compiler_params=pltpu.CompilerParams(vmem_limit_bytes=16 * 2**20),
+        cost_estimate=cost(2 * rows * depth * columns, 2 * depth * columns),
+    )(where, hidden, down_w, before)
+
+
+def in_vmem(body, out_shape, limit, scratch=()):
+    space = lambda _: pl.BlockSpec(memory_space=pltpu.VMEM)
+
+    def call(where, *operands):
+        return pl.pallas_call(
+            body,
+            out_shape=out_shape,
+            in_specs=[pl.BlockSpec(memory_space=pltpu.SMEM)] + [space(o) for o in operands],
+            out_specs=jax.tree.map(space, out_shape),
+            scratch_shapes=list(scratch),
+            compiler_params=pltpu.CompilerParams(vmem_limit_bytes=limit * 2**20),
+        )(where, *operands)
+
+    return call
+
+
+def fast_local(
+    frames, frame_counts, latents, w_kv, w_proj, norm_gain, router, expert_ids, w_gate, w_up, w_down
+):
+    _, frame_tokens, width = frames.shape
+    latent_count = latents.shape[0]
+    head_size = width // HEADS
+    e, f = lax.axis_index("expert"), lax.axis_index("frame")
+    rows = w_kv.shape[0]
+    quarter = width // 4
+    frames_here = frame_tokens // PATCH
+    valid_tokens = jnp.clip((frame_counts[0] - f * frames_here) * PATCH, 0, frame_tokens)
+    where = jnp.stack([e, f, valid_tokens]).astype(jnp.int32)
+
+    expert_total = router.shape[1]
+    capacity = latent_count // 2
+    pair_ids = expert_ids.reshape(-1)
+    onehot = (pair_ids[:, None] == jnp.arange(expert_total, dtype=jnp.int32)[None, :]).astype(jnp.int32)
+    pair_at = jnp.arange(pair_ids.shape[0], dtype=jnp.int32)
+    before = (pair_at[:, None] > pair_at[None, :]).astype(jnp.float32)
+    earlier_hits = jnp.dot(before, onehot.astype(jnp.float32)).astype(jnp.int32)
+    position = jnp.sum(earlier_hits * onehot, axis=-1)
+    slot_of = pair_ids * capacity + position
+    pair_hit = (
+        slot_of[None, :] == jnp.arange(expert_total * capacity, dtype=jnp.int32)[:, None]
+    ).astype(jnp.float32)
+    select = pair_hit.reshape(-1, latent_count, 2).sum(-1).astype(jnp.bfloat16)
+
+    head_here = f * 4 + jnp.arange(4, dtype=jnp.int32)
+    head_of = jnp.arange(width, dtype=jnp.int32) // head_size
+    spaced = jnp.where(
+        head_here[:, None, None] == head_of[None, None, :], latents[None], jnp.zeros((), jnp.bfloat16)
+    ).reshape(4 * latent_count, width)
+    asked = lax.dot_general(
+        w_kv[:, :width], spaced, (((1,), (1,)), ((), ())), preferred_element_type=jnp.float32
+    )
+    asked = (asked / math.sqrt(head_size)).astype(jnp.bfloat16)
+    asked_pieces, asked_last = spread(along_z(asked))
+    value_piece = lax.dynamic_slice(w_kv, (0, width + f * quarter), (rows, quarter))
+    value_column = along_z(value_piece)
+    pooled_frames, states = in_vmem(
+        attend_body,
+        (
+            jax.ShapeDtypeStruct((HEADS * latent_count, width), jnp.bfloat16),
+            jax.ShapeDtypeStruct((1, HEADS * latent_count), jnp.float32),
+        ),
+        28,
+        [pltpu.VMEM((width, HEADS * latent_count), jnp.bfloat16)],
+    )(where, frames[0], *asked_pieces, select)
+    value_pieces, value_last = spread(value_column)
+    proj_other = swap(hold(w_proj, value_last), "expert", 1, 8)
+    by_latent = jnp.transpose(states.reshape(4, 4, latent_count), (0, 2, 1))
+    high = lax.reduce_precision(by_latent, 8, 7)
+    middle = lax.reduce_precision(by_latent - high, 8, 7)
+    low = (by_latent - high) - middle
+    blank = jnp.zeros((4, latent_count, 20), jnp.float32)
+    state_columns = jnp.concatenate([high, middle, low, blank], axis=-1).astype(jnp.bfloat16)
+    packed = in_vmem(
+        values_body,
+        jax.ShapeDtypeStruct((4, 4, latent_count, 384), jnp.bfloat16),
+        20,
+        [pltpu.VMEM((4, width, quarter), jnp.bfloat16)],
+    )(where, pooled_frames, state_columns, *value_pieces)
+    same_x = [[8 * part + 2 * z + x for z in range(4) for part in range(4)] for x in range(2)]
+    parts = lax.all_to_all(
+        packed.reshape(16 * latent_count, 384), ("frame", "expert"), 0, 0, axis_index_groups=same_x, tiled=True
+    ).reshape(4, 4, latent_count, 384)
+    z_index = jnp.stack([e // 2]).astype(jnp.int32)
+    pooled = in_vmem(combine_body, jax.ShapeDtypeStruct((4, latent_count, 384), jnp.bfloat16), 8)(z_index, parts)
+
+    own_first = e % 2 == 0
+    proj_rows = jnp.where(
+        own_first, jnp.concatenate([w_proj, proj_other]), jnp.concatenate([proj_other, w_proj])
+    )
+    proj_rows = jnp.pad(proj_rows, ((0, 384 - 2 * rows), (0, 0)))
+    partial = jnp.dot(pooled.reshape(4 * latent_count, 384), proj_rows, preferred_element_type=jnp.float32).astype(jnp.bfloat16)
+    partial = partial.reshape(4, latent_count, -1)
+    x_sum = partial[0].astype(jnp.float32)
+    for d in (1, 2, 3):
+        x_sum = x_sum + swap(partial[d], "expert", 2 * d, 8).astype(jnp.float32)
+    x_part = x_sum.astype(jnp.bfloat16)
+    x_float = x_part.astype(jnp.float32)
+    part_width = x_part.shape[1]
+
+    send_rows = jnp.dot(select, x_part, preferred_element_type=jnp.float32).astype(jnp.bfloat16)
+    arrived = lax.all_to_all(
+        send_rows.reshape(expert_total, capacity, part_width), "expert", split_axis=0, concat_axis=0, tiled=True
+    ).reshape(-1, part_width)
+
+    gain = norm_gain.reshape(-1, 1, DEPTH)
+    w_gate, w_up, w_down = (pltpu.with_memory_space_constraint(w, pltpu.HBM) for w in (w_gate, w_up, w_down))
+    from_core = swap(arrived, "frame", 1, 4)
+    from_y = swap(arrived, "frame", 2, 4)
+    near = expert_near(where, arrived, from_core, gain, w_gate, w_up)
+    from_both = swap(hold(from_y, near[2]), "frame", 1, 4)
+    hidden, far_parts = expert_far(where, from_y, from_both, gain, w_gate, w_up, near, w_down)
+    chip_far = far_parts[0].astype(jnp.float32) + swap(far_parts[1], "frame", 1, 4).astype(jnp.float32)
+    chip_far = chip_far.astype(jnp.bfloat16)
+    y_sum = swap(chip_far, "frame", 2, 4)
+    for_core = expert_last(where, 1, hidden, w_down, chip_far, part_width)
+    for_own = expert_last(where, 0, hidden, w_down, for_core, part_width)
+    own_sum = for_own[0].astype(jnp.float32) + swap(for_core[0], "frame", 1, 4).astype(jnp.float32)
+    summed = (own_sum + y_sum.astype(jnp.float32)).astype(jnp.bfloat16)
+    returned = lax.all_to_all(
+        summed.reshape(expert_total, capacity, part_width), "expert", split_axis=0, concat_axis=0, tiled=True
+    ).reshape(-1, part_width)
+
+    gain_here = lax.dynamic_slice(norm_gain, (f * part_width,), (part_width,)).astype(jnp.float32)
+    router_here = lax.dynamic_slice(router, (f * part_width, 0), (part_width, expert_total)).astype(jnp.float32)
+    raw = jnp.dot(x_float * gain_here, router_here, precision=lax.Precision.HIGHEST)
+    sums = jnp.concatenate([raw, jnp.sum(x_float * x_float, axis=-1, keepdims=True)], axis=-1)
+    sums = hold(sums, chip_far)
+    sums = sums + swap(sums, "frame", 1, 4) + swap(sums, "frame", 2, 4) + swap(sums, "frame", 3, 4)
+    scale = lax.rsqrt(sums[:, expert_total] / router.shape[0] + EPSILON)
+    logits = sums[:, :expert_total] * scale[:, None]
+    chosen = jnp.take_along_axis(logits, expert_ids, axis=1)
+    gates = jax.nn.softmax(chosen, axis=-1)
+    mixing = (pair_hit * gates.reshape(-1)[None, :]).reshape(-1, latent_count, 2).sum(-1)
+    moe_part = lax.dot_general(
+        mixing, returned.astype(jnp.float32), (((0,), (0,)), ((), ())), precision=lax.Precision.HIGHEST
+    )
+    return (x_float + moe_part).astype(jnp.bfloat16)
+
+
 def solution(mesh):
     in_specs = (
         P("expert", "frame", None),
@@ -158,4 +566,6 @@
         P("expert", "frame", None),
     )
     out_specs = P("expert", "frame")
-    return jax.shard_map(local, mesh=mesh, in_specs=in_specs, out_specs=out_specs, check_vma=False)
+    small = mesh.shape["frame"] == 4 and mesh.shape["expert"] == 8
+    body = fast_local if small else local
+    return jax.shard_map(body, mesh=mesh, in_specs=in_specs, out_specs=out_specs, check_vma=False)

time: 342 us -> 168 us (0.49)
  waiting for transfers between devices: 172 us -> 43.6 us
  blocking collectives: 82.9 us -> 15.5 us
  matrix products: 49.8 us -> 3.33 us
  Pallas kernels: 0 us -> 45.1 us
  starting transfers between devices: 0.08 us -> 36.9 us
  between operations: 13.9 us -> 3.08 us
  local copies, waits for them, and re-layouts: 19.6 us -> 11 us
  other arithmetic: 3.75 us -> 9.2 us
    all_gather x2 -> x0, waiting for transfers between devices: 143 us -> none  [the longest x1 117 us: local(): lax.all_gather(w_kv, 'expert', axis=0, tiled=True)]
    dot_general x9 -> x6, matrix products: 49.8 us -> 3.33 us  [the longest x1 1.49 us: fast_local(): lax.dot_general(w_kv[:, :width], spaced, (((1,), (1,)), ((), ())), prefer...]
    pallas_call x0 -> x7, Pallas kernels: none -> 45.1 us  [the longest x1 14.9 us: expert_far(): pl.pallas_call(far_body, out_shape=(jax.ShapeDtypeStruct((rows, hidden_wi...]
    all_to_all x2 -> x1, blocking collectives: 57.8 us -> 15.5 us  [fast_local(): lax.all_to_all(send_rows.reshape(expert_total, capacity, part_width), 'ex...]
    ppermute x0 -> x33, starting transfers between devices: none -> 29.2 us  [the longest x31 26.2 us: swap(): return lax.ppermute(value, axis, [(i, i ^ bits) for i in range(size)])]
    reduce_scatter x1 -> x0, waiting for transfers between devices: 26.9 us -> none  [local(): lax.psum_scatter(lax.dot_general(columns, slot_rows, (((0,), (1,)), ((),...]
    ppermute x0 -> x33, waiting for transfers between devices: none -> 26.4 us  [the longest x31 26.4 us: swap(): return lax.ppermute(value, axis, [(i, i ^ bits) for i in range(size)])]
    all_gather x4 -> x0, blocking collectives: 25.2 us -> none  [the longest x3 18.7 us: joined(): pieces = jax.tree.map(lambda part: lax.all_gather(part, axis), value)]
  transfers between devices with their start and end apart: 3 -> 35, of which waited for: 3 -> 12; matrix products, arithmetic and copies ran while one was open for 10% -> 9% of each run, Pallas kernels for 0% -> 17%
where the time goes in v2:
time: 168 us
  Pallas kernels  45.1 us (27%)
  waiting for transfers between devices  43.6 us (26%)
  starting transfers between devices  36.9 us (22%)
  blocking collectives  15.5 us (9%)
  local copies, waits for them, and re-layouts  11 us (7%)
  other arithmetic  9.2 us (5%)
  matrix products  3.33 us (2%)
  between operations  3.08 us (2%)
    ppermute x31, waiting for transfers between devices, swap(): return lax.ppermute(value, axis, [(i, i ^ bits) for i in range(size)])  26.4 us
    ppermute x31, starting transfers between devices, swap(): return lax.ppermute(value, axis, [(i, i ^ bits) for i in range(size)])  26.2 us
    all_to_all x1, blocking collectives, fast_local(): lax.all_to_all(send_rows.reshape(expert_total, capacity, part_width), 'ex...  15.5 us
    pallas_call x1, Pallas kernels, expert_far(): pl.pallas_call(far_body, out_shape=(jax.ShapeDtypeStruct((rows, hidden_wi...  14.9 us
    pallas_call x3, Pallas kernels, call(): pl.pallas_call(body, out_shape=out_shape, in_specs=[pl.BlockSpec(memory_s...  11.9 us
    all_to_all x1, waiting for transfers between devices, fast_local(): lax.all_to_all(summed.reshape(expert_total, capacity, part_width), 'exper...  11.3 us
    pallas_call x1, Pallas kernels, expert_near(): pl.pallas_call(near_body, out_shape=sums, in_specs=[SMEM_SPEC] + [VMEM_SP...  9.48 us
    pallas_call x2, Pallas kernels, expert_last(): pl.pallas_call(functools.partial(last_body, bit), out_shape=jax.ShapeDtyp...  8.89 us
  transfers between devices with their start and end apart: 35, of which 12 were waited for; matrix products, arithmetic and copies ran while one was open for 9% of the time, Pallas kernels for 17%

profile of v2, /device:TPU:0, one launch (start us, length us, event | category | flops | bytes accessed | tf_op | source)
XLA Modules:
  0.0 167.8 jit_solution(11831060707187952298)
XLA Ops:
  0.1 0.9 broadcast_select_fusion.2
  1.1 1.5 fusion.2
  2.6 4.1 %collective-permute-start.1 = (bf16[176,128]{1,0:T(8,128)(2,1)S(1)}, bf16[176,128]{1,0:T(8,128)(2,1)S(1)}, u32[]{:S(2)}, u32[]{:S(2)}) collective-permute-start(bf16[176,128]{1,0:T(8,128)(2,1)S(1)} %bitcast.69), channel_id=1, source_target_pairs={{0,4},{1,5},{2,6},{3,7},{4,0},{5,1},{6,2},{7,3},{8,12},{9,13},{10,... | collective-permute-start | bytes 135176 | tf_op jit(solution)/shard_map/ppermute | solution.py:150
  6.7 1.3 collective-permute-start.2
  8.3 1.0 constant_dynamic-slice_fusion
  9.3 1.9 %collective-permute-start.10 = (bf16[176,352]{1,0:T(8,128)(2,1)S(1)}, bf16[176,352]{1,0:T(8,128)(2,1)}, u32[]{:S(2)}, u32[]{:S(2)}) collective-permute-start(bf16[176,352]{1,0:T(8,128)(2,1)S(1)} %constant_dynamic-slice_fusion), channel_id=1, source_target_pairs={{0,2},{1,3},{2,0},{3,1},{4,6},{5,7},{6,4},{7,5},{8,10},{9,11},{10,... | collective-permute-start | bytes 371720 | tf_op jit(solution)/shard_map/ppermute | solution.py:150
  11.2 1.7 %collective-permute-start.11 = (bf16[176,352]{1,0:T(8,128)(2,1)S(1)}, bf16[176,352]{1,0:T(8,128)(2,1)}, u32[]{:S(2)}, u32[]{:S(2)}) collective-permute-start(bf16[176,352]{1,0:T(8,128)(2,1)S(1)} %constant_dynamic-slice_fusion), channel_id=1, source_target_pairs={{0,4},{1,5},{2,6},{3,7},{4,0},{5,1},{6,2},{7,3},{8,12},{9,13},{10,... | collective-permute-start | bytes 371720 | tf_op jit(solution)/shard_map/ppermute | solution.py:150
  12.9 1.7 %fusion.35 = bf16[1,176,352]{2,1,0:T(8,128)(2,1)} fusion(bf16[176,2816]{1,0:T(8,128)(2,1)} %param.14, s32[]{:T(128)S(6)} %select_n.83), kind=kLoop, calls=%fused_computation.75 | loop fusion | bytes 247812 | tf_op jit(solution)/shard_map/stack | solution.py:165
  14.8 1.0 collective-permute-start.12
  15.7 0.7 pad_maximum_fusion.1.refs_0_
  16.4 1.5 collective-permute-start.4
  17.9 1.5 collective-permute-start.6
  19.4 0.5 collective-permute-start.8
  20.2 2.9 %collective-permute-done.11 = bf16[176,352]{1,0:T(8,128)(2,1)} collective-permute-done((bf16[176,352]{1,0:T(8,128)(2,1)S(1)}, bf16[176,352]{1,0:T(8,128)(2,1)}, u32[]{:S(2)}, u32[]{:S(2)}) %collective-permute-start.11) | collective-permute-done | bytes 123936 | tf_op jit(solution)/shard_map/ppermute | solution.py:150
  23.2 0.7 copy-done.8
  23.9 1.2 pad_maximum_fusion.refs_0_
  25.1 2.5 %collective-permute-start.18 = (bf16[4,176,352]{2,1,0:T(8,128)(2,1)S(1)}, bf16[4,176,352]{2,1,0:T(8,128)(2,1)}, u32[]{:S(2)}, u32[]{:S(2)}) collective-permute-start(bf16[4,176,352]{2,1,0:T(8,128)(2,1)S(1)} %pad_maximum_fusion.refs_0_), channel_id=1, source_target_pairs={{0,17},{1,16},{2,19},{3,18},{4,21},{5,20},{6,23},{7,22},{8,25},{9,... | collective-permute-start | bytes 1486856 | tf_op jit(solution)/shard_map/ppermute | solution.py:172
  27.6 0.5 collective-permute-start.14
  28.2 0.5 collective-permute-start.16
  29.3 0.6 collective-permute-start.7
  29.9 0.5 collective-permute-done.5.refs_3_
  30.6 0.7 convert_reduce_fusion
  31.2 0.8 copy.53.refs_8_
  32.1 0.7 pad.18.clone
  33.2 7.3 %shard_map.109 = (bf16[512,1408]{1,0:T(8,128)(2,1)S(1)}, f32[1,512]{1,0:T(1,128)S(1)}) custom-call(s32[3]{0:T(128)S(1)} %pad_add_fusion.where, bf16[1024,1408]{1,0:T(8,128)(2,1)S(1)} %bitcast.58, bf16[4,176,128]{2,1,0:T(8,128)(2,1)} %pad_maximum_fusion.1.refs_0_, bf16[4,176,128]{2,1,0:T(8,128)(2,1)} %collective-permute-done.3.refs_1_, ...), custom_call_target="tpu_custom_call" | custom-call | tf_op jit(solution)/shard_map/pallas_call | solution.py:419
  40.5 1.2 copy-done.2
  41.7 0.6 copy-done.6
  42.2 0.5 broadcast.128
  42.7 1.3 reduce.3
  44.2 1.2 slice.54
  46.3 6.3 %collective-permute-done.14.refs_2_ = bf16[4,176,352]{2,1,0:T(8,128)(2,1)} collective-permute-done((bf16[4,176,352]{2,1,0:T(8,128)(2,1)S(1)}, bf16[4,176,352]{2,1,0:T(8,128)(2,1)}, u32[]{:S(2)}, u32[]{:S(2)}) %collective-permute-start.14) | collective-permute-done | bytes 495648 | tf_op jit(solution)/shard_map/ppermute | solution.py:150
  52.5 0.5 collective-permute-start.17
  53.1 1.1 broadcast_select_fusion
  54.1 1.5 collective-permute-start.20
  55.9 3.7 %shard_map.110 = bf16[4,4,32,384]{3,2,1,0:T(8,128)(2,1)} custom-call(s32[3]{0:T(128)S(1)} %copy-done.5, bf16[512,1408]{1,0:T(8,128)(2,1)S(1)} %copy-done.3, bf16[4,32,32]{2,1,0:T(8,128)(2,1)S(1)} %maximum_maximum_fusion.states, bf16[4,176,352]{2,1,0:T(8,128)(2,1)S(1)} %pad_maximum_fusion.refs_0_, bf16[4,176,352]{2,1,0:T(8,128)(2,1)} %collective-permute-done.13.refs_1_, ...), custom_call_target="tpu_custom_call" | custom-call | tf_op jit(solution)/shard_map/pallas_call | solution.py:419
  59.5 4.3 %all-to-all-start = ((bf16[16,32,384]{2,1,0:T(8,128)(2,1)}), bf16[16,32,384]{2,1,0:T(8,128)(2,1)S(1)}, u32[]{:S(2)}, u32[]{:S(2)}) async-start(bf16[16,32,384]{2,1,0:T(8,128)(2,1)} %bitcast.17), calls=%async_computation | async-start | bytes 786432 | tf_op jit(solution)/shard_map/all_to_all | solution.py:494
  63.8 4.7 %collective-permute-done.20 = bf16[176,1536]{1,0:T(8,128)(2,1)} collective-permute-done((bf16[176,1536]{1,0:T(8,128)(2,1)S(1)}, bf16[176,1536]{1,0:T(8,128)(2,1)}, u32[]{:S(2)}, u32[]{:S(2)}) %collective-permute-start.20) | collective-permute-done | bytes 540704 | tf_op jit(solution)/shard_map/ppermute | solution.py:150
  68.5 1.6 maximum_select_fusion
  70.1 5.9 %all-to-all-done = bf16[16,32,384]{2,1,0:T(8,128)(2,1)S(1)} async-done(((bf16[16,32,384]{2,1,0:T(8,128)(2,1)}), bf16[16,32,384]{2,1,0:T(8,128)(2,1)S(1)}, u32[]{:S(2)}, u32[]{:S(2)}) %all-to-all-start) | async-done | bytes 393248 | tf_op jit(solution)/shard_map/all_to_all | solution.py:494
  76.0 0.9 shard_map.111
  77.3 0.7 collective-permute-start.21
  78.0 1.2 collective-permute-start.22
  79.2 2.6 %collective-permute-start.23 = (bf16[32,1536]{1,0:T(8,128)(2,1)S(1)}, bf16[32,1536]{1,0:T(8,128)(2,1)S(1)}, u32[]{:S(2)}, u32[]{:S(2)}) collective-permute-start(bf16[32,1536]{1,0:T(8,128)(2,1)S(1)} %get-tuple-element.24), channel_id=1, source_target_pairs={{0,6},{1,7},{2,4},{3,5},{4,2},{5,3},{6,0},{7,1},{8,14},{9,15},{10,... | collective-permute-start | bytes 294920 | tf_op jit(solution)/shard_map/ppermute | solution.py:150
  81.8 1.1 collective-permute-done.21
  82.9 5.8 %collective-permute-done.22 = bf16[32,1536]{1,0:T(8,128)(2,1)S(1)} collective-permute-done((bf16[32,1536]{1,0:T(8,128)(2,1)S(1)}, bf16[32,1536]{1,0:T(8,128)(2,1)S(1)}, u32[]{:S(2)}, u32[]{:S(2)}) %collective-permute-start.22) | collective-permute-done | bytes 98336 | tf_op jit(solution)/shard_map/ppermute | solution.py:150
  89.1 15.5 %all_to_all.19 = bf16[8,16,1536]{2,1,0:T(8,128)(2,1)S(1)} all-to-all(bf16[8,16,1536]{2,1,0:T(8,128)(2,1)S(1)} %bitcast.66), channel_id=1, replica_groups=mesh['frame'=4,'expert'=8] {'expert'}, dimensions={0} | all-to-all | bytes 786432 | tf_op jit(solution)/shard_map/all_to_all | solution.py:515
  104.5 0.6 collective-permute-start.24
  105.2 1.1 collective-permute-done.25.other
  106.3 9.5 %shard_map.112 = (f32[128,2048]{1,0:T(8,128)S(1)}, f32[128,2048]{1,0:T(8,128)S(1)}, f32[128,128]{1,0:T(8,128)S(1)}) custom-call(s32[3]{0:T(128)S(1)} %copy-done.5, bf16[128,1536]{1,0:T(8,128)(2,1)S(1)} %bitcast.61, bf16[128,1536]{1,0:T(8,128)(2,1)S(1)} %collective-permute-done.25.other, bf16[24,1,256]{2,1,0:T(2,128)(2,1)S(1)} %reshape.189.gain, ...), custom_call_target="tpu_custom_call" | custom-call | flops 3221225472 | bytes 25165824 | tf_op jit(solution)/shard_map/pallas_call | solution.py:372
  115.8 0.5 slice.46
  117.2 1.6 collective-permute-done.26.other
  118.8 14.9 %shard_map.113 = (bf16[128,2048]{1,0:T(8,128)(2,1)S(1)}, bf16[2,128,1536]{2,1,0:T(8,128)(2,1)S(1)}) custom-call(s32[3]{0:T(128)S(1)} %copy-done.5, bf16[128,1536]{1,0:T(8,128)(2,1)S(1)} %collective-permute-done.24.own, bf16[128,1536]{1,0:T(8,128)(2,1)S(1)} %collective-permute-done.26.other, bf16[24,1,256]{2,1,0:T(2,128)(2,1)S(1)} %reshape.189.gain, ...), custom_call_target="tpu_custom_call" | custom-call | flops 4831838208 | bytes 37748736 | tf_op jit(solution)/shard_map/pallas_call | solution.py:386
  134.4 1.1 collective-permute-done.27
  135.6 0.7 collective-permute-start.32
  136.3 0.5 slice.59
  137.6 1.4 collective-permute-start.29
  139.4 4.5 %shard_map.114.before = bf16[1,128,1536]{2,1,0:T(8,128)(2,1)S(1)} custom-call(s32[3]{0:T(128)S(1)} %copy-done.5, bf16[128,2048]{1,0:T(8,128)(2,1)S(1)} %get-tuple-element.18.hidden, bf16[1,2048,6144]{2,1,0:T(8,128)(2,1)} %down_w.5, bf16[128,1536]{1,0:T(8,128)(2,1)S(1)} %fusion.7.before), custom_call_target="tpu_custom_call" | custom-call | flops 805306368 | bytes 6291456 | tf_op jit(solution)/shard_map/pallas_call | solution.py:404
  144.0 4.3 %shard_map.115 = bf16[1,128,1536]{2,1,0:T(8,128)(2,1)S(1)} custom-call(s32[3]{0:T(128)S(1)} %copy-done.5, bf16[128,2048]{1,0:T(8,128)(2,1)S(1)} %get-tuple-element.18.hidden, bf16[1,2048,6144]{2,1,0:T(8,128)(2,1)} %down_w.5, bf16[1,128,1536]{2,1,0:T(8,128)(2,1)S(1)} %shard_map.114.before), custom_call_target="tpu_custom_call" | custom-call | flops 805306368 | bytes 6291456 | tf_op jit(solution)/shard_map/pallas_call | solution.py:404
  148.8 1.3 collective-permute-done.31
  150.1 0.9 fusion.6
  151.0 3.5 %all-to-all-start.2 = ((bf16[8,16,1536]{2,1,0:T(8,128)(2,1)}), bf16[8,16,1536]{2,1,0:T(8,128)(2,1)S(1)}, u32[]{:S(2)}, u32[]{:S(2)}) async-start(bf16[8,16,1536]{2,1,0:T(8,128)(2,1)} %bitcast.32), calls=%async_computation.2 | async-start | bytes 786432 | tf_op jit(solution)/shard_map/all_to_all | solution.py:533
  154.5 0.7 gather_fusion
  155.6 11.3 %all-to-all-done.2 = bf16[8,16,1536]{2,1,0:T(8,128)(2,1)S(1)} async-done(((bf16[8,16,1536]{2,1,0:T(8,128)(2,1)}), bf16[8,16,1536]{2,1,0:T(8,128)(2,1)S(1)}, u32[]{:S(2)}, u32[]{:S(2)}) %all-to-all-start.2) | async-done | bytes 393248 | tf_op jit(solution)/shard_map/all_to_all | solution.py:533
  166.9 0.9 fusion
  (101 shorter events, 5.2 us)
Async XLA Ops:
  0.0 134.2 %copy-start = (bf16[6144,8]{0,1:T(8,128)(2,1)S(1)}, bf16[6144,8]{0,1:T(8,128)(2,1)}, u32[]{:S(2)}) copy-start(bf16[6144,8]{0,1:T(8,128)(2,1)} %param.17) | copy-start | bytes 294916
  0.0 14.5 %copy-start.10 = (s32[32,2]{0,1:T(2,128)S(1)}, s32[32,2]{0,1:T(2,128)}, u32[]{:S(2)}) copy-start(s32[32,2]{0,1:T(2,128)} %param.18) | copy-start | bytes 772
  1.1 32.1 %copy-start.1 = (bf16[1,1024,1408]{2,1,0:T(8,128)(2,1)S(1)}, bf16[1,1024,1408]{2,1,0:T(8,128)(2,1)}, u32[]{:S(2)}) copy-start(bf16[1,1024,1408]{2,1,0:T(8,128)(2,1)} %param.11) | copy-start | bytes 8650756
  2.6 12.2 %collective-permute-start.1 = (bf16[176,128]{1,0:T(8,128)(2,1)S(1)}, bf16[176,128]{1,0:T(8,128)(2,1)S(1)}, u32[]{:S(2)}, u32[]{:S(2)}) collective-permute-start(bf16[176,128]{1,0:T(8,128)(2,1)S(1)} %bitcast.69), channel_id=1, source_target_pairs={{0,4},{1,5},{2,6},{3,7},{4,0},{5,1},{6,2},{7,3},{8,12},{9,13},{10,... | collective-permute-start | bytes 135176 | tf_op jit(solution)/shard_map/ppermute | solution.py:150
  6.7 9.0 %collective-permute-start.2 = (bf16[176,128]{1,0:T(8,128)(2,1)S(1)}, bf16[176,128]{1,0:T(8,128)(2,1)S(1)}, u32[]{:S(2)}, u32[]{:S(2)}) collective-permute-start(bf16[176,128]{1,0:T(8,128)(2,1)S(1)} %bitcast.70), channel_id=1, source_target_pairs={{0,6},{1,7},{2,4},{3,5},{4,2},{5,3},{6,0},{7,1},{8,14},{9,15},{10,... | collective-permute-start | bytes 135176 | tf_op jit(solution)/shard_map/ppermute | solution.py:150
  8.0 7.7 %collective-permute-start = (bf16[176,128]{1,0:T(8,128)(2,1)S(1)}, bf16[176,128]{1,0:T(8,128)(2,1)S(1)}, u32[]{:S(2)}, u32[]{:S(2)}) collective-permute-start(bf16[176,128]{1,0:T(8,128)(2,1)S(1)} %bitcast.71), channel_id=1, source_target_pairs={{0,2},{1,3},{2,0},{3,1},{4,6},{5,7},{6,4},{7,5},{8,10},{9,11},{10,... | collective-permute-start | bytes 135176 | tf_op jit(solution)/shard_map/ppermute | solution.py:150
  9.3 10.1 %collective-permute-start.10 = (bf16[176,352]{1,0:T(8,128)(2,1)S(1)}, bf16[176,352]{1,0:T(8,128)(2,1)}, u32[]{:S(2)}, u32[]{:S(2)}) collective-permute-start(bf16[176,352]{1,0:T(8,128)(2,1)S(1)} %constant_dynamic-slice_fusion), channel_id=1, source_target_pairs={{0,2},{1,3},{2,0},{3,1},{4,6},{5,7},{6,4},{7,5},{8,10},{9,11},{10,... | collective-permute-start | bytes 371720 | tf_op jit(solution)/shard_map/ppermute | solution.py:150
  11.2 12.0 %collective-permute-start.11 = (bf16[176,352]{1,0:T(8,128)(2,1)S(1)}, bf16[176,352]{1,0:T(8,128)(2,1)}, u32[]{:S(2)}, u32[]{:S(2)}) collective-permute-start(bf16[176,352]{1,0:T(8,128)(2,1)S(1)} %constant_dynamic-slice_fusion), channel_id=1, source_target_pairs={{0,4},{1,5},{2,6},{3,7},{4,0},{5,1},{6,2},{7,3},{8,12},{9,13},{10,... | collective-permute-start | bytes 371720 | tf_op jit(solution)/shard_map/ppermute | solution.py:150
  14.8 8.4 %collective-permute-start.12 = (bf16[176,352]{1,0:T(8,128)(2,1)S(1)}, bf16[176,352]{1,0:T(8,128)(2,1)S(1)}, u32[]{:S(2)}, u32[]{:S(2)}) collective-permute-start(bf16[176,352]{1,0:T(8,128)(2,1)S(1)} %constant_dynamic-slice_fusion), channel_id=1, source_target_pairs={{0,6},{1,7},{2,4},{3,5},{4,2},{5,3},{6,0},{7,1},{8,14},{9,15},{10,... | collective-permute-start | bytes 371720 | tf_op jit(solution)/shard_map/ppermute | solution.py:150
  16.4 11.2 %collective-permute-start.4 = (bf16[4,176,128]{2,1,0:T(8,128)(2,1)}, bf16[4,176,128]{2,1,0:T(8,128)(2,1)}, u32[]{:S(2)}, u32[]{:S(2)}) collective-permute-start(bf16[4,176,128]{2,1,0:T(8,128)(2,1)} %pad_maximum_fusion.1.refs_0_), channel_id=1, source_target_pairs={{0,1},{1,0},{2,3},{3,2},{4,5},{5,4},{6,7},{7,6},{8,9},{9,8},{10,11... | collective-permute-start | bytes 540680 | tf_op jit(solution)/shard_map/ppermute | solution.py:150
  17.9 10.2 %collective-permute-start.6 = (bf16[4,176,128]{2,1,0:T(8,128)(2,1)}, bf16[4,176,128]{2,1,0:T(8,128)(2,1)}, u32[]{:S(2)}, u32[]{:S(2)}) collective-permute-start(bf16[4,176,128]{2,1,0:T(8,128)(2,1)} %pad_maximum_fusion.1.refs_0_), channel_id=1, source_target_pairs={{0,16},{8,24},{16,0},{24,8},{1,17},{9,25},{17,1},{25,9},{2,18},{10... | collective-permute-start | bytes 540680 | tf_op jit(solution)/shard_map/ppermute | solution.py:150
  19.4 9.2 %collective-permute-start.8 = (bf16[4,176,128]{2,1,0:T(8,128)(2,1)}, bf16[4,176,128]{2,1,0:T(8,128)(2,1)}, u32[]{:S(2)}, u32[]{:S(2)}) collective-permute-start(bf16[4,176,128]{2,1,0:T(8,128)(2,1)} %pad_maximum_fusion.1.refs_0_), channel_id=1, source_target_pairs={{0,17},{1,16},{2,19},{3,18},{4,21},{5,20},{6,23},{7,22},{8,25},{9,... | collective-permute-start | bytes 540680 | tf_op jit(solution)/shard_map/ppermute | solution.py:172
  23.2 6.1 %collective-permute-start.3 = (bf16[4,176,128]{2,1,0:T(8,128)(2,1)}, bf16[4,176,128]{2,1,0:T(8,128)(2,1)}, u32[]{:S(2)}, u32[]{:S(2)}) collective-permute-start(bf16[4,176,128]{2,1,0:T(8,128)(2,1)} %pad_maximum_fusion.1.refs_0_), channel_id=1, source_target_pairs={{0,8},{8,0},{16,24},{24,16},{1,9},{9,1},{17,25},{25,17},{2,10},{10... | collective-permute-start | bytes 540680 | tf_op jit(solution)/shard_map/ppermute | solution.py:150
  23.2 0.7 copy-start.8
  25.1 19.1 %collective-permute-start.18 = (bf16[4,176,352]{2,1,0:T(8,128)(2,1)S(1)}, bf16[4,176,352]{2,1,0:T(8,128)(2,1)}, u32[]{:S(2)}, u32[]{:S(2)}) collective-permute-start(bf16[4,176,352]{2,1,0:T(8,128)(2,1)S(1)} %pad_maximum_fusion.refs_0_), channel_id=1, source_target_pairs={{0,17},{1,16},{2,19},{3,18},{4,21},{5,20},{6,23},{7,22},{8,25},{9,... | collective-permute-start | bytes 1486856 | tf_op jit(solution)/shard_map/ppermute | solution.py:172
  27.6 24.9 %collective-permute-start.14 = (bf16[4,176,352]{2,1,0:T(8,128)(2,1)S(1)}, bf16[4,176,352]{2,1,0:T(8,128)(2,1)}, u32[]{:S(2)}, u32[]{:S(2)}) collective-permute-start(bf16[4,176,352]{2,1,0:T(8,128)(2,1)S(1)} %pad_maximum_fusion.refs_0_), channel_id=1, source_target_pairs={{0,1},{1,0},{2,3},{3,2},{4,5},{5,4},{6,7},{7,6},{8,9},{9,8},{10,11... | collective-permute-start | bytes 1486856 | tf_op jit(solution)/shard_map/ppermute | solution.py:150
  28.2 24.4 %collective-permute-start.16 = (bf16[4,176,352]{2,1,0:T(8,128)(2,1)S(1)}, bf16[4,176,352]{2,1,0:T(8,128)(2,1)}, u32[]{:S(2)}, u32[]{:S(2)}) collective-permute-start(bf16[4,176,352]{2,1,0:T(8,128)(2,1)S(1)} %pad_maximum_fusion.refs_0_), channel_id=1, source_target_pairs={{0,16},{8,24},{16,0},{24,8},{1,17},{9,25},{17,1},{25,9},{2,18},{10... | collective-permute-start | bytes 1486856 | tf_op jit(solution)/shard_map/ppermute | solution.py:150
  28.7 1.8 %collective-permute-start.5 = (bf16[4,176,128]{2,1,0:T(8,128)(2,1)}, bf16[4,176,128]{2,1,0:T(8,128)(2,1)}, u32[]{:S(2)}, u32[]{:S(2)}) collective-permute-start(bf16[4,176,128]{2,1,0:T(8,128)(2,1)} %collective-permute-done.4.refs_2_), channel_id=1, source_target_pairs={{0,8},{8,0},{16,24},{24,16},{1,9},{9,1},{17,25},{25,17},{2,10},{10... | collective-permute-start | bytes 540680 | tf_op jit(solution)/shard_map/ppermute | solution.py:150
  28.7 1.9 %copy-start.12 = (s32[32,2]{0,1:T(2,128)}, s32[32,2]{0,1:T(2,128)S(1)}, u32[]{:S(2)}) copy-start(s32[32,2]{0,1:T(2,128)S(1)} %multiply_add_fusion) | copy-start | bytes 772
  29.3 3.5 %collective-permute-start.7 = (bf16[4,176,128]{2,1,0:T(8,128)(2,1)}, bf16[4,176,128]{2,1,0:T(8,128)(2,1)}, u32[]{:S(2)}, u32[]{:S(2)}) collective-permute-start(bf16[4,176,128]{2,1,0:T(8,128)(2,1)} %collective-permute-done.6.refs_4_), channel_id=1, source_target_pairs={{0,8},{8,0},{16,24},{24,16},{1,9},{9,1},{17,25},{25,17},{2,10},{10... | collective-permute-start | bytes 540680 | tf_op jit(solution)/shard_map/ppermute | solution.py:150
  30.4 2.8 %collective-permute-start.9 = (bf16[4,176,128]{2,1,0:T(8,128)(2,1)}, bf16[4,176,128]{2,1,0:T(8,128)(2,1)}, u32[]{:S(2)}, u32[]{:S(2)}) collective-permute-start(bf16[4,176,128]{2,1,0:T(8,128)(2,1)} %collective-permute-done.8.refs_6_), channel_id=1, source_target_pairs={{0,8},{8,0},{16,24},{24,16},{1,9},{9,1},{17,25},{25,17},{2,10},{10... | collective-permute-start | bytes 540680 | tf_op jit(solution)/shard_map/ppermute | solution.py:150
  32.8 7.7 %copy-start.4 = (s32[3]{0:T(128)}, s32[3]{0:T(128)S(1)}, u32[]{:S(2)}) copy-start(s32[3]{0:T(128)S(1)} %pad_add_fusion.where) | copy-start | bytes 40
  32.8 23.0 %collective-permute-start.13 = (bf16[4,176,352]{2,1,0:T(8,128)(2,1)S(1)}, bf16[4,176,352]{2,1,0:T(8,128)(2,1)}, u32[]{:S(2)}, u32[]{:S(2)}) collective-permute-start(bf16[4,176,352]{2,1,0:T(8,128)(2,1)S(1)} %pad_maximum_fusion.refs_0_), channel_id=1, source_target_pairs={{0,8},{8,0},{16,24},{24,16},{1,9},{9,1},{17,25},{25,17},{2,10},{10... | collective-permute-start | bytes 1486856 | tf_op jit(solution)/shard_map/ppermute | solution.py:150
  40.5 1.2 copy-start.2
  41.7 0.6 copy-start.6
  42.2 13.5 %copy-start.14 = (bf16[32]{0:T(256)(128)(2,1)S(1)}, bf16[32]{0:T(256)(128)(2,1)}, u32[]{:S(2)}) copy-start(bf16[32]{0:T(256)(128)(2,1)} %pad.18.clone) | copy-start | bytes 196
  42.2 13.6 %copy-start.3 = (bf16[512,1408]{1,0:T(8,128)(2,1)S(1)}, bf16[512,1408]{1,0:T(8,128)(2,1)}, u32[]{:S(2)}) copy-start(bf16[512,1408]{1,0:T(8,128)(2,1)} %copy-done.2) | copy-start | bytes 4325380
  42.2 13.6 %copy-start.5 = (s32[3]{0:T(128)S(1)}, s32[3]{0:T(128)}, u32[]{:S(2)}) copy-start(s32[3]{0:T(128)} %copy-done.4) | copy-start | bytes 40
  46.1 9.7 %collective-permute-start.19 = (bf16[4,176,352]{2,1,0:T(8,128)(2,1)}, bf16[4,176,352]{2,1,0:T(8,128)(2,1)S(1)}, u32[]{:S(2)}, u32[]{:S(2)}) collective-permute-start(bf16[4,176,352]{2,1,0:T(8,128)(2,1)} %collective-permute-done.18.refs_6_), channel_id=1, source_target_pairs={{0,8},{8,0},{16,24},{24,16},{1,9},{9,1},{17,25},{25,17},{2,10},{10... | collective-permute-start | bytes 1486856 | tf_op jit(solution)/shard_map/ppermute | solution.py:150
  52.5 3.3 %collective-permute-start.15 = (bf16[4,176,352]{2,1,0:T(8,128)(2,1)}, bf16[4,176,352]{2,1,0:T(8,128)(2,1)S(1)}, u32[]{:S(2)}, u32[]{:S(2)}) collective-permute-start(bf16[4,176,352]{2,1,0:T(8,128)(2,1)} %collective-permute-done.14.refs_2_), channel_id=1, source_target_pairs={{0,8},{8,0},{16,24},{24,16},{1,9},{9,1},{17,25},{25,17},{2,10},{10... | collective-permute-start | bytes 1486856 | tf_op jit(solution)/shard_map/ppermute | solution.py:150
  52.5 3.3 %collective-permute-start.17 = (bf16[4,176,352]{2,1,0:T(8,128)(2,1)}, bf16[4,176,352]{2,1,0:T(8,128)(2,1)S(1)}, u32[]{:S(2)}, u32[]{:S(2)}) collective-permute-start(bf16[4,176,352]{2,1,0:T(8,128)(2,1)} %collective-permute-done.16.refs_4_), channel_id=1, source_target_pairs={{0,8},{8,0},{16,24},{24,16},{1,9},{9,1},{17,25},{25,17},{2,10},{10... | collective-permute-start | bytes 1486856 | tf_op jit(solution)/shard_map/ppermute | solution.py:150
  54.1 14.4 %collective-permute-start.20 = (bf16[176,1536]{1,0:T(8,128)(2,1)S(1)}, bf16[176,1536]{1,0:T(8,128)(2,1)}, u32[]{:S(2)}, u32[]{:S(2)}) collective-permute-start(bf16[176,1536]{1,0:T(8,128)(2,1)S(1)} %broadcast_select_fusion), channel_id=1, source_target_pairs={{0,1},{1,0},{2,3},{3,2},{4,5},{5,4},{6,7},{7,6},{8,9},{9,8},{10,11... | collective-permute-start | bytes 1622024 | tf_op jit(solution)/shard_map/ppermute | solution.py:150
  59.5 9.0 %copy-start.7 = (bf16[176,1536]{1,0:T(8,128)(2,1)S(1)}, bf16[176,1536]{1,0:T(8,128)(2,1)}, u32[]{:S(2)}) copy-start(bf16[176,1536]{1,0:T(8,128)(2,1)} %param.15) | copy-start | bytes 1622020
  59.5 16.4 %all-to-all-start = ((bf16[16,32,384]{2,1,0:T(8,128)(2,1)}), bf16[16,32,384]{2,1,0:T(8,128)(2,1)S(1)}, u32[]{:S(2)}, u32[]{:S(2)}) async-start(bf16[16,32,384]{2,1,0:T(8,128)(2,1)} %bitcast.17), calls=%async_computation | async-start | bytes 786432 | tf_op jit(solution)/shard_map/all_to_all | solution.py:494
  77.3 27.9 %copy-start.9 = (bf16[6144]{0:T(1024)(128)(2,1)S(1)}, bf16[6144]{0:T(1024)(128)(2,1)}, u32[]{:S(2)}) copy-start(bf16[6144]{0:T(1024)(128)(2,1)} %param.16) | copy-start | bytes 36868
  77.3 5.5 %collective-permute-start.21 = (bf16[32,1536]{1,0:T(8,128)(2,1)S(1)}, bf16[32,1536]{1,0:T(8,128)(2,1)S(1)}, u32[]{:S(2)}, u32[]{:S(2)}) collective-permute-start(bf16[32,1536]{1,0:T(8,128)(2,1)S(1)} %get-tuple-element.23), channel_id=1, source_target_pairs={{0,2},{1,3},{2,0},{3,1},{4,6},{5,7},{6,4},{7,5},{8,10},{9,11},{10,... | collective-permute-start | bytes 294920 | tf_op jit(solution)/shard_map/ppermute | solution.py:150
  78.0 10.6 %collective-permute-start.22 = (bf16[32,1536]{1,0:T(8,128)(2,1)S(1)}, bf16[32,1536]{1,0:T(8,128)(2,1)S(1)}, u32[]{:S(2)}, u32[]{:S(2)}) collective-permute-start(bf16[32,1536]{1,0:T(8,128)(2,1)S(1)} %get-tuple-element.25), channel_id=1, source_target_pairs={{0,4},{1,5},{2,6},{3,7},{4,0},{5,1},{6,2},{7,3},{8,12},{9,13},{10,... | collective-permute-start | bytes 294920 | tf_op jit(solution)/shard_map/ppermute | solution.py:150
  79.2 9.5 %collective-permute-start.23 = (bf16[32,1536]{1,0:T(8,128)(2,1)S(1)}, bf16[32,1536]{1,0:T(8,128)(2,1)S(1)}, u32[]{:S(2)}, u32[]{:S(2)}) collective-permute-start(bf16[32,1536]{1,0:T(8,128)(2,1)S(1)} %get-tuple-element.24), channel_id=1, source_target_pairs={{0,6},{1,7},{2,4},{3,5},{4,2},{5,3},{6,0},{7,1},{8,14},{9,15},{10,... | collective-permute-start | bytes 294920 | tf_op jit(solution)/shard_map/ppermute | solution.py:150
  104.5 1.7 %collective-permute-start.25 = (bf16[128,1536]{1,0:T(8,128)(2,1)S(1)}, bf16[128,1536]{1,0:T(8,128)(2,1)S(1)}, u32[]{:S(2)}, u32[]{:S(2)}) collective-permute-start(bf16[128,1536]{1,0:T(8,128)(2,1)S(1)} %bitcast.59), channel_id=1, source_target_pairs={{0,8},{8,0},{16,24},{24,16},{1,9},{9,1},{17,25},{25,17},{2,10},{10... | collective-permute-start | bytes 1179656 | tf_op jit(solution)/shard_map/ppermute | solution.py:150
  104.5 12.4 %collective-permute-start.24 = (bf16[128,1536]{1,0:T(8,128)(2,1)S(1)}, bf16[128,1536]{1,0:T(8,128)(2,1)S(1)}, u32[]{:S(2)}, u32[]{:S(2)}) collective-permute-start(bf16[128,1536]{1,0:T(8,128)(2,1)S(1)} %bitcast.60), channel_id=1, source_target_pairs={{0,16},{8,24},{16,0},{24,8},{1,17},{9,25},{17,1},{25,9},{2,18},{10... | collective-permute-start | bytes 1179656 | tf_op jit(solution)/shard_map/ppermute | solution.py:150
  117.0 1.8 %collective-permute-start.26 = (bf16[128,1536]{1,0:T(8,128)(2,1)S(1)}, bf16[128,1536]{1,0:T(8,128)(2,1)S(1)}, u32[]{:S(2)}, u32[]{:S(2)}) collective-permute-start(bf16[128,1536]{1,0:T(8,128)(2,1)S(1)} %broadcast_select_fusion.1), channel_id=1, source_target_pairs={{0,8},{8,0},{16,24},{24,16},{1,9},{9,1},{17,25},{25,17},{2,10},{10... | collective-permute-start | bytes 1179656 | tf_op jit(solution)/shard_map/ppermute | solution.py:150
  118.8 15.1 %copy-start.11 = (s32[32,2]{0,1:T(2,128)S(1)}, s32[32,2]{0,1:T(2,128)}, u32[]{:S(2)}) copy-start(s32[32,2]{0,1:T(2,128)} %param.18) | copy-start | bytes 772
  133.7 1.8 %collective-permute-start.27 = (bf16[128,1536]{1,0:T(8,128)(2,1)S(1)}, bf16[128,1536]{1,0:T(8,128)(2,1)S(1)}, u32[]{:S(2)}, u32[]{:S(2)}) collective-permute-start(bf16[128,1536]{1,0:T(8,128)(2,1)S(1)} %slice_bitcast_fusion), channel_id=1, source_target_pairs={{0,8},{8,0},{16,24},{24,16},{1,9},{9,1},{17,25},{25,17},{2,10},{10... | collective-permute-start | bytes 1179656 | tf_op jit(solution)/shard_map/ppermute | solution.py:150
  135.6 14.5 %collective-permute-start.32 = (bf16[128,1536]{1,0:T(8,128)(2,1)S(1)}, bf16[128,1536]{1,0:T(8,128)(2,1)S(1)}, u32[]{:S(2)}, u32[]{:S(2)}) collective-permute-start(bf16[128,1536]{1,0:T(8,128)(2,1)S(1)} %fusion.7.before), channel_id=1, source_target_pairs={{0,16},{8,24},{16,0},{24,8},{1,17},{9,25},{17,1},{25,9},{2,18},{10... | collective-permute-start | bytes 1179656 | tf_op jit(solution)/shard_map/ppermute | solution.py:150
  137.5 11.3 %collective-permute-start.28 = (f32[32,9]{0,1:T(8,128)S(1)}, f32[32,9]{0,1:T(8,128)S(1)}, u32[]{:S(2)}, u32[]{:S(2)}) collective-permute-start(f32[32,9]{0,1:T(8,128)S(1)} %maximum_select_fusion.1), channel_id=1, source_target_pairs={{0,8},{8,0},{16,24},{24,16},{1,9},{9,1},{17,25},{25,17},{2,10},{10... | collective-permute-start | bytes 3464 | tf_op jit(solution)/shard_map/ppermute | solution.py:150
  137.6 11.2 %collective-permute-start.29 = (f32[32,9]{0,1:T(8,128)S(1)}, f32[32,9]{0,1:T(8,128)S(1)}, u32[]{:S(2)}, u32[]{:S(2)}) collective-permute-start(f32[32,9]{0,1:T(8,128)S(1)} %maximum_select_fusion.1), channel_id=1, source_target_pairs={{0,16},{8,24},{16,0},{24,8},{1,17},{9,25},{17,1},{25,9},{2,18},{10... | collective-permute-start | bytes 3464 | tf_op jit(solution)/shard_map/ppermute | solution.py:150
  139.0 9.7 %collective-permute-start.30 = (f32[32,9]{0,1:T(8,128)S(1)}, f32[32,9]{0,1:T(8,128)S(1)}, u32[]{:S(2)}, u32[]{:S(2)}) collective-permute-start(f32[32,9]{0,1:T(8,128)S(1)} %maximum_select_fusion.1), channel_id=1, source_target_pairs={{0,24},{8,16},{16,8},{24,0},{1,25},{9,17},{17,9},{25,1},{2,26},{10... | collective-permute-start | bytes 3464 | tf_op jit(solution)/shard_map/ppermute | solution.py:150
  148.3 1.8 %collective-permute-start.31 = (bf16[128,1536]{1,0:T(8,128)(2,1)S(1)}, bf16[128,1536]{1,0:T(8,128)(2,1)S(1)}, u32[]{:S(2)}, u32[]{:S(2)}) collective-permute-start(bf16[128,1536]{1,0:T(8,128)(2,1)S(1)} %bitcast.63), channel_id=1, source_target_pairs={{0,8},{8,0},{16,24},{24,16},{1,9},{9,1},{17,25},{25,17},{2,10},{10... | collective-permute-start | bytes 1179656 | tf_op jit(solution)/shard_map/ppermute | solution.py:150
  151.0 15.9 %all-to-all-start.2 = ((bf16[8,16,1536]{2,1,0:T(8,128)(2,1)}), bf16[8,16,1536]{2,1,0:T(8,128)(2,1)S(1)}, u32[]{:S(2)}, u32[]{:S(2)}) async-start(bf16[8,16,1536]{2,1,0:T(8,128)(2,1)} %bitcast.32), calls=%async_computation.2 | async-start | bytes 786432 | tf_op jit(solution)/shard_map/all_to_all | solution.py:533
  154.5 1.0 copy-start.13

commit v3 on v2

--- a/solution.py
+++ b/solution.py
@@ -162,7 +162,7 @@
 
 
 def along_z(piece):
-    return jnp.stack([piece] + [swap(piece, "expert", 2 * d, 8) for d in (1, 2, 3)])
+    return [piece] + [swap(piece, "expert", 2 * d, 8) for d in (1, 2, 3)]
 
 
 def spread(column):
@@ -173,7 +173,7 @@
     groups = []
     for value in (column, by_x, by_y, by_both):
         groups += [value, swap(value, "frame", 1, 4)]
-    return groups, by_both
+    return groups
 
 
 def each_piece(where, pieces):
@@ -181,20 +181,20 @@
     for places, piece in zip(PLACES, pieces):
         for at, (e_bits, f_bits) in enumerate(places):
             row = pl.multiple_of((where[0] ^ e_bits) * rows, 16)
-            yield pl.ds(row, rows), where[1] ^ f_bits, piece[at]
+            yield pl.ds(row, rows), f_bits, piece[at]
 
 
 def attend_body(where, frames, *refs):
-    pieces, (pooled_frames, states, whole) = refs[: len(PLACES)], refs[-3:]
-    for row_range, column, piece in each_piece(where, pieces):
+    pieces, (keep, give, states, whole) = refs[: len(PLACES)], refs[-4:]
+    for row_range, bits, piece in each_piece(where, pieces):
         columns = piece.shape[1]
-        whole[row_range, pl.ds(pl.multiple_of(column * columns, 128), columns)] = piece
+        first = (bits % 2 * 2 + bits // 2) * columns
+        whole[row_range, first : first + columns] = piece
     tokens = frames.shape[0]
     half = whole.shape[1] // 2
     valid = lax.broadcasted_iota(jnp.int32, (tokens, half), 0) < where[2]
-    for part in range(2):
-        columns = pl.ds(part * half, half)
-        scores = jnp.dot(frames[...], whole[:, columns], preferred_element_type=jnp.float32)
+    for part, out in ((1, give), (0, keep)):
+        scores = jnp.dot(frames[...], whole[:, part * half : (part + 1) * half], preferred_element_type=jnp.float32)
         masked = jnp.where(valid, scores, NEG_BIG)
         peak = jnp.max(masked, axis=0, keepdims=True)
         expos = jnp.where(valid, jnp.exp(masked - peak), 0.0)
@@ -202,57 +202,65 @@
         some = total > 0.0
         safe = jnp.where(some, total, 1.0)
         weights = (expos * (1.0 / safe)).astype(jnp.bfloat16)
-        states[:, columns] = jnp.where(some, peak + jnp.log(safe), NEG_BIG)
-        pooled_frames[columns, :] = lax.dot_general(
+        state = jnp.where(some, peak + jnp.log(safe), NEG_BIG)
+        pairs = states.shape[1]
+        for at in range(2):
+            bits = part + 2 * at
+            states[bits : bits + 1, :] = state[:, at * pairs : (at + 1) * pairs]
+        out[...] = lax.dot_general(
             weights, frames[...], (((0,), (0,)), ((), ())), preferred_element_type=jnp.float32
         ).astype(jnp.bfloat16)
 
 
-def values_body(where, pooled_frames, states, *refs):
-    pieces, (packed, whole) = refs[: len(PLACES)], refs[len(PLACES) :]
-    for row_range, column, piece in each_piece(where, pieces):
-        whole[column, row_range, :] = piece
-    groups, _, width = whole.shape
-    head_size = width // 4
-    pairs = pooled_frames.shape[0] // groups
-    latents = pairs // 4
-    head_of = lax.broadcasted_iota(jnp.int32, (latents, width), 1) // head_size
-    for group in range(groups):
-        rows = pooled_frames[group * pairs : (group + 1) * pairs, :]
-        every = jnp.dot(rows, whole[group], preferred_element_type=jnp.float32)
-        own = jnp.zeros((latents, width), jnp.float32)
-        for head in range(4):
-            own = jnp.where(head_of == head, every[head * latents : (head + 1) * latents, :], own)
-        for copy in range(packed.shape[1]):
-            packed[group, copy, :, :width] = own.astype(jnp.bfloat16)
-            packed[group, copy, :, width:] = states[group]
-
-
-def combine_body(where, parts, pooled):
-    latents = parts.shape[2]
-    width = 352
-    head_size = width // 4
-    head_of = lax.broadcasted_iota(jnp.int32, (latents, width), 1) // head_size
-    for turn in range(4):
-        logs, values = [], []
-        for part in range(4):
-            block = parts[where[0] ^ turn, part].astype(jnp.float32)
-            state = block[:, width : width + 4] + block[:, width + 4 : width + 8]
-            state = state + block[:, width + 8 : width + 12]
-            logs.append(state)
-            values.append(block[:, :width])
+def pair_body(keep, got, own_states, core_states, y_states, both_states, mine, theirs):
+    pairs = own_states.shape[1]
+    all_states = (own_states, core_states, y_states, both_states)
+    for at, out in ((1, theirs), (0, mine)):
+        logs = [states[(2 * at) ^ bits : ((2 * at) ^ bits) + 1, :] for bits, states in enumerate(all_states)]
         peak = jnp.maximum(jnp.maximum(logs[0], logs[1]), jnp.maximum(logs[2], logs[3]))
         shares = [jnp.exp(state - peak) for state in logs]
         inverse = 1.0 / (shares[0] + shares[1] + shares[2] + shares[3])
-        joined_up = jnp.zeros((latents, width), jnp.float32)
-        for share, value in zip(shares, values):
-            share = share * inverse
-            spread_out = jnp.zeros((latents, width), jnp.float32)
-            for head in range(4):
-                spread_out = jnp.where(head_of == head, share[:, head : head + 1], spread_out)
-            joined_up = joined_up + value * spread_out
-        pooled[turn] = jnp.zeros((latents, 384), jnp.bfloat16)
-        pooled[turn, :, :width] = joined_up.astype(jnp.bfloat16)
+        scaled = []
+        for share, part in ((shares[0], keep), (shares[1], got)):
+            column = jnp.transpose(jnp.broadcast_to(share * inverse, (pairs, pairs)))[:, :1]
+            scaled.append(part[at * pairs : (at + 1) * pairs, :].astype(jnp.float32) * column)
+        out[...] = (scaled[0] + scaled[1]).astype(jnp.bfloat16)
+
+
+def values_body(where, mine, other, column, by_x, pooled, whole):
+    rows = column.shape[1]
+    width = whole.shape[1]
+    for bit, pieces in ((0, column), (1, by_x)):
+        for d in range(4):
+            row = pl.multiple_of((where[0] ^ (2 * d + bit)) * rows, 16)
+            whole[pl.ds(row, rows), :] = pieces[d]
+    head_size = width // 4
+    latents = mine.shape[0] // 4
+    head_of = lax.broadcasted_iota(jnp.int32, (latents, width), 1) // head_size
+    both = (mine[...].astype(jnp.float32) + other[...].astype(jnp.float32)).astype(jnp.bfloat16)
+    every = jnp.dot(both, whole[...], preferred_element_type=jnp.float32)
+    own = jnp.zeros((latents, width), jnp.float32)
+    for head in range(4):
+        own = jnp.where(head_of == head, every[head * latents : (head + 1) * latents, :], own)
+    pooled[...] = jnp.zeros_like(pooled)
+    pooled[:, :width] = own.astype(jnp.bfloat16)
+
+
+def project_body(where, *refs):
+    pooled, (own_rows, other_rows, partial, gathered, weight) = refs[:4], refs[4:]
+    rows = own_rows.shape[0]
+    x_bit = where[0] % 2
+    weight[pl.ds(pl.multiple_of(x_bit * rows, 16), rows), :] = own_rows[...]
+    weight[pl.ds(pl.multiple_of((1 - x_bit) * rows, 16), rows), :] = other_rows[...]
+    spare = weight.shape[0] - 2 * rows
+    weight[2 * rows :, :] = jnp.zeros((spare, weight.shape[1]), jnp.bfloat16)
+    latents = partial.shape[1]
+    for bits in range(4):
+        turn = where[0] // 2 ^ where[1] ^ bits
+        gathered[pl.ds(pl.multiple_of(turn * latents, latents), latents), :] = pooled[bits][...]
+    product = jnp.dot(gathered[...], weight[...], preferred_element_type=jnp.float32).astype(jnp.bfloat16)
+    for turn in range(4):
+        partial[turn] = product[turn * latents : (turn + 1) * latents, :]
 
 
 DEPTH = 256
@@ -354,6 +362,7 @@
 SMEM_SPEC = pl.BlockSpec(memory_space=pltpu.SMEM)
 VMEM_SPEC = pl.BlockSpec(memory_space=pltpu.VMEM)
 HBM_SPEC = pl.BlockSpec(memory_space=pltpu.HBM)
+ANY_SPEC = pl.BlockSpec(memory_space=pl.ANY)
 
 
 def weight_buffers(hidden_width):
@@ -415,15 +424,15 @@
 def in_vmem(body, out_shape, limit, scratch=()):
     space = lambda _: pl.BlockSpec(memory_space=pltpu.VMEM)
 
-    def call(where, *operands):
+    def call(*operands, before=()):
         return pl.pallas_call(
             body,
             out_shape=out_shape,
-            in_specs=[pl.BlockSpec(memory_space=pltpu.SMEM)] + [space(o) for o in operands],
+            in_specs=[SMEM_SPEC if o.ndim == 1 else space(o) for o in operands] + [ANY_SPEC] * len(before),
             out_specs=jax.tree.map(space, out_shape),
             scratch_shapes=list(scratch),
             compiler_params=pltpu.CompilerParams(vmem_limit_bytes=limit * 2**20),
-        )(where, *operands)
+        )(*operands, *before)
 
     return call
 
@@ -464,46 +473,46 @@
         w_kv[:, :width], spaced, (((1,), (1,)), ((), ())), preferred_element_type=jnp.float32
     )
     asked = (asked / math.sqrt(head_size)).astype(jnp.bfloat16)
-    asked_pieces, asked_last = spread(along_z(asked))
+    asked_along = along_z(asked)
+    asked_column = jnp.stack(asked_along)
+    asked_pieces = spread(asked_column)
     value_piece = lax.dynamic_slice(w_kv, (0, width + f * quarter), (rows, quarter))
-    value_column = along_z(value_piece)
-    pooled_frames, states = in_vmem(
+    value_column = jnp.stack(along_z(hold(value_piece, asked_along[1], asked_along[3])))
+    value_x = swap(value_column, "expert", 1, 8)
+    proj_other = swap(hold(w_proj, value_x), "expert", 1, 8)
+
+    half = jax.ShapeDtypeStruct((HEADS // 2 * latent_count, width), jnp.bfloat16)
+    piece = jax.ShapeDtypeStruct((4 * latent_count, width), jnp.bfloat16)
+    keep, give, states = in_vmem(
         attend_body,
-        (
-            jax.ShapeDtypeStruct((HEADS * latent_count, width), jnp.bfloat16),
-            jax.ShapeDtypeStruct((1, HEADS * latent_count), jnp.float32),
-        ),
+        (half, half, jax.ShapeDtypeStruct((4, 4 * latent_count), jnp.float32)),
         28,
         [pltpu.VMEM((width, HEADS * latent_count), jnp.bfloat16)],
-    )(where, frames[0], *asked_pieces, select)
-    value_pieces, value_last = spread(value_column)
-    proj_other = swap(hold(w_proj, value_last), "expert", 1, 8)
-    by_latent = jnp.transpose(states.reshape(4, 4, latent_count), (0, 2, 1))
-    high = lax.reduce_precision(by_latent, 8, 7)
-    middle = lax.reduce_precision(by_latent - high, 8, 7)
-    low = (by_latent - high) - middle
-    blank = jnp.zeros((4, latent_count, 20), jnp.float32)
-    state_columns = jnp.concatenate([high, middle, low, blank], axis=-1).astype(jnp.bfloat16)
-    packed = in_vmem(
+    )(where, frames[0], *asked_pieces, before=(select, value_column))
+    got = swap(give, "frame", 1, 4)
+    other_states = [swap(states, "frame", bits, 4) for bits in (1, 2, 3)]
+    mine, theirs = in_vmem(pair_body, (piece, piece), 16)(keep, got, states, *other_states)
+    from_across = swap(theirs, "frame", 2, 4)
+    pooled = in_vmem(
         values_body,
-        jax.ShapeDtypeStruct((4, 4, latent_count, 384), jnp.bfloat16),
-        20,
-        [pltpu.VMEM((4, width, quarter), jnp.bfloat16)],
-    )(where, pooled_frames, state_columns, *value_pieces)
-    same_x = [[8 * part + 2 * z + x for z in range(4) for part in range(4)] for x in range(2)]
-    parts = lax.all_to_all(
-        packed.reshape(16 * latent_count, 384), ("frame", "expert"), 0, 0, axis_index_groups=same_x, tiled=True
-    ).reshape(4, 4, latent_count, 384)
-    z_index = jnp.stack([e // 2]).astype(jnp.int32)
-    pooled = in_vmem(combine_body, jax.ShapeDtypeStruct((4, latent_count, 384), jnp.bfloat16), 8)(z_index, parts)
-
-    own_first = e % 2 == 0
-    proj_rows = jnp.where(
-        own_first, jnp.concatenate([w_proj, proj_other]), jnp.concatenate([proj_other, w_proj])
-    )
-    proj_rows = jnp.pad(proj_rows, ((0, 384 - 2 * rows), (0, 0)))
-    partial = jnp.dot(pooled.reshape(4 * latent_count, 384), proj_rows, preferred_element_type=jnp.float32).astype(jnp.bfloat16)
-    partial = partial.reshape(4, latent_count, -1)
+        jax.ShapeDtypeStruct((latent_count, 384), jnp.bfloat16),
+        12,
+        [pltpu.VMEM((width, quarter), jnp.bfloat16)],
+    )(where, mine, from_across, value_column, value_x)
+    pooled_here = [
+        lax.ppermute(
+            pooled,
+            ("frame", "expert"),
+            [(8 * f + 2 * z + x, 8 * (z ^ bits) + 2 * f + x) for f in range(4) for z in range(4) for x in range(2)],
+        )
+        for bits in range(4)
+    ]
+    partial = in_vmem(
+        project_body,
+        jax.ShapeDtypeStruct((4, latent_count, w_proj.shape[1]), jnp.bfloat16),
+        16,
+        [pltpu.VMEM((4 * latent_count, 384), jnp.bfloat16), pltpu.VMEM((384, w_proj.shape[1]), jnp.bfloat16)],
+    )(where, *pooled_here, w_proj, proj_other)
     x_sum = partial[0].astype(jnp.float32)
     for d in (1, 2, 3):
         x_sum = x_sum + swap(partial[d], "expert", 2 * d, 8).astype(jnp.float32)

time: 168 us -> 167 us (level)
  starting transfers between devices: 36.9 us -> 40.4 us
  Pallas kernels: 45.1 us -> 42.2 us
  local copies, waits for them, and re-layouts: 11 us -> 8.47 us
  waiting for transfers between devices: 43.6 us -> 45.9 us
  other arithmetic: 9.2 us -> 7.36 us
    ppermute x0 -> x4, starting transfers between devices: none -> 7.85 us  [fast_local(): lax.ppermute(pooled, ('frame', 'expert'), [(8 * f + 2 * z + x, 8 * (z ^ b...]
    all_to_all x1 -> x0, waiting for transfers between devices: 5.91 us -> none  [fast_local(): lax.all_to_all(packed.reshape(16 * latent_count, 384), ('frame', 'expert'...]
    ppermute x0 -> x4, waiting for transfers between devices: none -> 5.61 us  [fast_local(): lax.ppermute(pooled, ('frame', 'expert'), [(8 * f + 2 * z + x, 8 * (z ^ b...]
    all_to_all x1 -> x0, starting transfers between devices: 4.27 us -> none  [fast_local(): lax.all_to_all(packed.reshape(16 * latent_count, 384), ('frame', 'expert'...]
    pallas_call x3 -> x4, Pallas kernels: 11.9 us -> 8.96 us  [call(): pl.pallas_call(body, out_shape=out_shape, in_specs=[SMEM_SPEC if o.ndim =...]
    ppermute x2 -> x1, starting transfers between devices: 3 us -> 0.55 us  [spread(): by_both = lax.ppermute(column, ('frame', 'expert'), diagonal)]
    ppermute x31, starting transfers between devices: 26.2 us -> 28.6 us  [swap(): return lax.ppermute(value, axis, [(i, i ^ bits) for i in range(size)])]
    ppermute x31, waiting for transfers between devices: 26.4 us -> 28.6 us  [swap(): return lax.ppermute(value, axis, [(i, i ^ bits) for i in range(size)])]
  transfers between devices with their start and end apart: 35 -> 37, of which waited for: 12 -> 18; matrix products, arithmetic and copies ran while one was open for 9% -> 7% of each run, Pallas kernels for 17% -> 16%
where the time goes in v3:
time: 167 us
  waiting for transfers between devices  45.9 us (27%)
  Pallas kernels  42.2 us (25%)
  starting transfers between devices  40.4 us (24%)
  blocking collectives  15.2 us (9%)
  local copies, waits for them, and re-layouts  8.47 us (5%)
  other arithmetic  7.36 us (4%)
  between operations  4.3 us (3%)
  matrix products  2.78 us (2%)
    ppermute x31, waiting for transfers between devices, swap(): return lax.ppermute(value, axis, [(i, i ^ bits) for i in range(size)])  28.6 us
    ppermute x31, starting transfers between devices, swap(): return lax.ppermute(value, axis, [(i, i ^ bits) for i in range(size)])  28.6 us
    all_to_all x1, blocking collectives, fast_local(): lax.all_to_all(send_rows.reshape(expert_total, capacity, part_width), 'ex...  15.2 us
    pallas_call x1, Pallas kernels, expert_far(): pl.pallas_call(far_body, out_shape=(jax.ShapeDtypeStruct((rows, hidden_wi...  14.9 us
    all_to_all x1, waiting for transfers between devices, fast_local(): lax.all_to_all(summed.reshape(expert_total, capacity, part_width), 'exper...  11.3 us
    pallas_call x1, Pallas kernels, expert_near(): pl.pallas_call(near_body, out_shape=sums, in_specs=[SMEM_SPEC] + [VMEM_SP...  9.49 us
    pallas_call x4, Pallas kernels, call(): pl.pallas_call(body, out_shape=out_shape, in_specs=[SMEM_SPEC if o.ndim =...  8.96 us
    pallas_call x2, Pallas kernels, expert_last(): pl.pallas_call(functools.partial(last_body, bit), out_shape=jax.ShapeDtyp...  8.89 us
  transfers between devices with their start and end apart: 37, of which 18 were waited for; matrix products, arithmetic and copies ran while one was open for 7% of the time, Pallas kernels for 16%

profile of v3, /device:TPU:0, one launch (start us, length us, event | category | flops | bytes accessed | tf_op | source)
XLA Modules:
  0.0 166.6 jit_solution(2100960844725257671)
XLA Ops:
  0.1 0.9 broadcast_select_fusion.2
  1.1 1.3 fusion.1
  2.4 3.1 %collective-permute-start = (bf16[176,128]{1,0:T(8,128)(2,1)S(1)}, bf16[176,128]{1,0:T(8,128)(2,1)S(1)}, u32[]{:S(2)}, u32[]{:S(2)}) collective-permute-start(bf16[176,128]{1,0:T(8,128)(2,1)S(1)} %bitcast.70), channel_id=1, source_target_pairs={{0,2},{1,3},{2,0},{3,1},{4,6},{5,7},{6,4},{7,5},{8,10},{9,11},{10,... | collective-permute-start | bytes 135176 | tf_op jit(solution)/shard_map/ppermute | solution.py:150
  5.5 2.5 %collective-permute-start.2 = (bf16[176,128]{1,0:T(8,128)(2,1)S(1)}, bf16[176,128]{1,0:T(8,128)(2,1)S(1)}, u32[]{:S(2)}, u32[]{:S(2)}) collective-permute-start(bf16[176,128]{1,0:T(8,128)(2,1)S(1)} %bitcast.71), channel_id=1, source_target_pairs={{0,6},{1,7},{2,4},{3,5},{4,2},{5,3},{6,0},{7,1},{8,14},{9,15},{10,... | collective-permute-start | bytes 135176 | tf_op jit(solution)/shard_map/ppermute | solution.py:150
  8.1 0.8 copy.49
  10.0 0.5 slice.58
  11.2 0.8 collective-permute-done.2
  11.9 0.5 slice.59
  13.1 1.0 dynamic-slice_select_fusion
  14.2 1.1 collective-permute-start.10
  15.3 1.7 %collective-permute-start.11 = (bf16[176,352]{1,0:T(8,128)(2,1)S(1)}, bf16[176,352]{1,0:T(8,128)(2,1)S(1)}, u32[]{:S(2)}, u32[]{:S(2)}) collective-permute-start(bf16[176,352]{1,0:T(8,128)(2,1)S(1)} %dynamic-slice_select_fusion), channel_id=1, source_target_pairs={{0,4},{1,5},{2,6},{3,7},{4,0},{5,1},{6,2},{7,3},{8,12},{9,13},{10,... | collective-permute-start | bytes 371720 | tf_op jit(solution)/shard_map/ppermute | solution.py:150
  16.9 1.7 %collective-permute-start.12 = (bf16[176,352]{1,0:T(8,128)(2,1)S(1)}, bf16[176,352]{1,0:T(8,128)(2,1)S(1)}, u32[]{:S(2)}, u32[]{:S(2)}) collective-permute-start(bf16[176,352]{1,0:T(8,128)(2,1)S(1)} %dynamic-slice_select_fusion), channel_id=1, source_target_pairs={{0,6},{1,7},{2,4},{3,5},{4,2},{5,3},{6,0},{7,1},{8,14},{9,15},{10,... | collective-permute-start | bytes 371720 | tf_op jit(solution)/shard_map/ppermute | solution.py:150
  18.7 1.5 collective-permute-start.4
  20.2 1.5 collective-permute-start.6
  21.7 1.0 fusion.34
  22.8 0.6 collective-permute-start.8
  23.3 4.3 %collective-permute-done.11 = bf16[176,352]{1,0:T(8,128)(2,1)S(1)} collective-permute-done((bf16[176,352]{1,0:T(8,128)(2,1)S(1)}, bf16[176,352]{1,0:T(8,128)(2,1)S(1)}, u32[]{:S(2)}, u32[]{:S(2)}) %collective-permute-start.11) | collective-permute-done | bytes 123936 | tf_op jit(solution)/shard_map/ppermute | solution.py:150
  27.7 1.6 collective-permute-start.18
  29.3 0.7 multiply_add_fusion
  30.0 0.5 collective-permute-start.5
  32.3 1.8 %copy-done.1 = bf16[1,1024,1408]{2,1,0:T(8,128)(2,1)S(1)} copy-done((bf16[1,1024,1408]{2,1,0:T(8,128)(2,1)S(1)}, bf16[1,1024,1408]{2,1,0:T(8,128)(2,1)}, u32[]{:S(2)}) %copy-start.1) | copy-done | bytes 2883608
  34.1 6.5 %shard_map.109 = (bf16[256,1408]{1,0:T(8,128)(2,1)S(1)}, bf16[256,1408]{1,0:T(8,128)(2,1)S(1)}, f32[4,128]{1,0:T(4,128)S(1)}) custom-call(s32[3]{0:T(128)S(1)} %pad_add_fusion.where, bf16[1024,1408]{1,0:T(8,128)(2,1)S(1)} %bitcast.59, bf16[4,176,128]{2,1,0:T(8,128)(2,1)S(1)} %pad_maximum_fusion.1.refs_0_, ...), custom_call_target="tpu_custom_call" | custom-call | tf_op jit(solution)/shard_map/pallas_call | solution.py:428
  40.8 0.5 slice.60
  42.0 1.1 broadcast_select_fusion
  43.1 0.6 collective-permute-start.23
  43.7 1.5 collective-permute-start.15
  45.5 1.7 %collective-permute-done.15.y_states = f32[4,128]{1,0:T(4,128)S(1)} collective-permute-done((f32[4,128]{1,0:T(4,128)S(1)}, f32[4,128]{1,0:T(4,128)S(1)}, u32[]{:S(2)}, u32[]{:S(2)}) %collective-permute-start.15) | collective-permute-done | bytes 2080 | tf_op jit(solution)/shard_map/ppermute | solution.py:150
  47.2 0.9 collective-permute-done.16.both_states
  48.2 0.5 shard_map.110
  48.7 0.6 collective-permute-start.17
  49.3 10.3 %collective-permute-done.17.other = bf16[128,1408]{1,0:T(8,128)(2,1)S(1)} collective-permute-done((bf16[128,1408]{1,0:T(8,128)(2,1)S(1)}, bf16[128,1408]{1,0:T(8,128)(2,1)S(1)}, u32[]{:S(2)}, u32[]{:S(2)}) %collective-permute-start.17) | collective-permute-done | bytes 360480 | tf_op jit(solution)/shard_map/ppermute | solution.py:150
  59.6 1.0 shard_map.111
  60.6 0.7 collective-permute-start.19
  61.3 4.2 %collective-permute-start.20 = (bf16[32,384]{1,0:T(8,128)(2,1)S(1)}, bf16[32,384]{1,0:T(8,128)(2,1)S(1)}, u32[]{:S(2)}, u32[]{:S(2)}) collective-permute-start(bf16[32,384]{1,0:T(8,128)(2,1)S(1)} %shard_map.111), channel_id=1, source_target_pairs={{0,8},{1,9},{2,0},{3,1},{4,24},{5,25},{6,16},{7,17},{8,10},{9,11},... | collective-permute-start | bytes 73736 | tf_op jit(solution)/shard_map/ppermute | solution.py:503
  65.5 3.0 %collective-permute-start.21 = (bf16[32,384]{1,0:T(8,128)(2,1)S(1)}, bf16[32,384]{1,0:T(8,128)(2,1)S(1)}, u32[]{:S(2)}, u32[]{:S(2)}) collective-permute-start(bf16[32,384]{1,0:T(8,128)(2,1)S(1)} %shard_map.111), channel_id=1, source_target_pairs={{0,16},{1,17},{2,24},{3,25},{4,0},{5,1},{6,8},{7,9},{8,18},{9,19},... | collective-permute-start | bytes 73736 | tf_op jit(solution)/shard_map/ppermute | solution.py:503
  68.5 2.1 %collective-permute-done.21.refs_2_ = bf16[32,384]{1,0:T(8,128)(2,1)S(1)} collective-permute-done((bf16[32,384]{1,0:T(8,128)(2,1)S(1)}, bf16[32,384]{1,0:T(8,128)(2,1)S(1)}, u32[]{:S(2)}, u32[]{:S(2)}) %collective-permute-start.21) | collective-permute-done | bytes 24608 | tf_op jit(solution)/shard_map/ppermute | solution.py:503
  70.5 3.5 %collective-permute-done.22.refs_3_ = bf16[32,384]{1,0:T(8,128)(2,1)S(1)} collective-permute-done((bf16[32,384]{1,0:T(8,128)(2,1)S(1)}, bf16[32,384]{1,0:T(8,128)(2,1)S(1)}, u32[]{:S(2)}, u32[]{:S(2)}) %collective-permute-start.22) | collective-permute-done | bytes 24608 | tf_op jit(solution)/shard_map/ppermute | solution.py:503
  74.1 1.0 copy-done.2
  75.1 1.0 shard_map.112
  76.2 2.3 %collective-permute-start.25 = (bf16[32,1536]{1,0:T(8,128)(2,1)S(1)}, bf16[32,1536]{1,0:T(8,128)(2,1)S(1)}, u32[]{:S(2)}, u32[]{:S(2)}) collective-permute-start(bf16[32,1536]{1,0:T(8,128)(2,1)S(1)} %get-tuple-element.31), channel_id=1, source_target_pairs={{0,4},{1,5},{2,6},{3,7},{4,0},{5,1},{6,2},{7,3},{8,12},{9,13},{10,... | collective-permute-start | bytes 294920 | tf_op jit(solution)/shard_map/ppermute | solution.py:150
  78.5 2.1 %collective-permute-start.26 = (bf16[32,1536]{1,0:T(8,128)(2,1)S(1)}, bf16[32,1536]{1,0:T(8,128)(2,1)S(1)}, u32[]{:S(2)}, u32[]{:S(2)}) collective-permute-start(bf16[32,1536]{1,0:T(8,128)(2,1)S(1)} %get-tuple-element.30), channel_id=1, source_target_pairs={{0,6},{1,7},{2,4},{3,5},{4,2},{5,3},{6,0},{7,1},{8,14},{9,15},{10,... | collective-permute-start | bytes 294920 | tf_op jit(solution)/shard_map/ppermute | solution.py:150
  80.6 1.2 collective-permute-done.24
  81.8 5.2 %collective-permute-done.25 = bf16[32,1536]{1,0:T(8,128)(2,1)S(1)} collective-permute-done((bf16[32,1536]{1,0:T(8,128)(2,1)S(1)}, bf16[32,1536]{1,0:T(8,128)(2,1)S(1)}, u32[]{:S(2)}, u32[]{:S(2)}) %collective-permute-start.25) | collective-permute-done | bytes 98336 | tf_op jit(solution)/shard_map/ppermute | solution.py:150
  87.4 15.2 %all_to_all.10 = bf16[8,16,1536]{2,1,0:T(8,128)(2,1)S(1)} all-to-all(bf16[8,16,1536]{2,1,0:T(8,128)(2,1)S(1)} %bitcast.65), channel_id=1, replica_groups=mesh['frame'=4,'expert'=8] {'expert'}, dimensions={0} | all-to-all | bytes 786432 | tf_op jit(solution)/shard_map/all_to_all | solution.py:524
  102.6 1.4 collective-permute-start.27
  104.0 0.7 reshape.171.gain
  104.8 9.5 %shard_map.113 = (f32[128,2048]{1,0:T(8,128)S(1)}, f32[128,2048]{1,0:T(8,128)S(1)}, f32[128,128]{1,0:T(8,128)S(1)}) custom-call(s32[3]{0:T(128)S(1)} %pad_add_fusion.where, bf16[128,1536]{1,0:T(8,128)(2,1)S(1)} %bitcast.62, bf16[128,1536]{1,0:T(8,128)(2,1)S(1)} %collective-permute-done.28.other, bf16[24,1,256]{2,1,0:T(2,128)(2,1)S(1)} %reshape.171.gain, ...), custom_call_target="tpu_custom_call" | custom-call | flops 3221225472 | bytes 25165824 | tf_op jit(solution)/shard_map/pallas_call | solution.py:381
  114.3 0.5 slice.50
  115.8 1.5 collective-permute-done.29.other
  117.3 14.9 %shard_map.114 = (bf16[128,2048]{1,0:T(8,128)(2,1)S(1)}, bf16[2,128,1536]{2,1,0:T(8,128)(2,1)S(1)}) custom-call(s32[3]{0:T(128)S(1)} %pad_add_fusion.where, bf16[128,1536]{1,0:T(8,128)(2,1)S(1)} %collective-permute-done.27.own, bf16[128,1536]{1,0:T(8,128)(2,1)S(1)} %collective-permute-done.29.other, bf16[24,1,256]{2,1,0:T(2,128)(2,1)S(1)} %reshape.171.gain, ...), custom_call_target="tpu_custom_call" | custom-call | flops 4831838208 | bytes 37748736 | tf_op jit(solution)/shard_map/pallas_call | solution.py:395
  132.7 0.8 dynamic-slice_convert_fusion
  134.1 1.1 collective-permute-start.35
  135.1 0.5 slice.65
  136.4 1.1 collective-permute-start.32
  137.5 0.7 collective-permute-start.33
  138.2 4.5 %shard_map.115.before = bf16[1,128,1536]{2,1,0:T(8,128)(2,1)S(1)} custom-call(s32[3]{0:T(128)S(1)} %pad_add_fusion.where, bf16[128,2048]{1,0:T(8,128)(2,1)S(1)} %get-tuple-element.24.hidden, bf16[1,2048,6144]{2,1,0:T(8,128)(2,1)} %down_w.5, bf16[128,1536]{1,0:T(8,128)(2,1)S(1)} %fusion.6.before), custom_call_target="tpu_custom_call" | custom-call | flops 805306368 | bytes 6291456 | tf_op jit(solution)/shard_map/pallas_call | solution.py:413
  142.8 4.3 %shard_map.116 = bf16[1,128,1536]{2,1,0:T(8,128)(2,1)S(1)} custom-call(s32[3]{0:T(128)S(1)} %pad_add_fusion.where, bf16[128,2048]{1,0:T(8,128)(2,1)S(1)} %get-tuple-element.24.hidden, bf16[1,2048,6144]{2,1,0:T(8,128)(2,1)} %down_w.5, bf16[1,128,1536]{2,1,0:T(8,128)(2,1)S(1)} %shard_map.115.before), custom_call_target="tpu_custom_call" | custom-call | flops 805306368 | bytes 6291456 | tf_op jit(solution)/shard_map/pallas_call | solution.py:413
  147.2 0.4 collective-permute-start.34
  147.6 1.3 collective-permute-done.34
  148.9 0.9 fusion.5
  149.9 3.5 %all-to-all-start.1 = ((bf16[8,16,1536]{2,1,0:T(8,128)(2,1)}), bf16[8,16,1536]{2,1,0:T(8,128)(2,1)S(1)}, u32[]{:S(2)}, u32[]{:S(2)}) async-start(bf16[8,16,1536]{2,1,0:T(8,128)(2,1)} %bitcast.32), calls=%async_computation.1 | async-start | bytes 786432 | tf_op jit(solution)/shard_map/all_to_all | solution.py:542
  153.3 0.7 gather_fusion
  154.4 11.3 %all-to-all-done.1 = bf16[8,16,1536]{2,1,0:T(8,128)(2,1)S(1)} async-done(((bf16[8,16,1536]{2,1,0:T(8,128)(2,1)}), bf16[8,16,1536]{2,1,0:T(8,128)(2,1)S(1)}, u32[]{:S(2)}, u32[]{:S(2)}) %all-to-all-start.1) | async-done | bytes 393248 | tf_op jit(solution)/shard_map/all_to_all | solution.py:542
  165.7 0.9 fusion
  (76 shorter events, 5.6 us)
Async XLA Ops:
  0.0 133.5 %copy-start = (bf16[6144,8]{0,1:T(8,128)(2,1)S(1)}, bf16[6144,8]{0,1:T(8,128)(2,1)}, u32[]{:S(2)}) copy-start(bf16[6144,8]{0,1:T(8,128)(2,1)} %param.17) | copy-start | bytes 294916
  2.4 7.6 %collective-permute-start = (bf16[176,128]{1,0:T(8,128)(2,1)S(1)}, bf16[176,128]{1,0:T(8,128)(2,1)S(1)}, u32[]{:S(2)}, u32[]{:S(2)}) collective-permute-start(bf16[176,128]{1,0:T(8,128)(2,1)S(1)} %bitcast.70), channel_id=1, source_target_pairs={{0,2},{1,3},{2,0},{3,1},{4,6},{5,7},{6,4},{7,5},{8,10},{9,11},{10,... | collective-permute-start | bytes 135176 | tf_op jit(solution)/shard_map/ppermute | solution.py:150
  5.5 6.4 %collective-permute-start.2 = (bf16[176,128]{1,0:T(8,128)(2,1)S(1)}, bf16[176,128]{1,0:T(8,128)(2,1)S(1)}, u32[]{:S(2)}, u32[]{:S(2)}) collective-permute-start(bf16[176,128]{1,0:T(8,128)(2,1)S(1)} %bitcast.71), channel_id=1, source_target_pairs={{0,6},{1,7},{2,4},{3,5},{4,2},{5,3},{6,0},{7,1},{8,14},{9,15},{10,... | collective-permute-start | bytes 135176 | tf_op jit(solution)/shard_map/ppermute | solution.py:150
  8.0 10.6 %collective-permute-start.1 = (bf16[176,128]{1,0:T(8,128)(2,1)S(1)}, bf16[176,128]{1,0:T(8,128)(2,1)S(1)}, u32[]{:S(2)}, u32[]{:S(2)}) collective-permute-start(bf16[176,128]{1,0:T(8,128)(2,1)S(1)} %bitcast.72), channel_id=1, source_target_pairs={{0,4},{1,5},{2,6},{3,7},{4,0},{5,1},{6,2},{7,3},{8,12},{9,13},{10,... | collective-permute-start | bytes 135176 | tf_op jit(solution)/shard_map/ppermute | solution.py:150
  14.2 8.6 %collective-permute-start.10 = (bf16[176,352]{1,0:T(8,128)(2,1)S(1)}, bf16[176,352]{1,0:T(8,128)(2,1)S(1)}, u32[]{:S(2)}, u32[]{:S(2)}) collective-permute-start(bf16[176,352]{1,0:T(8,128)(2,1)S(1)} %dynamic-slice_select_fusion), channel_id=1, source_target_pairs={{0,2},{1,3},{2,0},{3,1},{4,6},{5,7},{6,4},{7,5},{8,10},{9,11},{10,... | collective-permute-start | bytes 371720 | tf_op jit(solution)/shard_map/ppermute | solution.py:150
  15.3 12.3 %collective-permute-start.11 = (bf16[176,352]{1,0:T(8,128)(2,1)S(1)}, bf16[176,352]{1,0:T(8,128)(2,1)S(1)}, u32[]{:S(2)}, u32[]{:S(2)}) collective-permute-start(bf16[176,352]{1,0:T(8,128)(2,1)S(1)} %dynamic-slice_select_fusion), channel_id=1, source_target_pairs={{0,4},{1,5},{2,6},{3,7},{4,0},{5,1},{6,2},{7,3},{8,12},{9,13},{10,... | collective-permute-start | bytes 371720 | tf_op jit(solution)/shard_map/ppermute | solution.py:150
  16.9 10.7 %collective-permute-start.12 = (bf16[176,352]{1,0:T(8,128)(2,1)S(1)}, bf16[176,352]{1,0:T(8,128)(2,1)S(1)}, u32[]{:S(2)}, u32[]{:S(2)}) collective-permute-start(bf16[176,352]{1,0:T(8,128)(2,1)S(1)} %dynamic-slice_select_fusion), channel_id=1, source_target_pairs={{0,6},{1,7},{2,4},{3,5},{4,2},{5,3},{6,0},{7,1},{8,14},{9,15},{10,... | collective-permute-start | bytes 371720 | tf_op jit(solution)/shard_map/ppermute | solution.py:150
  18.7 11.3 %collective-permute-start.4 = (bf16[4,176,128]{2,1,0:T(8,128)(2,1)S(1)}, bf16[4,176,128]{2,1,0:T(8,128)(2,1)S(1)}, u32[]{:S(2)}, u32[]{:S(2)}) collective-permute-start(bf16[4,176,128]{2,1,0:T(8,128)(2,1)S(1)} %pad_maximum_fusion.1.refs_0_), channel_id=1, source_target_pairs={{0,1},{1,0},{2,3},{3,2},{4,5},{5,4},{6,7},{7,6},{8,9},{9,8},{10,11... | collective-permute-start | bytes 540680 | tf_op jit(solution)/shard_map/ppermute | solution.py:150
  20.2 10.3 %collective-permute-start.6 = (bf16[4,176,128]{2,1,0:T(8,128)(2,1)S(1)}, bf16[4,176,128]{2,1,0:T(8,128)(2,1)S(1)}, u32[]{:S(2)}, u32[]{:S(2)}) collective-permute-start(bf16[4,176,128]{2,1,0:T(8,128)(2,1)S(1)} %pad_maximum_fusion.1.refs_0_), channel_id=1, source_target_pairs={{0,16},{8,24},{16,0},{24,8},{1,17},{9,25},{17,1},{25,9},{2,18},{10... | collective-permute-start | bytes 540680 | tf_op jit(solution)/shard_map/ppermute | solution.py:150
  22.8 8.1 %collective-permute-start.8 = (bf16[4,176,128]{2,1,0:T(8,128)(2,1)S(1)}, bf16[4,176,128]{2,1,0:T(8,128)(2,1)S(1)}, u32[]{:S(2)}, u32[]{:S(2)}) collective-permute-start(bf16[4,176,128]{2,1,0:T(8,128)(2,1)S(1)} %pad_maximum_fusion.1.refs_0_), channel_id=1, source_target_pairs={{0,17},{1,16},{2,19},{3,18},{4,21},{5,20},{6,23},{7,22},{8,25},{9,... | collective-permute-start | bytes 540680 | tf_op jit(solution)/shard_map/ppermute | solution.py:172
  27.7 13.1 %collective-permute-start.18 = (bf16[4,176,352]{2,1,0:T(8,128)(2,1)S(1)}, bf16[4,176,352]{2,1,0:T(8,128)(2,1)S(1)}, u32[]{:S(2)}, u32[]{:S(2)}) collective-permute-start(bf16[4,176,352]{2,1,0:T(8,128)(2,1)S(1)} %pad_maximum_fusion.refs_9_.column), channel_id=1, source_target_pairs={{0,1},{1,0},{2,3},{3,2},{4,5},{5,4},{6,7},{7,6},{8,9},{9,8},{10,11... | collective-permute-start | bytes 1486856 | tf_op jit(solution)/shard_map/ppermute | solution.py:150
  30.0 1.4 collective-permute-start.3
  30.0 1.7 %collective-permute-start.5 = (bf16[4,176,128]{2,1,0:T(8,128)(2,1)S(1)}, bf16[4,176,128]{2,1,0:T(8,128)(2,1)S(1)}, u32[]{:S(2)}, u32[]{:S(2)}) collective-permute-start(bf16[4,176,128]{2,1,0:T(8,128)(2,1)S(1)} %collective-permute-done.4.refs_2_), channel_id=1, source_target_pairs={{0,8},{8,0},{16,24},{24,16},{1,9},{9,1},{17,25},{25,17},{2,10},{10... | collective-permute-start | bytes 540680 | tf_op jit(solution)/shard_map/ppermute | solution.py:150
  30.5 1.4 collective-permute-start.7
  30.9 1.4 collective-permute-start.9
  32.3 1.8 %copy-start.1 = (bf16[1,1024,1408]{2,1,0:T(8,128)(2,1)S(1)}, bf16[1,1024,1408]{2,1,0:T(8,128)(2,1)}, u32[]{:S(2)}) copy-start(bf16[1,1024,1408]{2,1,0:T(8,128)(2,1)} %param.11) | copy-start | bytes 8650756
  40.6 7.6 %collective-permute-start.13 = (bf16[256,1408]{1,0:T(8,128)(2,1)S(1)}, bf16[256,1408]{1,0:T(8,128)(2,1)S(1)}, u32[]{:S(2)}, u32[]{:S(2)}) collective-permute-start(bf16[256,1408]{1,0:T(8,128)(2,1)S(1)} %get-tuple-element.16), channel_id=1, source_target_pairs={{0,8},{8,0},{16,24},{24,16},{1,9},{9,1},{17,25},{25,17},{2,10},{10... | collective-permute-start | bytes 2162696 | tf_op jit(solution)/shard_map/ppermute | solution.py:150
  43.1 25.4 %collective-permute-start.23 = (bf16[176,1536]{1,0:T(8,128)(2,1)S(1)}, bf16[176,1536]{1,0:T(8,128)(2,1)S(1)}, u32[]{:S(2)}, u32[]{:S(2)}) collective-permute-start(bf16[176,1536]{1,0:T(8,128)(2,1)S(1)} %broadcast_select_fusion), channel_id=1, source_target_pairs={{0,1},{1,0},{2,3},{3,2},{4,5},{5,4},{6,7},{7,6},{8,9},{9,8},{10,11... | collective-permute-start | bytes 1622024 | tf_op jit(solution)/shard_map/ppermute | solution.py:150
  43.7 1.9 %collective-permute-start.14 = (f32[4,128]{1,0:T(4,128)S(1)}, f32[4,128]{1,0:T(4,128)S(1)}, u32[]{:S(2)}, u32[]{:S(2)}) collective-permute-start(f32[4,128]{1,0:T(4,128)S(1)} %get-tuple-element.17.own_states), channel_id=1, source_target_pairs={{0,8},{8,0},{16,24},{24,16},{1,9},{9,1},{17,25},{25,17},{2,10},{10... | collective-permute-start | bytes 6152 | tf_op jit(solution)/shard_map/ppermute | solution.py:150
  43.7 3.6 %collective-permute-start.15 = (f32[4,128]{1,0:T(4,128)S(1)}, f32[4,128]{1,0:T(4,128)S(1)}, u32[]{:S(2)}, u32[]{:S(2)}) collective-permute-start(f32[4,128]{1,0:T(4,128)S(1)} %get-tuple-element.17.own_states), channel_id=1, source_target_pairs={{0,16},{8,24},{16,0},{24,8},{1,17},{9,25},{17,1},{25,9},{2,18},{10... | collective-permute-start | bytes 6152 | tf_op jit(solution)/shard_map/ppermute | solution.py:150
  45.2 3.0 %collective-permute-start.16 = (f32[4,128]{1,0:T(4,128)S(1)}, f32[4,128]{1,0:T(4,128)S(1)}, u32[]{:S(2)}, u32[]{:S(2)}) collective-permute-start(f32[4,128]{1,0:T(4,128)S(1)} %get-tuple-element.17.own_states), channel_id=1, source_target_pairs={{0,24},{8,16},{16,8},{24,0},{1,25},{9,17},{17,9},{25,1},{2,26},{10... | collective-permute-start | bytes 6152 | tf_op jit(solution)/shard_map/ppermute | solution.py:150
  48.7 10.9 %collective-permute-start.17 = (bf16[128,1408]{1,0:T(8,128)(2,1)S(1)}, bf16[128,1408]{1,0:T(8,128)(2,1)S(1)}, u32[]{:S(2)}, u32[]{:S(2)}) collective-permute-start(bf16[128,1408]{1,0:T(8,128)(2,1)S(1)} %get-tuple-element.19), channel_id=1, source_target_pairs={{0,16},{8,24},{16,0},{24,8},{1,17},{9,25},{17,1},{25,9},{2,18},{10... | collective-permute-start | bytes 1081352 | tf_op jit(solution)/shard_map/ppermute | solution.py:150
  60.6 7.9 %collective-permute-start.19 = (bf16[32,384]{1,0:T(8,128)(2,1)S(1)}, bf16[32,384]{1,0:T(8,128)(2,1)S(1)}, u32[]{:S(2)}, u32[]{:S(2)}) collective-permute-start(bf16[32,384]{1,0:T(8,128)(2,1)S(1)} %shard_map.111), channel_id=1, source_target_pairs={{0,0},{1,1},{2,8},{3,9},{4,16},{5,17},{6,24},{7,25},{8,2},{9,3},{1... | collective-permute-start | bytes 73736 | tf_op jit(solution)/shard_map/ppermute | solution.py:503
  61.3 7.2 %collective-permute-start.20 = (bf16[32,384]{1,0:T(8,128)(2,1)S(1)}, bf16[32,384]{1,0:T(8,128)(2,1)S(1)}, u32[]{:S(2)}, u32[]{:S(2)}) collective-permute-start(bf16[32,384]{1,0:T(8,128)(2,1)S(1)} %shard_map.111), channel_id=1, source_target_pairs={{0,8},{1,9},{2,0},{3,1},{4,24},{5,25},{6,16},{7,17},{8,10},{9,11},... | collective-permute-start | bytes 73736 | tf_op jit(solution)/shard_map/ppermute | solution.py:503
  65.5 5.1 %collective-permute-start.21 = (bf16[32,384]{1,0:T(8,128)(2,1)S(1)}, bf16[32,384]{1,0:T(8,128)(2,1)S(1)}, u32[]{:S(2)}, u32[]{:S(2)}) collective-permute-start(bf16[32,384]{1,0:T(8,128)(2,1)S(1)} %shard_map.111), channel_id=1, source_target_pairs={{0,16},{1,17},{2,24},{3,25},{4,0},{5,1},{6,8},{7,9},{8,18},{9,19},... | collective-permute-start | bytes 73736 | tf_op jit(solution)/shard_map/ppermute | solution.py:503
  68.4 5.6 %collective-permute-start.22 = (bf16[32,384]{1,0:T(8,128)(2,1)S(1)}, bf16[32,384]{1,0:T(8,128)(2,1)S(1)}, u32[]{:S(2)}, u32[]{:S(2)}) collective-permute-start(bf16[32,384]{1,0:T(8,128)(2,1)S(1)} %shard_map.111), channel_id=1, source_target_pairs={{0,24},{1,25},{2,16},{3,17},{4,8},{5,9},{6,0},{7,1},{8,26},{9,27},... | collective-permute-start | bytes 73736 | tf_op jit(solution)/shard_map/ppermute | solution.py:503
  74.1 1.0 copy-start.2
  76.2 5.7 %collective-permute-start.24 = (bf16[32,1536]{1,0:T(8,128)(2,1)S(1)}, bf16[32,1536]{1,0:T(8,128)(2,1)S(1)}, u32[]{:S(2)}, u32[]{:S(2)}) collective-permute-start(bf16[32,1536]{1,0:T(8,128)(2,1)S(1)} %get-tuple-element.29), channel_id=1, source_target_pairs={{0,2},{1,3},{2,0},{3,1},{4,6},{5,7},{6,4},{7,5},{8,10},{9,11},{10,... | collective-permute-start | bytes 294920 | tf_op jit(solution)/shard_map/ppermute | solution.py:150
  76.2 10.8 %collective-permute-start.25 = (bf16[32,1536]{1,0:T(8,128)(2,1)S(1)}, bf16[32,1536]{1,0:T(8,128)(2,1)S(1)}, u32[]{:S(2)}, u32[]{:S(2)}) collective-permute-start(bf16[32,1536]{1,0:T(8,128)(2,1)S(1)} %get-tuple-element.31), channel_id=1, source_target_pairs={{0,4},{1,5},{2,6},{3,7},{4,0},{5,1},{6,2},{7,3},{8,12},{9,13},{10,... | collective-permute-start | bytes 294920 | tf_op jit(solution)/shard_map/ppermute | solution.py:150
  78.5 8.5 %collective-permute-start.26 = (bf16[32,1536]{1,0:T(8,128)(2,1)S(1)}, bf16[32,1536]{1,0:T(8,128)(2,1)S(1)}, u32[]{:S(2)}, u32[]{:S(2)}) collective-permute-start(bf16[32,1536]{1,0:T(8,128)(2,1)S(1)} %get-tuple-element.30), channel_id=1, source_target_pairs={{0,6},{1,7},{2,4},{3,5},{4,2},{5,3},{6,0},{7,1},{8,14},{9,15},{10,... | collective-permute-start | bytes 294920 | tf_op jit(solution)/shard_map/ppermute | solution.py:150
  102.6 2.1 %collective-permute-start.28 = (bf16[128,1536]{1,0:T(8,128)(2,1)S(1)}, bf16[128,1536]{1,0:T(8,128)(2,1)S(1)}, u32[]{:S(2)}, u32[]{:S(2)}) collective-permute-start(bf16[128,1536]{1,0:T(8,128)(2,1)S(1)} %bitcast.60), channel_id=1, source_target_pairs={{0,8},{8,0},{16,24},{24,16},{1,9},{9,1},{17,25},{25,17},{2,10},{10... | collective-permute-start | bytes 1179656 | tf_op jit(solution)/shard_map/ppermute | solution.py:150
  102.6 12.8 %collective-permute-start.27 = (bf16[128,1536]{1,0:T(8,128)(2,1)S(1)}, bf16[128,1536]{1,0:T(8,128)(2,1)S(1)}, u32[]{:S(2)}, u32[]{:S(2)}) collective-permute-start(bf16[128,1536]{1,0:T(8,128)(2,1)S(1)} %bitcast.61), channel_id=1, source_target_pairs={{0,16},{8,24},{16,0},{24,8},{1,17},{9,25},{17,1},{25,9},{2,18},{10... | collective-permute-start | bytes 1179656 | tf_op jit(solution)/shard_map/ppermute | solution.py:150
  115.5 1.8 %collective-permute-start.29 = (bf16[128,1536]{1,0:T(8,128)(2,1)S(1)}, bf16[128,1536]{1,0:T(8,128)(2,1)S(1)}, u32[]{:S(2)}, u32[]{:S(2)}) collective-permute-start(bf16[128,1536]{1,0:T(8,128)(2,1)S(1)} %broadcast_select_fusion.1), channel_id=1, source_target_pairs={{0,8},{8,0},{16,24},{24,16},{1,9},{9,1},{17,25},{25,17},{2,10},{10... | collective-permute-start | bytes 1179656 | tf_op jit(solution)/shard_map/ppermute | solution.py:150
  117.3 15.2 %copy-start.3 = (s32[32,2]{0,1:T(2,128)S(1)}, s32[32,2]{0,1:T(2,128)}, u32[]{:S(2)}) copy-start(s32[32,2]{0,1:T(2,128)} %param.18) | copy-start | bytes 772
  132.2 1.8 %collective-permute-start.30 = (bf16[128,1536]{1,0:T(8,128)(2,1)S(1)}, bf16[128,1536]{1,0:T(8,128)(2,1)S(1)}, u32[]{:S(2)}, u32[]{:S(2)}) collective-permute-start(bf16[128,1536]{1,0:T(8,128)(2,1)S(1)} %slice_bitcast_fusion), channel_id=1, source_target_pairs={{0,8},{8,0},{16,24},{24,16},{1,9},{9,1},{17,25},{25,17},{2,10},{10... | collective-permute-start | bytes 1179656 | tf_op jit(solution)/shard_map/ppermute | solution.py:150
  134.1 14.9 %collective-permute-start.35 = (bf16[128,1536]{1,0:T(8,128)(2,1)S(1)}, bf16[128,1536]{1,0:T(8,128)(2,1)S(1)}, u32[]{:S(2)}, u32[]{:S(2)}) collective-permute-start(bf16[128,1536]{1,0:T(8,128)(2,1)S(1)} %fusion.6.before), channel_id=1, source_target_pairs={{0,16},{8,24},{16,0},{24,8},{1,17},{9,25},{17,1},{25,9},{2,18},{10... | collective-permute-start | bytes 1179656 | tf_op jit(solution)/shard_map/ppermute | solution.py:150
  136.3 11.3 %collective-permute-start.31 = (f32[32,9]{0,1:T(8,128)S(1)}, f32[32,9]{0,1:T(8,128)S(1)}, u32[]{:S(2)}, u32[]{:S(2)}) collective-permute-start(f32[32,9]{0,1:T(8,128)S(1)} %maximum_select_fusion), channel_id=1, source_target_pairs={{0,8},{8,0},{16,24},{24,16},{1,9},{9,1},{17,25},{25,17},{2,10},{10... | collective-permute-start | bytes 3464 | tf_op jit(solution)/shard_map/ppermute | solution.py:150
  136.4 11.2 %collective-permute-start.32 = (f32[32,9]{0,1:T(8,128)S(1)}, f32[32,9]{0,1:T(8,128)S(1)}, u32[]{:S(2)}, u32[]{:S(2)}) collective-permute-start(f32[32,9]{0,1:T(8,128)S(1)} %maximum_select_fusion), channel_id=1, source_target_pairs={{0,16},{8,24},{16,0},{24,8},{1,17},{9,25},{17,1},{25,9},{2,18},{10... | collective-permute-start | bytes 3464 | tf_op jit(solution)/shard_map/ppermute | solution.py:150
  137.5 10.1 %collective-permute-start.33 = (f32[32,9]{0,1:T(8,128)S(1)}, f32[32,9]{0,1:T(8,128)S(1)}, u32[]{:S(2)}, u32[]{:S(2)}) collective-permute-start(f32[32,9]{0,1:T(8,128)S(1)} %maximum_select_fusion), channel_id=1, source_target_pairs={{0,24},{8,16},{16,8},{24,0},{1,25},{9,17},{17,9},{25,1},{2,26},{10... | collective-permute-start | bytes 3464 | tf_op jit(solution)/shard_map/ppermute | solution.py:150
  147.2 1.8 %collective-permute-start.34 = (bf16[128,1536]{1,0:T(8,128)(2,1)S(1)}, bf16[128,1536]{1,0:T(8,128)(2,1)S(1)}, u32[]{:S(2)}, u32[]{:S(2)}) collective-permute-start(bf16[128,1536]{1,0:T(8,128)(2,1)S(1)} %bitcast.63), channel_id=1, source_target_pairs={{0,8},{8,0},{16,24},{24,16},{1,9},{9,1},{17,25},{25,17},{2,10},{10... | collective-permute-start | bytes 1179656 | tf_op jit(solution)/shard_map/ppermute | solution.py:150
  149.9 15.9 %all-to-all-start.1 = ((bf16[8,16,1536]{2,1,0:T(8,128)(2,1)}), bf16[8,16,1536]{2,1,0:T(8,128)(2,1)S(1)}, u32[]{:S(2)}, u32[]{:S(2)}) async-start(bf16[8,16,1536]{2,1,0:T(8,128)(2,1)} %bitcast.32), calls=%async_computation.1 | async-start | bytes 786432 | tf_op jit(solution)/shard_map/all_to_all | solution.py:542
